TPU v7x, 32 devices: a whole 2x2x4 slice. The times are simulated.
32 devices in a mesh: stream: 8 (over z, y), span: 4 (over x, core).
Axes of the slice: x: 2, y: 2, z: 4, core: 2. Of those that a mesh axis runs over, the one named last changes fastest.
Arguments:
- right_sides: bfloat16 [8, 4, 4, 512, 128], P('stream', 'span'), may hold values from -2.5 to 2.5
- inverse: bfloat16 [8, 4, 4, 512, 512], P('stream', 'span'), as said below
- coupling: bfloat16 [8, 4, 4, 3, 64, 512], P('stream', 'span')
- sweep_order: int32 [8, 4, 4], P('stream', 'span'), may hold values from 0 to 3, each once within a row
Outputs:
- solution: bfloat16 [8, 4, 4, 512, 128], P('stream', 'span')
Inputs may be any that keep to these rules, and one draw needn't show every extreme that they name: `sweep_order`: each group's 4 slots appear once each. Every diagonal block's inverse is well conditioned and of order one.
All inputs are finite; a program needn't handle non-finite values.
Results may differ from a plain program's by a relative error of at most 0.024.
Values may be sent and summed in bfloat16 or wider, within the bound.
No kernel may reach another device: no remote copies, remote signals or barrier semaphores. Data moves between devices by JAX's collectives and lax.ppermute only.
A program may use at most 64 MiB of HBM per device.

v0:
```python
import functools

import jax
import jax.numpy as jnp
from jax import lax
from jax.experimental import pallas as pl
from jax.experimental.pallas import tpu as pltpu
from jax.sharding import PartitionSpec as P

NP = 8
SWEEPS = 6
VMEM = pl.BlockSpec(memory_space=pltpu.VMEM)
SMEM = pl.BlockSpec(memory_space=pltpu.SMEM)
HBM = pl.BlockSpec(memory_space=pltpu.HBM)
F32 = jnp.float32
BF16 = jnp.bfloat16


def bits_of(count):
    return [1 << i for i in range(count.bit_length() - 1)]


def reversed_bits(value, count):
    bits = bits_of(count)
    total = 0
    for low, high in zip(bits, bits[::-1]):
        total = total + jnp.where((value & low) != 0, high, 0)
    return total


def reversed_static(value, count):
    bits = bits_of(count)
    return sum(high for low, high in zip(bits, bits[::-1]) if value & low)


def swap(value, axis, mask):
    count = lax.axis_size(axis)
    return lax.ppermute(value, axis, [(i, i ^ mask) for i in range(count)])


def crossing(masks):
    pairs = []
    for i in range(2 * masks[-1]):
        inner = bool(i & masks[-1]) != bool(i & masks[-2])
        pairs.append((i, i ^ (masks[-1] | masks[-2] if inner else 1)))
    return pairs


def dot(left, right):
    return jnp.dot(left, right, preferred_element_type=F32)


def dot_nt(left, right):
    return lax.dot_general(left, right, (((1,), (1,)), ((), ())), preferred_element_type=F32)


def by_half(low, high):
    lane = lax.broadcasted_iota(jnp.int32, low.shape, low.ndim - 1)
    return jnp.where(lane < low.shape[-1] // 2, low, high)


def turned(value):
    return pltpu.roll(value.astype(F32), value.shape[-1] // 2, 1).astype(value.dtype)


def facemap_kernel(place, order_far, inverse_far, coupling_far, given_far, kept, *refs):
    sends = refs[:-7]
    order, inverse, coupling, given, gathered, order_done, done = refs[-7:]
    groups = 1 << len(sends)
    count, nodes, width = given.shape
    face = coupling.shape[1] // 3
    part = nodes // NP
    first = pltpu.make_async_copy(order_far, order, order_done)
    first.start()
    pairs = ((inverse_far, inverse), (coupling_far, coupling), (given_far, given))

    def fetch(kind, slot):
        far, near = pairs[kind]
        return pltpu.make_async_copy(far.at[slot], near.at[slot], done.at[kind, slot])

    for slot in range(count):
        for kind in range(3):
            fetch(kind, slot).start()
    first.wait()
    layer = part // NP
    share = width // groups
    outs = []
    every = []
    for p in range(count):
        slot = order[p]
        for kind in range(3):
            fetch(kind, slot).wait()
        lower = []
        upper = []
        for a in range(NP):
            head = inverse[slot, a * part : a * part + 2 * layer, :].astype(F32)
            tail = inverse[slot, (a + 1) * part - 2 * layer : (a + 1) * part, :].astype(F32)
            lower.append(head[:layer])
            upper.append(tail[layer:])
        faces = jnp.concatenate(lower + upper, axis=0).astype(BF16)
        outflow = inverse[slot, nodes - face :, :]
        rows = jnp.concatenate([faces, outflow, outflow], axis=0)
        full = dot_nt(coupling[slot], rows)
        full = jnp.concatenate([full[2 * face :], full[face : 2 * face], full[:face]], axis=0).astype(BF16)
        for maps in sends:
            maps[p * 3 * face : (p + 1) * 3 * face, :] = full[:, : 2 * face]
        outs.append(full[:, 2 * face :])
        if p % 2 == 1:
            at = (count + p // 2) * 3 * face
            both = by_half(outs[p - 1], outs[p])
            for maps in sends:
                maps[at : at + 3 * face, :] = both
        every.append(dot(rows, given[slot]).T)
    tiles = [gain[:, : 2 * face] for gain in every]
    for p in range(0, count, 2):
        tiles.append(by_half(every[p][:, 2 * face :], every[p + 1][:, 2 * face :]))
    for m, tile in enumerate(tiles):
        gathered[m] = tile
    for rel in range(groups):
        at = pl.multiple_of((place[0] ^ rel) * share, share)
        for m in range(len(tiles)):
            piece = gathered[m, pl.ds(at, share), :].astype(BF16)
            if rel == 0:
                kept[m * share : (m + 1) * share, :] = piece
            else:
                target = sends[rel.bit_length() - 1]
                low = gain_row(rel, count, face, share) + m * share
                target[low : low + share, :] = piece


def gain_row(rel, count, face, share):
    first = 1 << (rel.bit_length() - 1)
    return (count + count // 2) * (3 * face + (rel - first) * share)


def unpack(map_refs, kept, weights, gains, count, face):
    for pos, ref in enumerate(map_refs):
        for p in range(count):
            sides = ref[p * 3 * face : (p + 1) * 3 * face, :]
            at = (count + p // 2) * 3 * face
            outs = ref[at : at + 3 * face, :]
            other = turned(outs)
            outs = by_half(outs, other) if p % 2 == 0 else by_half(other, outs)
            full = jnp.concatenate([sides, outs], axis=1)
            weights[pos, p, : 3 * face, :] = full
            weights[pos, p, 3 * face :, :] = full[2 * face :]
    for pos in range(len(map_refs)):
        rel = reversed_static(pos, len(map_refs))
        ref = map_refs[pos] if rel else kept
        share = gains.shape[2]
        first = gain_row(rel, count, face, share) if rel else 0
        for p in range(count):
            outs = ref[first + (count + p // 2) * share : first + (count + p // 2 + 1) * share]
            other = turned(outs)
            outs = by_half(outs, other) if p % 2 == 0 else by_half(other, outs)
            sides = ref[first + p * share : first + (p + 1) * share]
            gains[pos, p] = jnp.concatenate([sides, outs], axis=1).astype(F32)


def neighbours(me, pos, groups):
    own = me ^ reversed_bits(pos, groups)
    below = jnp.where(own > 0, reversed_bits(((own - 1) & (groups - 1)) ^ me, groups), groups)
    above = jnp.where(own < groups - 1, reversed_bits(((own + 1) & (groups - 1)) ^ me, groups), groups)
    return below, above


def read_lags(me, states, lags, groups, count):
    def read(pos):
        below, above = neighbours(me, pos, groups)
        for p in range(count):
            lags[pos, p] = by_half(states[above, p], states[below, p])

    over(groups, read)


def over(count, body, limit=4):
    if count <= limit:
        for i in range(count):
            body(i)
    else:

        def step(i, carry):
            body(i)
            return carry

        lax.fori_loop(0, count, step, 0)


def split_trace(out):
    high = out.astype(BF16)
    return by_half(high, (out - high.astype(F32)).astype(BF16)), high


def run_chains(chosen, entries, lags, weights, gains, states, count, face):
    share = gains.shape[2]
    outs = [[] for _ in chosen]
    for p in range(count):
        for i, pos in enumerate(chosen):
            rows = entries[i].shape[0]
            result = dot(jnp.concatenate([lags[pos, p, :rows], entries[i]], axis=1), weights[pos, p])
            first = result[:share] + gains[pos, p]
            if result.shape[0] == share:
                result = first
            else:
                result = jnp.concatenate([first, result[share:]], axis=0)
            states[pos, p, :rows] = result[:, : 2 * face].astype(BF16)
            outs[i].append(result[:, 2 * face :])
        if p < count - 1:
            entries = [split_trace(o[p])[0] for o in outs]
    return outs


def respond_kernel(place, *refs, groups, count, face):
    map_refs = refs[:groups]
    kept, pack, weights, gains, states, lags, unit = refs[groups:]
    me = place[0]
    share = gains.shape[2]
    rows = lags.shape[2]
    half = groups // 2
    unpack(map_refs, kept, weights, gains, count, face)
    states[...] = jnp.zeros_like(states)
    unit[...] = jnp.zeros_like(unit)
    row = lax.broadcasted_iota(jnp.int32, (rows, 2 * face), 0) - share
    lane = lax.broadcasted_iota(jnp.int32, (rows, 2 * face), 1)
    for pos in range(half):
        hit = jnp.logical_and(lane < face, row == lane + pos * face)
        unit[0, pos] = jnp.where(hit, 1.0, 0.0).astype(BF16)

    def sweep(k, parity):
        read_lags(me, states, lags, groups, count)

        def block(t):
            live = [2 * t + half * parity, 2 * t + 1 + half * parity]
            bare = [2 * t + half * (1 - parity), 2 * t + 1 + half * (1 - parity)]
            entries = [unit[jnp.minimum(k, 1), pos] for pos in live]
            entries += [jnp.zeros((share, 2 * face), BF16)] * 2
            chosen = live + bare
            ends = [outs[-1] for outs in run_chains(chosen, entries, lags, weights, gains, states, count, face)]
            at = pl.ds(pl.multiple_of(t * 2 * face, 2 * face), 2 * face)
            answered = half * face
            full = by_half(ends[0], ends[1])
            pack[k, :answered, at] = full[share:].astype(BF16)
            for target, tile in ((parity, full[:share]), (1 - parity, by_half(ends[2], ends[3]))):
                low = answered + target * share
                pack[k, low : low + share, at] = tile.astype(BF16)

        over(groups // 4, block, 1)

    def both(i, carry):
        sweep(2 * i, 0)
        sweep(2 * i + 1, 1)
        return carry

    lax.fori_loop(0, SWEEPS // 2, both, 0)


def pick(flag, first, second):
    return jnp.where(flag != 0, first, second)


def offsets_of(ref, k):
    width = ref.shape[2]
    share = (ref.shape[1] - width) // 2
    return ref[k, width : width + share], ref[k, width + share :]


def compose_kernel(line, own, own_other, got, got_other, *outs, mask):
    down = (line[0] // mask) % 2
    width = own.shape[2]
    share = (own.shape[1] - width) // 2
    after = []
    before = []
    inner = []
    for k in range(SWEEPS):
        mine = own[k, :width], own_other[k, :width]
        theirs = got[k, :width], got_other[k, :width]
        after.append([pick(down, a, b) for a, b in zip(mine, theirs)])
        before.append(pick(down, theirs[0], mine[0]))
        inner.append([pick(down, b, a) for a, b in zip(offsets_of(own, k), offsets_of(got, k))])
    for m in range(SWEEPS):
        for target in (m % 2, 1 - m % 2):
            stack = jnp.concatenate([after[d][(target + d) % 2] for d in range(m + 1)], axis=0)
            left = jnp.concatenate([inner[m - d][(target + d) % 2] for d in range(m + 1)], axis=1)
            if target == m % 2:
                top = jnp.concatenate([before[m - d] for d in range(m + 1)], axis=1)
                left = jnp.concatenate([top, left], axis=0)
            total = dot(left, stack)
            if target == m % 2:
                outs[0][m, :width] = total[:width].astype(BF16)
                total = total[width:]
            added = pick(down, offsets_of(own, m)[target], offsets_of(got, m)[target]).astype(F32)
            at = target * share if len(outs) == 2 else width + target * share
            outs[-1][m, at : at + share] = (total + added).astype(BF16)


def halves_of(ref, k):
    share = ref.shape[1] // 2
    return ref[k, :share], ref[k, share:]


def moved_by(values, maps, k):
    pair = []
    for target in (0, 1):
        stack = jnp.concatenate([maps[d][(target + d) % 2] for d in range(k + 1)], axis=0)
        left = jnp.concatenate([values[k - d][(target + d) % 2] for d in range(k + 1)], axis=1)
        pair.append(dot(left, stack))
    return pair


def join_kernel(even, odd, entry, own, joined):
    maps = [(even[k], odd[k]) for k in range(SWEEPS)]
    values = [halves_of(entry, k) for k in range(SWEEPS)]
    share = own.shape[1] // 2
    for k in range(SWEEPS):
        added = halves_of(own, k)
        for target, total in enumerate(moved_by(values, maps, k)):
            total = total + added[target].astype(F32)
            joined[k, target * share : (target + 1) * share] = total.astype(BF16)


def resolve_kernel(place, line, *refs, groups, count, face, masks):
    weights, gains, ahead, second, third, ahead_even, ahead_odd = refs[:7]
    levels = len(masks) - 2
    lower = refs[7 : 7 + 2 * levels]
    wanted = refs[7 + 2 * levels : 7 + 2 * levels + groups]
    states, lags, inflows = refs[7 + 2 * levels + groups :]
    me = place[0]
    half = groups // 2
    states[...] = jnp.zeros_like(states)
    flags = [(line[0] // mask) % 2 for mask in masks]
    maps = [(ahead_even[k], ahead_odd[k]) for k in range(SWEEPS)]
    given = [halves_of(third, k) for k in range(SWEEPS)]
    values = []
    for k in range(SWEEPS):
        pair = []
        for target, total in enumerate(moved_by(given, maps, k)):
            own = halves_of(ahead, k)[target]
            last = (total + own.astype(F32)).astype(BF16)
            upper = pick(flags[-2], last, halves_of(second, k)[target])
            pair.append(pick(flags[-1], upper, pick(flags[-2], own, jnp.zeros_like(own))))
        values.append(pair)
    for level in range(levels - 1, -1, -1):
        even, odd = lower[2 * level : 2 * level + 2]
        width = even.shape[2]
        maps = [(even[k, :width], odd[k, :width]) for k in range(SWEEPS)]
        moved = []
        for k in range(SWEEPS):
            pair = []
            for target, total in enumerate(moved_by(values, maps, k)):
                total = total + offsets_of(even, k)[target].astype(F32)
                pair.append(pick(flags[level], total.astype(BF16), values[k][target]))
            moved.append(pair)
        values = moved
    blank = jnp.zeros((values[0][0].shape[0], 2 * face), BF16)
    for k in range(SWEEPS):
        for pos in range(groups):
            tile = (pos % half) // 2
            both = values[k][pos // half][:, tile * 2 * face : (tile + 1) * 2 * face]
            inflows[k, pos] = by_half(both if pos % 2 == 0 else turned(both), blank)

    def sweep(k, carry):
        read_lags(me, states, lags, groups, count)

        def block(t):
            chosen = tuple(4 * t + i for i in range(4))
            run_chains(
                chosen, [inflows[k, pos] for pos in chosen], lags, weights, gains, states, count, face
            )

        over(groups // 4, block, 1)
        return carry

    lax.fori_loop(0, SWEEPS - 1, sweep, 0)
    read_lags(me, states, lags, groups, count)
    for t in range(groups // 4):
        chosen = tuple(4 * t + i for i in range(4))
        entries = [inflows[SWEEPS - 1, pos] for pos in chosen]
        outs = run_chains(chosen, entries, lags, weights, gains, states, count, face)
        for i, pos in enumerate(chosen):
            target = wanted[reversed_static(pos, groups)]
            traces = [entries[i]] + [o.astype(BF16) for o in outs[i][:-1]]
            for p in range(count):
                target[p] = lags[pos, p]
            target[count] = by_half(traces[0], traces[-1])
            for m in range(1, count // 2):
                target[count + m] = by_half(traces[2 * m - 1], traces[2 * m])


def final_kernel(place, order, inverse, coupling, given, *refs):
    wanted = refs[:-2]
    placed, gathered = refs[-2:]
    count, nodes, width = given.shape
    face = coupling.shape[1] // 3
    share = width // len(wanted)
    for rel, ref in enumerate(wanted):
        at = pl.multiple_of((place[0] ^ rel) * share, share)
        for m in range(ref.shape[0]):
            gathered[m, pl.ds(at, share), :] = ref[m].astype(F32)
    blank = jnp.zeros((face, nodes), BF16)
    for p in range(count):
        slot = order[p]
        rows = coupling[slot]
        second = p == count - 1 or (p > 0 and p % 2 == 0)
        tile = 0 if p == count - 1 else (p + 1) // 2
        pair = [blank, rows[:face]] if second else [rows[:face], blank]
        sides = jnp.concatenate([rows[2 * face :], rows[face : 2 * face]] + pair, axis=0)
        traces = jnp.concatenate([gathered[p], gathered[count + tile]], axis=1).astype(BF16)
        source = given[slot].astype(F32) + dot(traces, sides).T
        placed[slot] = dot(inverse[slot], source.astype(BF16)).astype(BF16)


def gather_list(sends, axis):
    masks = bits_of(lax.axis_size(axis))
    values = [sends[0]]
    for mask, send in zip(masks[::-1], sends[::-1]):
        values = values + [swap(send if i == 0 else v, axis, mask) for i, v in enumerate(values)]
    return values


def exchange(values, axis):
    return [v if rel == 0 else swap(v, axis, rel) for rel, v in enumerate(values)]


def call(kernel, outs, scratch, scalars, arrays, far=0, others=(), grant=0):
    def size(shape, kind):
        total = jnp.dtype(kind).itemsize
        for extent in shape:
            total *= extent
        return total

    held = sum(size(o.shape, o.dtype) for o in outs) + sum(size(a.shape, a.dtype) for a in arrays)
    held += sum(size(shape, kind) for shape, kind in scratch)
    return pl.pallas_call(
        kernel,
        out_shape=outs,
        in_specs=[SMEM] * len(scalars) + [VMEM] * (len(arrays) - far) + [HBM] * far,
        out_specs=[VMEM] * len(outs),
        scratch_shapes=[*others[:1], *[pltpu.VMEM(shape, kind) for shape, kind in scratch], *others[1:]],
        compiler_params=pltpu.CompilerParams(vmem_limit_bytes=grant or min(held + (6 << 20), 60 << 20)),
    )(*scalars, *arrays)


def shards(right_sides, inverse, coupling, sweep_order):
    given = right_sides[0, 0]
    inverse = inverse[0, 0]
    order = sweep_order[0, 0]
    count, nodes, width = given.shape
    face = coupling.shape[4]
    coupling = coupling[0, 0].reshape(count, 3 * face, nodes)
    groups = lax.axis_size("span")
    share = width // groups
    half = groups // 2
    place = lax.axis_index("span").astype(jnp.int32).reshape(1)
    line = lax.axis_index("stream").astype(jnp.int32).reshape(1)
    masks = bits_of(lax.axis_size("stream"))
    tiles = count + count // 2
    shape = jax.ShapeDtypeStruct
    spans = bits_of(groups)
    kept, *sends = call(
        facemap_kernel,
        [shape((tiles * share, 2 * face), BF16)]
        + [shape((tiles * (3 * face + mask * share), 2 * face), BF16) for mask in spans],
        [
            (inverse.shape, BF16),
            (coupling.shape, BF16),
            (given.shape, BF16),
            ((tiles, width, 2 * face), F32),
        ],
        [place],
        [pltpu.with_memory_space_constraint(a, pltpu.HBM) for a in (order, inverse, coupling, given)],
        4,
        (pltpu.SMEM(order.shape, order.dtype), pltpu.SemaphoreType.DMA, pltpu.SemaphoreType.DMA((3, count))),
    )
    arrays = gather_list(sends, "span")
    rows = share + half * face
    sizes = dict(groups=groups, count=count, face=face)
    pack, weights, gains = call(
        functools.partial(respond_kernel, **sizes),
        [
            shape((SWEEPS, half * face + 2 * share, half * face), BF16),
            shape((groups, count, 4 * face, 4 * face), BF16),
            shape((groups, count, share, 4 * face), F32),
        ],
        [
            ((groups + 1, count, rows, 2 * face), BF16),
            ((groups, count, rows, 2 * face), BF16),
            ((2, groups, rows, 2 * face), BF16),
        ],
        [place],
        [*arrays, kept],
    )
    levels = []
    for mask in masks[:-2]:
        other = swap(pack, "span", 1)
        got = swap(pack, "stream", mask)
        got_other = swap(got, "span", 1)
        levels += [got, got_other]
        if mask == masks[-3]:
            wide = [pack.shape[2], 2 * share]
        else:
            wide = [pack.shape[1]]
        pack, *rest = call(
            functools.partial(compose_kernel, mask=mask),
            [shape((SWEEPS, extent, pack.shape[2]), BF16) for extent in wide],
            [],
            [line],
            [pack, other, got, got_other],
        )
    (offset,) = rest
    ahead = swap(offset, "stream", masks[-2])
    other = swap(pack, "span", 1)
    ahead_even = swap(pack, "stream", masks[-2])
    (joined,) = call(join_kernel, [shape(offset.shape, BF16)], [], [], [pack, other, ahead, offset])
    second = lax.ppermute(joined, "stream", crossing(masks))
    third = swap(joined, "stream", masks[-1])
    ahead_odd = swap(ahead_even, "span", 1)
    wanted = call(
        functools.partial(resolve_kernel, masks=masks, **sizes),
        [shape((tiles, share, 2 * face), BF16)] * groups,
        [
            ((groups + 1, count, share, 2 * face), BF16),
            ((groups, count, share, 2 * face), BF16),
            ((SWEEPS, groups, share, 2 * face), BF16),
        ],
        [place, line],
        [weights, gains, ahead, second, third, ahead_even, ahead_odd, *levels],
    )
    wanted = exchange(wanted, "span")
    (placed,) = call(
        final_kernel,
        [shape((count, nodes, width), BF16)],
        [((tiles, width, 2 * face), F32)],
        [place, order],
        [inverse, coupling, given, *wanted],
    )
    return placed[None, None]


def solution(mesh):
    in_specs = (
        P("stream", "span", None, None, None),
        P("stream", "span", None, None, None),
        P("stream", "span", None, None, None, None),
        P("stream", "span", None),
    )
    out_specs = P("stream", "span", None, None, None)
    return jax.shard_map(shards, mesh=mesh, in_specs=in_specs, out_specs=out_specs, check_vma=False)
```

profile of v0, /device:TPU:0, one launch (start us, length us, event | category | flops | bytes accessed | tf_op | source)
XLA Modules:
  0.0 63.9 jit_solution(12171598225862537606)
XLA Ops:
  0.0 3.1 %shard_map.46 = (bf16[192,128]{1,0:T(8,128)(2,1)S(1)}, bf16[1344,128]{1,0:T(8,128)(2,1)S(1)}, bf16[1536,128]{1,0:T(8,128)(2,1)S(1)}) custom-call(s32[1]{0:T(128)} %bitcast.place, s32[4]{0:T(128)} %bitcast.13, bf16[4,512,512]{2,1,0:T(8,128)(2,1)} %bitcast.7, bf16[4,192,512]{2,1,0:T(8,128)(2,1)} %bitcast.9, bf16[4,512,128]{2,1,0:T(8,128)(2,1)} %bitcast.11), custom_call_target="tpu_custom_call" | custom-call | tf_op jit(solution)/shard_map/pallas_call | solution.py:433
  3.1 2.8 %collective-permute-start = (bf16[1536,128]{1,0:T(8,128)(2,1)S(1)}, bf16[1536,128]{1,0:T(8,128)(2,1)S(1)}, u32[]{:S(2)}, u32[]{:S(2)}) collective-permute-start(bf16[1536,128]{1,0:T(8,128)(2,1)S(1)} %get-tuple-element.18), channel_id=1, source_target_pairs={{0,2},{1,3},{2,0},{3,1},{4,6},{5,7},{6,4},{7,5},{8,10},{9,11},{10,... | collective-permute-start | bytes 1179656 | tf_op jit(solution)/shard_map/ppermute | solution.py:38
  5.9 9.5 %collective-permute-done.refs_1_ = bf16[1536,128]{1,0:T(8,128)(2,1)S(1)} collective-permute-done((bf16[1536,128]{1,0:T(8,128)(2,1)S(1)}, bf16[1536,128]{1,0:T(8,128)(2,1)S(1)}, u32[]{:S(2)}, u32[]{:S(2)}) %collective-permute-start) | collective-permute-done | bytes 393248 | tf_op jit(solution)/shard_map/ppermute | solution.py:38
  15.4 0.5 collective-permute-start.1
  15.9 1.7 %collective-permute-done.1.refs_2_ = bf16[1344,128]{1,0:T(8,128)(2,1)S(1)} collective-permute-done((bf16[1344,128]{1,0:T(8,128)(2,1)S(1)}, bf16[1344,128]{1,0:T(8,128)(2,1)S(1)}, u32[]{:S(2)}, u32[]{:S(2)}) %collective-permute-start.1) | collective-permute-done | bytes 344096 | tf_op jit(solution)/shard_map/ppermute | solution.py:38
  17.6 4.4 %shard_map.47 = (bf16[6,192,128]{2,1,0:T(8,128)(2,1)S(1)}, bf16[4,4,256,256]{3,2,1,0:T(8,128)(2,1)S(1)}, f32[4,4,32,256]{3,2,1,0:T(8,128)S(1)}) custom-call(s32[1]{0:T(128)} %bitcast.place, bf16[1344,128]{1,0:T(8,128)(2,1)S(1)} %get-tuple-element.17.refs_0_, bf16[1536,128]{1,0:T(8,128)(2,1)S(1)} %collective-permute-done.refs_1_, ...), custom_call_target="tpu_custom_call" | custom-call | tf_op jit(solution)/shard_map/pallas_call | solution.py:433
  22.0 2.1 %collective-permute-start.4 = (bf16[6,192,128]{2,1,0:T(8,128)(2,1)S(1)}, bf16[6,192,128]{2,1,0:T(8,128)(2,1)S(1)}, u32[]{:S(2)}, u32[]{:S(2)}) collective-permute-start(bf16[6,192,128]{2,1,0:T(8,128)(2,1)S(1)} %get-tuple-element.22.own), channel_id=1, source_target_pairs={{0,4},{4,0},{8,12},{12,8},{16,20},{20,16},{24,28},{28,24},{1,5},{5... | collective-permute-start | bytes 884744 | tf_op jit(solution)/shard_map/ppermute | solution.py:38
  24.1 7.3 %collective-permute-done.4.got.refs_7_ = bf16[6,192,128]{2,1,0:T(8,128)(2,1)S(1)} collective-permute-done((bf16[6,192,128]{2,1,0:T(8,128)(2,1)S(1)}, bf16[6,192,128]{2,1,0:T(8,128)(2,1)S(1)}, u32[]{:S(2)}, u32[]{:S(2)}) %collective-permute-start.4) | collective-permute-done | bytes 294944 | tf_op jit(solution)/shard_map/ppermute | solution.py:38
  31.4 1.6 %collective-permute-done.5.got_other.refs_8_ = bf16[6,192,128]{2,1,0:T(8,128)(2,1)S(1)} collective-permute-done((bf16[6,192,128]{2,1,0:T(8,128)(2,1)S(1)}, bf16[6,192,128]{2,1,0:T(8,128)(2,1)S(1)}, u32[]{:S(2)}, u32[]{:S(2)}) %collective-permute-start.5) | collective-permute-done | bytes 294944 | tf_op jit(solution)/shard_map/ppermute | solution.py:38
  33.0 1.5 %shard_map.48 = (bf16[6,128,128]{2,1,0:T(8,128)(2,1)S(1)}, bf16[6,64,128]{2,1,0:T(8,128)(2,1)S(1)}) custom-call(s32[1]{0:T(128)} %bitcast.5.line, bf16[6,192,128]{2,1,0:T(8,128)(2,1)S(1)} %get-tuple-element.22.own, bf16[6,192,128]{2,1,0:T(8,128)(2,1)} %collective-permute-done.3.own_other, bf16[6,192,128]{2,1,0:T(8,128)(2,1)S(1)} %collective-permute-done.4.got.refs_7_, ...), custom_call_target="tpu_custom_call" | custom-call | tf_op jit(solution)/shard_map/pallas_call | solution.py:433
  34.4 1.9 %collective-permute-start.10 = (bf16[6,128,128]{2,1,0:T(8,128)(2,1)S(1)}, bf16[6,128,128]{2,1,0:T(8,128)(2,1)S(1)}, u32[]{:S(2)}, u32[]{:S(2)}) collective-permute-start(bf16[6,128,128]{2,1,0:T(8,128)(2,1)S(1)} %get-tuple-element.24.even), channel_id=1, source_target_pairs={{0,8},{4,12},{8,0},{12,4},{16,24},{20,28},{24,16},{28,20},{1,9},{5... | collective-permute-start | bytes 589832 | tf_op jit(solution)/shard_map/ppermute | solution.py:38
  36.3 0.2 collective-permute-start.6
  36.5 5.7 %collective-permute-done.10.refs_5_ = bf16[6,128,128]{2,1,0:T(8,128)(2,1)S(1)} collective-permute-done((bf16[6,128,128]{2,1,0:T(8,128)(2,1)S(1)}, bf16[6,128,128]{2,1,0:T(8,128)(2,1)S(1)}, u32[]{:S(2)}, u32[]{:S(2)}) %collective-permute-start.10) | collective-permute-done | bytes 196640 | tf_op jit(solution)/shard_map/ppermute | solution.py:38
  42.3 1.3 %collective-permute-done.6.entry.refs_2_ = bf16[6,64,128]{2,1,0:T(8,128)(2,1)S(1)} collective-permute-done((bf16[6,64,128]{2,1,0:T(8,128)(2,1)S(1)}, bf16[6,64,128]{2,1,0:T(8,128)(2,1)S(1)}, u32[]{:S(2)}, u32[]{:S(2)}) %collective-permute-start.6) | collective-permute-done | bytes 98336 | tf_op jit(solution)/shard_map/ppermute | solution.py:38
  43.6 0.3 shard_map.49
  44.0 2.3 %collective-permute-start.9 = (bf16[6,64,128]{2,1,0:T(8,128)(2,1)S(1)}, bf16[6,64,128]{2,1,0:T(8,128)(2,1)S(1)}, u32[]{:S(2)}, u32[]{:S(2)}) collective-permute-start(bf16[6,64,128]{2,1,0:T(8,128)(2,1)S(1)} %shard_map.49), channel_id=1, source_target_pairs={{0,16},{4,20},{8,24},{12,28},{16,0},{20,4},{24,8},{28,12},{1,17},{... | collective-permute-start | bytes 294920 | tf_op jit(solution)/shard_map/ppermute | solution.py:38
  46.3 1.7 %collective-permute-start.8 = (bf16[6,64,128]{2,1,0:T(8,128)(2,1)S(1)}, bf16[6,64,128]{2,1,0:T(8,128)(2,1)S(1)}, u32[]{:S(2)}, u32[]{:S(2)}) collective-permute-start(bf16[6,64,128]{2,1,0:T(8,128)(2,1)S(1)} %shard_map.49), channel_id=1, source_target_pairs={{0,4},{4,0},{8,16},{12,20},{16,8},{20,12},{24,28},{28,24},{1,5},{5... | collective-permute-start | bytes 294920 | tf_op jit(solution)/shard_map/ppermute | solution.py:514
  48.1 4.1 %collective-permute-done.9.refs_4_ = bf16[6,64,128]{2,1,0:T(8,128)(2,1)S(1)} collective-permute-done((bf16[6,64,128]{2,1,0:T(8,128)(2,1)S(1)}, bf16[6,64,128]{2,1,0:T(8,128)(2,1)S(1)}, u32[]{:S(2)}, u32[]{:S(2)}) %collective-permute-start.9) | collective-permute-done | bytes 98336 | tf_op jit(solution)/shard_map/ppermute | solution.py:38
  52.2 4.0 %shard_map.50 = (bf16[6,32,128]{2,1,0:T(8,128)(2,1)S(1)}, bf16[6,32,128]{2,1,0:T(8,128)(2,1)S(1)}, bf16[6,32,128]{2,1,0:T(8,128)(2,1)S(1)}, bf16[6,32,128]{2,1,0:T(8,128)(2,1)S(1)}) custom-call(s32[1]{0:T(128)} %bitcast.place, s32[1]{0:T(128)} %bitcast.5.line, bf16[4,4,256,256]{3,2,1,0:T(8,128)(2,1)S(1)} %get-tuple-element.20.refs_0_, ...), custom_call_target="tpu_custom_call" | custom-call | tf_op jit(solution)/shard_map/pallas_call | solution.py:433
  56.3 1.2 %collective-permute-start.13 = (bf16[6,32,128]{2,1,0:T(8,128)(2,1)S(1)}, bf16[6,32,128]{2,1,0:T(8,128)(2,1)S(1)}, u32[]{:S(2)}, u32[]{:S(2)}) collective-permute-start(bf16[6,32,128]{2,1,0:T(8,128)(2,1)S(1)} %get-tuple-element.27), channel_id=1, source_target_pairs={{0,2},{1,3},{2,0},{3,1},{4,6},{5,7},{6,4},{7,5},{8,10},{9,11},{10,... | collective-permute-start | bytes 147464 | tf_op jit(solution)/shard_map/ppermute | solution.py:38
  57.5 0.6 collective-permute-start.14
  58.2 2.3 %collective-permute-done.13.refs_2_ = bf16[6,32,128]{2,1,0:T(8,128)(2,1)S(1)} collective-permute-done((bf16[6,32,128]{2,1,0:T(8,128)(2,1)S(1)}, bf16[6,32,128]{2,1,0:T(8,128)(2,1)S(1)}, u32[]{:S(2)}, u32[]{:S(2)}) %collective-permute-start.13) | collective-permute-done | bytes 49184 | tf_op jit(solution)/shard_map/ppermute | solution.py:38
  60.5 0.8 %collective-permute-done.14.refs_3_ = bf16[6,32,128]{2,1,0:T(8,128)(2,1)S(1)} collective-permute-done((bf16[6,32,128]{2,1,0:T(8,128)(2,1)S(1)}, bf16[6,32,128]{2,1,0:T(8,128)(2,1)S(1)}, u32[]{:S(2)}, u32[]{:S(2)}) %collective-permute-start.14) | collective-permute-done | bytes 49184 | tf_op jit(solution)/shard_map/ppermute | solution.py:38
  61.3 2.6 %shard_map.51 = bf16[4,512,128]{2,1,0:T(8,128)(2,1)} custom-call(s32[1]{0:T(128)} %bitcast.place, s32[4]{0:T(128)S(1)} %bitcast.14, bf16[4,512,512]{2,1,0:T(8,128)(2,1)S(1)} %bitcast.8, bf16[4,192,512]{2,1,0:T(8,128)(2,1)S(1)} %bitcast.10, bf16[4,512,128]{2,1,0:T(8,128)(2,1)S(1)} %bitcast.12, bf16[6,32,128]{2,1,0:T(8,128)(2,1)S(1)} %get-tuple-element.25.refs_0_, ...), custom_call_target="tpu_custom_call" | custom-call | tf_op jit(solution)/shard_map/pallas_call | solution.py:433
  (20 shorter events, 0.1 us)
Async XLA Ops:
  3.1 12.2 %collective-permute-start = (bf16[1536,128]{1,0:T(8,128)(2,1)S(1)}, bf16[1536,128]{1,0:T(8,128)(2,1)S(1)}, u32[]{:S(2)}, u32[]{:S(2)}) collective-permute-start(bf16[1536,128]{1,0:T(8,128)(2,1)S(1)} %get-tuple-element.18), channel_id=1, source_target_pairs={{0,2},{1,3},{2,0},{3,1},{4,6},{5,7},{6,4},{7,5},{8,10},{9,11},{10,... | collective-permute-start | bytes 1179656 | tf_op jit(solution)/shard_map/ppermute | solution.py:38
  15.4 2.2 %collective-permute-start.2 = (bf16[1536,128]{1,0:T(8,128)(2,1)S(1)}, bf16[1536,128]{1,0:T(8,128)(2,1)S(1)}, u32[]{:S(2)}, u32[]{:S(2)}) collective-permute-start(bf16[1536,128]{1,0:T(8,128)(2,1)S(1)} %collective-permute-done.refs_1_), channel_id=1, source_target_pairs={{0,1},{1,0},{2,3},{3,2},{4,5},{5,4},{6,7},{7,6},{8,9},{9,8},{10,11... | collective-permute-start | bytes 1179656 | tf_op jit(solution)/shard_map/ppermute | solution.py:38
  15.4 2.2 %collective-permute-start.1 = (bf16[1344,128]{1,0:T(8,128)(2,1)S(1)}, bf16[1344,128]{1,0:T(8,128)(2,1)S(1)}, u32[]{:S(2)}, u32[]{:S(2)}) collective-permute-start(bf16[1344,128]{1,0:T(8,128)(2,1)S(1)} %get-tuple-element.17.refs_0_), channel_id=1, source_target_pairs={{0,1},{1,0},{2,3},{3,2},{4,5},{5,4},{6,7},{7,6},{8,9},{9,8},{10,11... | collective-permute-start | bytes 1032200 | tf_op jit(solution)/shard_map/ppermute | solution.py:38
  22.0 9.4 %collective-permute-start.4 = (bf16[6,192,128]{2,1,0:T(8,128)(2,1)S(1)}, bf16[6,192,128]{2,1,0:T(8,128)(2,1)S(1)}, u32[]{:S(2)}, u32[]{:S(2)}) collective-permute-start(bf16[6,192,128]{2,1,0:T(8,128)(2,1)S(1)} %get-tuple-element.22.own), channel_id=1, source_target_pairs={{0,4},{4,0},{8,12},{12,8},{16,20},{20,16},{24,28},{28,24},{1,5},{5... | collective-permute-start | bytes 884744 | tf_op jit(solution)/shard_map/ppermute | solution.py:38
  24.1 7.3 %collective-permute-start.3 = (bf16[6,192,128]{2,1,0:T(8,128)(2,1)S(1)}, bf16[6,192,128]{2,1,0:T(8,128)(2,1)}, u32[]{:S(2)}, u32[]{:S(2)}) collective-permute-start(bf16[6,192,128]{2,1,0:T(8,128)(2,1)S(1)} %get-tuple-element.22.own), channel_id=1, source_target_pairs={{0,1},{1,0},{2,3},{3,2},{4,5},{5,4},{6,7},{7,6},{8,9},{9,8},{10,11... | collective-permute-start | bytes 884744 | tf_op jit(solution)/shard_map/ppermute | solution.py:38
  31.4 1.6 %collective-permute-start.5 = (bf16[6,192,128]{2,1,0:T(8,128)(2,1)S(1)}, bf16[6,192,128]{2,1,0:T(8,128)(2,1)S(1)}, u32[]{:S(2)}, u32[]{:S(2)}) collective-permute-start(bf16[6,192,128]{2,1,0:T(8,128)(2,1)S(1)} %collective-permute-done.4.got.refs_7_), channel_id=1, source_target_pairs={{0,1},{1,0},{2,3},{3,2},{4,5},{5,4},{6,7},{7,6},{8,9},{9,8},{10,11... | collective-permute-start | bytes 884744 | tf_op jit(solution)/shard_map/ppermute | solution.py:38
  34.4 7.8 %collective-permute-start.10 = (bf16[6,128,128]{2,1,0:T(8,128)(2,1)S(1)}, bf16[6,128,128]{2,1,0:T(8,128)(2,1)S(1)}, u32[]{:S(2)}, u32[]{:S(2)}) collective-permute-start(bf16[6,128,128]{2,1,0:T(8,128)(2,1)S(1)} %get-tuple-element.24.even), channel_id=1, source_target_pairs={{0,8},{4,12},{8,0},{12,4},{16,24},{20,28},{24,16},{28,20},{1,9},{5... | collective-permute-start | bytes 589832 | tf_op jit(solution)/shard_map/ppermute | solution.py:38
  36.3 7.3 %collective-permute-start.7 = (bf16[6,128,128]{2,1,0:T(8,128)(2,1)S(1)}, bf16[6,128,128]{2,1,0:T(8,128)(2,1)S(1)}, u32[]{:S(2)}, u32[]{:S(2)}) collective-permute-start(bf16[6,128,128]{2,1,0:T(8,128)(2,1)S(1)} %get-tuple-element.24.even), channel_id=1, source_target_pairs={{0,1},{1,0},{2,3},{3,2},{4,5},{5,4},{6,7},{7,6},{8,9},{9,8},{10,11... | collective-permute-start | bytes 589832 | tf_op jit(solution)/shard_map/ppermute | solution.py:38
  36.3 7.3 %collective-permute-start.6 = (bf16[6,64,128]{2,1,0:T(8,128)(2,1)S(1)}, bf16[6,64,128]{2,1,0:T(8,128)(2,1)S(1)}, u32[]{:S(2)}, u32[]{:S(2)}) collective-permute-start(bf16[6,64,128]{2,1,0:T(8,128)(2,1)S(1)} %get-tuple-element.23.own), channel_id=1, source_target_pairs={{0,8},{4,12},{8,0},{12,4},{16,24},{20,28},{24,16},{28,20},{1,9},{5... | collective-permute-start | bytes 294920 | tf_op jit(solution)/shard_map/ppermute | solution.py:38
  42.3 9.9 %collective-permute-start.11 = (bf16[6,128,128]{2,1,0:T(8,128)(2,1)S(1)}, bf16[6,128,128]{2,1,0:T(8,128)(2,1)S(1)}, u32[]{:S(2)}, u32[]{:S(2)}) collective-permute-start(bf16[6,128,128]{2,1,0:T(8,128)(2,1)S(1)} %collective-permute-done.10.refs_5_), channel_id=1, source_target_pairs={{0,1},{1,0},{2,3},{3,2},{4,5},{5,4},{6,7},{7,6},{8,9},{9,8},{10,11... | collective-permute-start | bytes 589832 | tf_op jit(solution)/shard_map/ppermute | solution.py:38
  43.9 17.3 %copy-start = (bf16[1,1,4,512,512]{4,3,2,1,0:T(8,128)(2,1)S(1)}, bf16[1,1,4,512,512]{4,3,2,1,0:T(8,128)(2,1)}, u32[]{:S(2)}) copy-start(bf16[1,1,4,512,512]{4,3,2,1,0:T(8,128)(2,1)} %param.5) | copy-start | bytes 6291460
  44.0 17.3 %copy-start.1 = (bf16[1,1,4,3,64,512]{5,4,3,2,1,0:T(8,128)(2,1)S(1)}, bf16[1,1,4,3,64,512]{5,4,3,2,1,0:T(8,128)(2,1)}, u32[]{:S(2)}) copy-start(bf16[1,1,4,3,64,512]{5,4,3,2,1,0:T(8,128)(2,1)} %param.6) | copy-start | bytes 2359300
  44.0 17.3 %copy-start.2 = (bf16[1,1,4,512,128]{4,3,2,1,0:T(8,128)(2,1)S(1)}, bf16[1,1,4,512,128]{4,3,2,1,0:T(8,128)(2,1)}, u32[]{:S(2)}) copy-start(bf16[1,1,4,512,128]{4,3,2,1,0:T(8,128)(2,1)} %param.4) | copy-start | bytes 1572868
  44.0 17.3 %copy-start.3 = (s32[1,1,4]{2,1,0:T(1,128)S(1)}, s32[1,1,4]{2,1,0:T(1,128)}, u32[]{:S(2)}) copy-start(s32[1,1,4]{2,1,0:T(1,128)} %param.7) | copy-start | bytes 52
  44.0 8.2 %collective-permute-start.9 = (bf16[6,64,128]{2,1,0:T(8,128)(2,1)S(1)}, bf16[6,64,128]{2,1,0:T(8,128)(2,1)S(1)}, u32[]{:S(2)}, u32[]{:S(2)}) collective-permute-start(bf16[6,64,128]{2,1,0:T(8,128)(2,1)S(1)} %shard_map.49), channel_id=1, source_target_pairs={{0,16},{4,20},{8,24},{12,28},{16,0},{20,4},{24,8},{28,12},{1,17},{... | collective-permute-start | bytes 294920 | tf_op jit(solution)/shard_map/ppermute | solution.py:38
  46.3 5.8 %collective-permute-start.8 = (bf16[6,64,128]{2,1,0:T(8,128)(2,1)S(1)}, bf16[6,64,128]{2,1,0:T(8,128)(2,1)S(1)}, u32[]{:S(2)}, u32[]{:S(2)}) collective-permute-start(bf16[6,64,128]{2,1,0:T(8,128)(2,1)S(1)} %shard_map.49), channel_id=1, source_target_pairs={{0,4},{4,0},{8,16},{12,20},{16,8},{20,12},{24,28},{28,24},{1,5},{5... | collective-permute-start | bytes 294920 | tf_op jit(solution)/shard_map/ppermute | solution.py:514
  56.2 1.9 %collective-permute-start.12 = (bf16[6,32,128]{2,1,0:T(8,128)(2,1)S(1)}, bf16[6,32,128]{2,1,0:T(8,128)(2,1)S(1)}, u32[]{:S(2)}, u32[]{:S(2)}) collective-permute-start(bf16[6,32,128]{2,1,0:T(8,128)(2,1)S(1)} %get-tuple-element.26), channel_id=1, source_target_pairs={{0,1},{1,0},{2,3},{3,2},{4,5},{5,4},{6,7},{7,6},{8,9},{9,8},{10,11... | collective-permute-start | bytes 147464 | tf_op jit(solution)/shard_map/ppermute | solution.py:38
  56.3 4.2 %collective-permute-start.13 = (bf16[6,32,128]{2,1,0:T(8,128)(2,1)S(1)}, bf16[6,32,128]{2,1,0:T(8,128)(2,1)S(1)}, u32[]{:S(2)}, u32[]{:S(2)}) collective-permute-start(bf16[6,32,128]{2,1,0:T(8,128)(2,1)S(1)} %get-tuple-element.27), channel_id=1, source_target_pairs={{0,2},{1,3},{2,0},{3,1},{4,6},{5,7},{6,4},{7,5},{8,10},{9,11},{10,... | collective-permute-start | bytes 147464 | tf_op jit(solution)/shard_map/ppermute | solution.py:38
  57.5 3.7 %collective-permute-start.14 = (bf16[6,32,128]{2,1,0:T(8,128)(2,1)S(1)}, bf16[6,32,128]{2,1,0:T(8,128)(2,1)S(1)}, u32[]{:S(2)}, u32[]{:S(2)}) collective-permute-start(bf16[6,32,128]{2,1,0:T(8,128)(2,1)S(1)} %get-tuple-element.28), channel_id=1, source_target_pairs={{0,3},{1,2},{2,1},{3,0},{4,7},{5,6},{6,5},{7,4},{8,11},{9,10},{10,... | collective-permute-start | bytes 147464 | tf_op jit(solution)/shard_map/ppermute | solution.py:38
where the time goes:
time: 64.1 us; the launch traced here: 63.9 us
  waiting for transfers between devices  34.3 us (54%)
  Pallas kernels  16 us (25%)
  starting transfers between devices  13.5 us (21%)
    ppermute x14, waiting for transfers between devices, swap(): return lax.ppermute(value, axis, [(i, i ^ mask) for i in range(count)])  34.3 us
    pallas_call x6, Pallas kernels, call(): pl.pallas_call(kernel, out_shape=outs, in_specs=[SMEM] * len(scalars) + [...  16 us
    ppermute x14, starting transfers between devices, swap(): return lax.ppermute(value, axis, [(i, i ^ mask) for i in range(count)])  11.7 us
    ppermute x1, starting transfers between devices, shards(): second = lax.ppermute(joined, 'stream', crossing(masks))  1.74 us
  transfers between devices with their start and end apart: 15, of which 9 were waited for; matrix products, arithmetic and copies ran while one was open for 0% of the time, Pallas kernels for 1%

commit v1 on v0

--- a/solution.py
+++ b/solution.py
@@ -63,10 +63,10 @@
     return pltpu.roll(value.astype(F32), value.shape[-1] // 2, 1).astype(value.dtype)
 
 
-def facemap_kernel(place, order_far, inverse_far, coupling_far, given_far, kept, *refs):
-    sends = refs[:-7]
+def facemap_kernel(place, order_far, inverse_far, coupling_far, given_far, maps, *refs):
+    gains = refs[:-7]
     order, inverse, coupling, given, gathered, order_done, done = refs[-7:]
-    groups = 1 << len(sends)
+    groups = len(gains)
     count, nodes, width = given.shape
     face = coupling.shape[1] // 3
     part = nodes // NP
@@ -102,14 +102,11 @@
         rows = jnp.concatenate([faces, outflow, outflow], axis=0)
         full = dot_nt(coupling[slot], rows)
         full = jnp.concatenate([full[2 * face :], full[face : 2 * face], full[:face]], axis=0).astype(BF16)
-        for maps in sends:
-            maps[p * 3 * face : (p + 1) * 3 * face, :] = full[:, : 2 * face]
+        maps[p * 3 * face : (p + 1) * 3 * face, :] = full[:, : 2 * face]
         outs.append(full[:, 2 * face :])
         if p % 2 == 1:
             at = (count + p // 2) * 3 * face
-            both = by_half(outs[p - 1], outs[p])
-            for maps in sends:
-                maps[at : at + 3 * face, :] = both
+            maps[at : at + 3 * face, :] = by_half(outs[p - 1], outs[p])
         every.append(dot(rows, given[slot]).T)
     tiles = [gain[:, : 2 * face] for gain in every]
     for p in range(0, count, 2):
@@ -119,21 +116,10 @@
     for rel in range(groups):
         at = pl.multiple_of((place[0] ^ rel) * share, share)
         for m in range(len(tiles)):
-            piece = gathered[m, pl.ds(at, share), :].astype(BF16)
-            if rel == 0:
-                kept[m * share : (m + 1) * share, :] = piece
-            else:
-                target = sends[rel.bit_length() - 1]
-                low = gain_row(rel, count, face, share) + m * share
-                target[low : low + share, :] = piece
-
-
-def gain_row(rel, count, face, share):
-    first = 1 << (rel.bit_length() - 1)
-    return (count + count // 2) * (3 * face + (rel - first) * share)
-
-
-def unpack(map_refs, kept, weights, gains, count, face):
+            gains[rel][m] = gathered[m, pl.ds(at, share), :].astype(BF16)
+
+
+def unpack_maps(map_refs, weights, count, face):
     for pos, ref in enumerate(map_refs):
         for p in range(count):
             sides = ref[p * 3 * face : (p + 1) * 3 * face, :]
@@ -144,17 +130,15 @@
             full = jnp.concatenate([sides, outs], axis=1)
             weights[pos, p, : 3 * face, :] = full
             weights[pos, p, 3 * face :, :] = full[2 * face :]
-    for pos in range(len(map_refs)):
-        rel = reversed_static(pos, len(map_refs))
-        ref = map_refs[pos] if rel else kept
-        share = gains.shape[2]
-        first = gain_row(rel, count, face, share) if rel else 0
+
+
+def unpack_gains(gain_refs, gains, count):
+    for rel, ref in enumerate(gain_refs):
         for p in range(count):
-            outs = ref[first + (count + p // 2) * share : first + (count + p // 2 + 1) * share]
+            outs = ref[count + p // 2]
             other = turned(outs)
             outs = by_half(outs, other) if p % 2 == 0 else by_half(other, outs)
-            sides = ref[first + p * share : first + (p + 1) * share]
-            gains[pos, p] = jnp.concatenate([sides, outs], axis=1).astype(F32)
+            gains[reversed_static(rel, len(gain_refs)), p] = jnp.concatenate([ref[p], outs], axis=1).astype(F32)
 
 
 def neighbours(me, pos, groups):
@@ -164,13 +148,14 @@
     return below, above
 
 
-def read_lags(me, states, lags, groups, count):
-    def read(pos):
+def read_lags(me, states, lags, groups, count, first=0, live=None):
+    def read(i):
+        pos = first + i
         below, above = neighbours(me, pos, groups)
         for p in range(count):
             lags[pos, p] = by_half(states[above, p], states[below, p])
 
-    over(groups, read)
+    over(live or groups, read)
 
 
 def over(count, body, limit=4):
@@ -192,18 +177,13 @@
 
 
 def run_chains(chosen, entries, lags, weights, gains, states, count, face):
-    share = gains.shape[2]
     outs = [[] for _ in chosen]
     for p in range(count):
         for i, pos in enumerate(chosen):
-            rows = entries[i].shape[0]
-            result = dot(jnp.concatenate([lags[pos, p, :rows], entries[i]], axis=1), weights[pos, p])
-            first = result[:share] + gains[pos, p]
-            if result.shape[0] == share:
-                result = first
-            else:
-                result = jnp.concatenate([first, result[share:]], axis=0)
-            states[pos, p, :rows] = result[:, : 2 * face].astype(BF16)
+            result = dot(jnp.concatenate([lags[pos, p], entries[i]], axis=1), weights[pos, p])
+            if gains is not None:
+                result = result + gains[pos, p]
+            states[pos, p] = result[:, : 2 * face].astype(BF16)
             outs[i].append(result[:, 2 * face :])
         if p < count - 1:
             entries = [split_trace(o[p])[0] for o in outs]
@@ -212,37 +192,27 @@
 
 def respond_kernel(place, *refs, groups, count, face):
     map_refs = refs[:groups]
-    kept, pack, weights, gains, states, lags, unit = refs[groups:]
+    response, weights, states, lags, unit = refs[groups:]
     me = place[0]
-    share = gains.shape[2]
-    rows = lags.shape[2]
     half = groups // 2
-    unpack(map_refs, kept, weights, gains, count, face)
+    unpack_maps(map_refs, weights, count, face)
     states[...] = jnp.zeros_like(states)
     unit[...] = jnp.zeros_like(unit)
-    row = lax.broadcasted_iota(jnp.int32, (rows, 2 * face), 0) - share
-    lane = lax.broadcasted_iota(jnp.int32, (rows, 2 * face), 1)
+    row = lax.broadcasted_iota(jnp.int32, unit.shape[2:], 0)
+    lane = lax.broadcasted_iota(jnp.int32, unit.shape[2:], 1)
     for pos in range(half):
         hit = jnp.logical_and(lane < face, row == lane + pos * face)
         unit[0, pos] = jnp.where(hit, 1.0, 0.0).astype(BF16)
 
     def sweep(k, parity):
-        read_lags(me, states, lags, groups, count)
+        read_lags(me, states, lags, groups, count, half * parity, half)
 
         def block(t):
-            live = [2 * t + half * parity, 2 * t + 1 + half * parity]
-            bare = [2 * t + half * (1 - parity), 2 * t + 1 + half * (1 - parity)]
-            entries = [unit[jnp.minimum(k, 1), pos] for pos in live]
-            entries += [jnp.zeros((share, 2 * face), BF16)] * 2
-            chosen = live + bare
-            ends = [outs[-1] for outs in run_chains(chosen, entries, lags, weights, gains, states, count, face)]
+            chosen = [2 * t + half * parity, 2 * t + 1 + half * parity]
+            entries = [unit[jnp.minimum(k, 1), pos] for pos in chosen]
+            ends = [outs[-1] for outs in run_chains(chosen, entries, lags, weights, None, states, count, face)]
             at = pl.ds(pl.multiple_of(t * 2 * face, 2 * face), 2 * face)
-            answered = half * face
-            full = by_half(ends[0], ends[1])
-            pack[k, :answered, at] = full[share:].astype(BF16)
-            for target, tile in ((parity, full[:share]), (1 - parity, by_half(ends[2], ends[3]))):
-                low = answered + target * share
-                pack[k, low : low + share, at] = tile.astype(BF16)
+            response[k, :, at] = by_half(ends[0], ends[1]).astype(BF16)
 
         over(groups // 4, block, 1)
 
@@ -254,43 +224,64 @@
     lax.fori_loop(0, SWEEPS // 2, both, 0)
 
 
+def offset_kernel(place, weights, *refs, groups, count, face):
+    gain_refs = refs[:groups]
+    offset, gains, states, lags = refs[groups:]
+    me = place[0]
+    half = groups // 2
+    unpack_gains(gain_refs, gains, count)
+    states[...] = jnp.zeros_like(states)
+    share = gains.shape[2]
+    blank = jnp.zeros((share, 2 * face), BF16)
+
+    def sweep(k, carry):
+        read_lags(me, states, lags, groups, count)
+
+        def block(t):
+            chosen = [2 * t, 2 * t + 1, 2 * t + half, 2 * t + 1 + half]
+            outs = run_chains(chosen, [blank] * 4, lags, weights, gains, states, count, face)
+            ends = [out[-1] for out in outs]
+            at = pl.ds(pl.multiple_of(t * 2 * face, 2 * face), 2 * face)
+            offset[k, :share, at] = by_half(ends[0], ends[1]).astype(BF16)
+            offset[k, share:, at] = by_half(ends[2], ends[3]).astype(BF16)
+
+        over(groups // 4, block, 1)
+        return carry
+
+    lax.fori_loop(0, SWEEPS, sweep, 0)
+
+
 def pick(flag, first, second):
     return jnp.where(flag != 0, first, second)
 
 
-def offsets_of(ref, k):
-    width = ref.shape[2]
-    share = (ref.shape[1] - width) // 2
-    return ref[k, width : width + share], ref[k, width + share :]
-
-
-def compose_kernel(line, own, own_other, got, got_other, *outs, mask):
+def pair_offset_kernel(line, own, other, got, got_other, own_offset, got_offset, offset, *, mask):
     down = (line[0] // mask) % 2
-    width = own.shape[2]
-    share = (own.shape[1] - width) // 2
-    after = []
-    before = []
-    inner = []
+    share = own_offset.shape[1] // 2
+    maps = [
+        (pick(down, own[k], got[k]), pick(down, other[k], got_other[k])) for k in range(SWEEPS)
+    ]
+    values = []
     for k in range(SWEEPS):
-        mine = own[k, :width], own_other[k, :width]
-        theirs = got[k, :width], got_other[k, :width]
-        after.append([pick(down, a, b) for a, b in zip(mine, theirs)])
-        before.append(pick(down, theirs[0], mine[0]))
-        inner.append([pick(down, b, a) for a, b in zip(offsets_of(own, k), offsets_of(got, k))])
+        both = zip(halves_of(got_offset, k), halves_of(own_offset, k))
+        values.append([pick(down, a, b) for a, b in both])
+    for k in range(SWEEPS):
+        both = zip(halves_of(own_offset, k), halves_of(got_offset, k))
+        added = [pick(down, a, b).astype(F32) for a, b in both]
+        for target, total in enumerate(moved_by(values, maps, k)):
+            offset[k, target * share : (target + 1) * share] = (total + added[target]).astype(BF16)
+
+
+def pair_map_kernel(line, own, other, got, got_other, response, *, mask):
+    down = (line[0] // mask) % 2
+    after = [
+        (pick(down, own[k], got[k]), pick(down, other[k], got_other[k])) for k in range(SWEEPS)
+    ]
+    before = [pick(down, got[k], own[k]) for k in range(SWEEPS)]
     for m in range(SWEEPS):
-        for target in (m % 2, 1 - m % 2):
-            stack = jnp.concatenate([after[d][(target + d) % 2] for d in range(m + 1)], axis=0)
-            left = jnp.concatenate([inner[m - d][(target + d) % 2] for d in range(m + 1)], axis=1)
-            if target == m % 2:
-                top = jnp.concatenate([before[m - d] for d in range(m + 1)], axis=1)
-                left = jnp.concatenate([top, left], axis=0)
-            total = dot(left, stack)
-            if target == m % 2:
-                outs[0][m, :width] = total[:width].astype(BF16)
-                total = total[width:]
-            added = pick(down, offsets_of(own, m)[target], offsets_of(got, m)[target]).astype(F32)
-            at = target * share if len(outs) == 2 else width + target * share
-            outs[-1][m, at : at + share] = (total + added).astype(BF16)
+        stack = jnp.concatenate([after[d][(m + d) % 2] for d in range(m + 1)], axis=0)
+        left = jnp.concatenate([before[m - d] for d in range(m + 1)], axis=1)
+        response[m] = dot(left, stack).astype(BF16)
 
 
 def halves_of(ref, k):
@@ -321,9 +312,9 @@
 def resolve_kernel(place, line, *refs, groups, count, face, masks):
     weights, gains, ahead, second, third, ahead_even, ahead_odd = refs[:7]
     levels = len(masks) - 2
-    lower = refs[7 : 7 + 2 * levels]
-    wanted = refs[7 + 2 * levels : 7 + 2 * levels + groups]
-    states, lags, inflows = refs[7 + 2 * levels + groups :]
+    lower = refs[7 : 7 + 3 * levels]
+    wanted = refs[7 + 3 * levels : 7 + 3 * levels + groups]
+    states, lags, inflows = refs[7 + 3 * levels + groups :]
     me = place[0]
     half = groups // 2
     states[...] = jnp.zeros_like(states)
@@ -340,14 +331,13 @@
             pair.append(pick(flags[-1], upper, pick(flags[-2], own, jnp.zeros_like(own))))
         values.append(pair)
     for level in range(levels - 1, -1, -1):
-        even, odd = lower[2 * level : 2 * level + 2]
-        width = even.shape[2]
-        maps = [(even[k, :width], odd[k, :width]) for k in range(SWEEPS)]
+        even, odd, offset = lower[3 * level : 3 * level + 3]
+        maps = [(even[k], odd[k]) for k in range(SWEEPS)]
         moved = []
         for k in range(SWEEPS):
             pair = []
             for target, total in enumerate(moved_by(values, maps, k)):
-                total = total + offsets_of(even, k)[target].astype(F32)
+                total = total + halves_of(offset, k)[target].astype(F32)
                 pair.append(pick(flags[level], total.astype(BF16), values[k][target]))
             moved.append(pair)
         values = moved
@@ -409,11 +399,10 @@
         placed[slot] = dot(inverse[slot], source.astype(BF16)).astype(BF16)
 
 
-def gather_list(sends, axis):
-    masks = bits_of(lax.axis_size(axis))
-    values = [sends[0]]
-    for mask, send in zip(masks[::-1], sends[::-1]):
-        values = values + [swap(send if i == 0 else v, axis, mask) for i, v in enumerate(values)]
+def gather_list(value, axis):
+    values = [value]
+    for mask in bits_of(lax.axis_size(axis))[::-1]:
+        values = values + [swap(v, axis, mask) for v in values]
     return values
 
 
@@ -455,11 +444,9 @@
     masks = bits_of(lax.axis_size("stream"))
     tiles = count + count // 2
     shape = jax.ShapeDtypeStruct
-    spans = bits_of(groups)
-    kept, *sends = call(
+    maps, *gains = call(
         facemap_kernel,
-        [shape((tiles * share, 2 * face), BF16)]
-        + [shape((tiles * (3 * face + mask * share), 2 * face), BF16) for mask in spans],
+        [shape((tiles * 3 * face, 2 * face), BF16)] + [shape((tiles, share, 2 * face), BF16)] * groups,
         [
             (inverse.shape, BF16),
             (coupling.shape, BF16),
@@ -469,48 +456,65 @@
         [place],
         [pltpu.with_memory_space_constraint(a, pltpu.HBM) for a in (order, inverse, coupling, given)],
         4,
-        (pltpu.SMEM(order.shape, order.dtype), pltpu.SemaphoreType.DMA, pltpu.SemaphoreType.DMA((3, count))),
+        (
+            pltpu.SMEM(order.shape, order.dtype),
+            pltpu.SemaphoreType.DMA,
+            pltpu.SemaphoreType.DMA((3, count)),
+        ),
     )
-    arrays = gather_list(sends, "span")
-    rows = share + half * face
+    all_maps = gather_list(maps, "span")
+    gains = exchange(gains, "span")
     sizes = dict(groups=groups, count=count, face=face)
-    pack, weights, gains = call(
+    wide = half * face
+    response, weights = call(
         functools.partial(respond_kernel, **sizes),
         [
-            shape((SWEEPS, half * face + 2 * share, half * face), BF16),
+            shape((SWEEPS, wide, wide), BF16),
             shape((groups, count, 4 * face, 4 * face), BF16),
+        ],
+        [
+            ((groups + 1, count, wide, 2 * face), BF16),
+            ((groups, count, wide, 2 * face), BF16),
+            ((2, groups, wide, 2 * face), BF16),
+        ],
+        [place],
+        all_maps,
+    )
+    offset, gains = call(
+        functools.partial(offset_kernel, **sizes),
+        [
+            shape((SWEEPS, 2 * share, wide), BF16),
             shape((groups, count, share, 4 * face), F32),
         ],
         [
-            ((groups + 1, count, rows, 2 * face), BF16),
-            ((groups, count, rows, 2 * face), BF16),
-            ((2, groups, rows, 2 * face), BF16),
+            ((groups + 1, count, share, 2 * face), BF16),
+            ((groups, count, share, 2 * face), BF16),
         ],
         [place],
-        [*arrays, kept],
+        [weights, *gains],
     )
     levels = []
     for mask in masks[:-2]:
-        other = swap(pack, "span", 1)
-        got = swap(pack, "stream", mask)
+        got = swap(response, "stream", mask)
+        other = swap(response, "span", 1)
         got_other = swap(got, "span", 1)
-        levels += [got, got_other]
-        if mask == masks[-3]:
-            wide = [pack.shape[2], 2 * share]
-        else:
-            wide = [pack.shape[1]]
-        pack, *rest = call(
-            functools.partial(compose_kernel, mask=mask),
-            [shape((SWEEPS, extent, pack.shape[2]), BF16) for extent in wide],
+        got_offset = swap(offset, "stream", mask)
+        levels += [got, got_other, got_offset]
+        arrays = [response, other, got, got_other]
+        (offset,) = call(
+            functools.partial(pair_offset_kernel, mask=mask),
+            [shape(offset.shape, BF16)],
             [],
             [line],
-            [pack, other, got, got_other],
+            arrays + [offset, got_offset],
         )
-    (offset,) = rest
+        (response,) = call(
+            functools.partial(pair_map_kernel, mask=mask), [shape(response.shape, BF16)], [], [line], arrays
+        )
     ahead = swap(offset, "stream", masks[-2])
-    other = swap(pack, "span", 1)
-    ahead_even = swap(pack, "stream", masks[-2])
-    (joined,) = call(join_kernel, [shape(offset.shape, BF16)], [], [], [pack, other, ahead, offset])
+    other = swap(response, "span", 1)
+    ahead_even = swap(response, "stream", masks[-2])
+    (joined,) = call(join_kernel, [shape(offset.shape, BF16)], [], [], [response, other, ahead, offset])
     second = lax.ppermute(joined, "stream", crossing(masks))
     third = swap(joined, "stream", masks[-1])
     ahead_odd = swap(ahead_even, "span", 1)

time: 64.1 us -> 68.7 us (1.072)
  Pallas kernels: 16 us -> 17.8 us
  starting transfers between devices: 13.5 us -> 15.3 us
  waiting for transfers between devices: 34.3 us -> 35.3 us
    ppermute x1, waiting for transfers between devices: 0.01 us -> 2.25 us  [shards(): second = lax.ppermute(joined, 'stream', crossing(masks))]
    ppermute x14 -> x18, starting transfers between devices: 11.7 us -> 13.7 us  [swap(): return lax.ppermute(value, axis, [(i, i ^ mask) for i in range(count)])]
    pallas_call x6 -> x8, Pallas kernels: 16 us -> 17.8 us  [call(): pl.pallas_call(kernel, out_shape=outs, in_specs=[SMEM] * len(scalars) + [...]
    ppermute x14 -> x18, waiting for transfers between devices: 34.3 us -> 33 us  [swap(): return lax.ppermute(value, axis, [(i, i ^ mask) for i in range(count)])]
  transfers between devices with their start and end apart: 15 -> 19, of which waited for: 9 -> 12; matrix products, arithmetic and copies ran while one was open for 0% -> 0% of each run, Pallas kernels for 1% -> 6%
where the time goes in v1:
time: 68.7 us; the launch traced here: 68.6 us
  waiting for transfers between devices  35.3 us (51%)
  Pallas kernels  17.8 us (26%)
  starting transfers between devices  15.3 us (22%)
    ppermute x18, waiting for transfers between devices, swap(): return lax.ppermute(value, axis, [(i, i ^ mask) for i in range(count)])  33 us
    pallas_call x8, Pallas kernels, call(): pl.pallas_call(kernel, out_shape=outs, in_specs=[SMEM] * len(scalars) + [...  17.8 us
    ppermute x18, starting transfers between devices, swap(): return lax.ppermute(value, axis, [(i, i ^ mask) for i in range(count)])  13.7 us
    ppermute x1, waiting for transfers between devices, shards(): second = lax.ppermute(joined, 'stream', crossing(masks))  2.25 us
    ppermute x1, starting transfers between devices, shards(): second = lax.ppermute(joined, 'stream', crossing(masks))  1.6 us
  transfers between devices with their start and end apart: 19, of which 12 were waited for; matrix products, arithmetic and copies ran while one was open for 0% of the time, Pallas kernels for 6%

profile of v1, /device:TPU:0, one launch (start us, length us, event | category | flops | bytes accessed | tf_op | source)
XLA Modules:
  0.0 68.6 jit_solution(12255892459349220113)
XLA Ops:
  0.0 3.1 %shard_map.46 = (bf16[1152,128]{1,0:T(8,128)(2,1)S(1)}, bf16[6,32,128]{2,1,0:T(8,128)(2,1)S(1)}, bf16[6,32,128]{2,1,0:T(8,128)(2,1)S(1)}, bf16[6,32,128]{2,1,0:T(8,128)(2,1)S(1)}, bf16[6,32,128]{2,1,0:T(8,128)(2,1)S(1)}) custom-call(s32[1]{0:T(128)} %bitcast.place, s32[4]{0:T(128)} %bitcast.13, bf16[4,512,512]{2,1,0:T(8,128)(2,1)} %bitcast.7, ...), custom_call_target="tpu_custom_call" | custom-call | tf_op jit(solution)/shard_map/pallas_call | solution.py:422
  3.1 2.8 %collective-permute-start = (bf16[1152,128]{1,0:T(8,128)(2,1)S(1)}, bf16[1152,128]{1,0:T(8,128)(2,1)S(1)}, u32[]{:S(2)}, u32[]{:S(2)}) collective-permute-start(bf16[1152,128]{1,0:T(8,128)(2,1)S(1)} %get-tuple-element.18.refs_0_), channel_id=1, source_target_pairs={{0,2},{1,3},{2,0},{3,1},{4,6},{5,7},{6,4},{7,5},{8,10},{9,11},{10,... | collective-permute-start | bytes 884744 | tf_op jit(solution)/shard_map/ppermute | solution.py:38
  5.9 7.4 %collective-permute-done.refs_1_ = bf16[1152,128]{1,0:T(8,128)(2,1)S(1)} collective-permute-done((bf16[1152,128]{1,0:T(8,128)(2,1)S(1)}, bf16[1152,128]{1,0:T(8,128)(2,1)S(1)}, u32[]{:S(2)}, u32[]{:S(2)}) %collective-permute-start) | collective-permute-done | bytes 294944 | tf_op jit(solution)/shard_map/ppermute | solution.py:38
  13.3 1.6 %collective-permute-done.2.refs_3_ = bf16[1152,128]{1,0:T(8,128)(2,1)S(1)} collective-permute-done((bf16[1152,128]{1,0:T(8,128)(2,1)S(1)}, bf16[1152,128]{1,0:T(8,128)(2,1)S(1)}, u32[]{:S(2)}, u32[]{:S(2)}) %collective-permute-start.2) | collective-permute-done | bytes 294944 | tf_op jit(solution)/shard_map/ppermute | solution.py:38
  14.9 3.5 %shard_map.47 = (bf16[6,128,128]{2,1,0:T(8,128)(2,1)S(1)}, bf16[4,4,256,256]{3,2,1,0:T(8,128)(2,1)S(1)}) custom-call(s32[1]{0:T(128)} %bitcast.place, bf16[1152,128]{1,0:T(8,128)(2,1)S(1)} %get-tuple-element.18.refs_0_, bf16[1152,128]{1,0:T(8,128)(2,1)S(1)} %collective-permute-done.refs_1_, bf16[1152,128]{1,0:T(8,128)(2,1)S(1)} %collective-permute-done.1.refs_2_, ...), custom_call_target="tpu_custom_call" | custom-call | tf_op jit(solution)/shard_map/pallas_call | solution.py:422
  18.3 2.1 %collective-permute-start.7 = (bf16[6,128,128]{2,1,0:T(8,128)(2,1)S(1)}, bf16[6,128,128]{2,1,0:T(8,128)(2,1)S(1)}, u32[]{:S(2)}, u32[]{:S(2)}) collective-permute-start(bf16[6,128,128]{2,1,0:T(8,128)(2,1)S(1)} %get-tuple-element.25.own), channel_id=1, source_target_pairs={{0,4},{4,0},{8,12},{12,8},{16,20},{20,16},{24,28},{28,24},{1,5},{5... | collective-permute-start | bytes 589832 | tf_op jit(solution)/shard_map/ppermute | solution.py:38
  20.4 5.2 %collective-permute-done.7.got.refs_7_ = bf16[6,128,128]{2,1,0:T(8,128)(2,1)S(1)} collective-permute-done((bf16[6,128,128]{2,1,0:T(8,128)(2,1)S(1)}, bf16[6,128,128]{2,1,0:T(8,128)(2,1)S(1)}, u32[]{:S(2)}, u32[]{:S(2)}) %collective-permute-start.7) | collective-permute-done | bytes 196640 | tf_op jit(solution)/shard_map/ppermute | solution.py:38
  25.6 1.4 %collective-permute-done.8.got_other.refs_8_ = bf16[6,128,128]{2,1,0:T(8,128)(2,1)S(1)} collective-permute-done((bf16[6,128,128]{2,1,0:T(8,128)(2,1)S(1)}, bf16[6,128,128]{2,1,0:T(8,128)(2,1)S(1)}, u32[]{:S(2)}, u32[]{:S(2)}) %collective-permute-start.8) | collective-permute-done | bytes 196640 | tf_op jit(solution)/shard_map/ppermute | solution.py:38
  27.4 1.9 %collective-permute-start.14 = (bf16[6,128,128]{2,1,0:T(8,128)(2,1)S(1)}, bf16[6,128,128]{2,1,0:T(8,128)(2,1)S(1)}, u32[]{:S(2)}, u32[]{:S(2)}) collective-permute-start(bf16[6,128,128]{2,1,0:T(8,128)(2,1)S(1)} %shard_map.50.even), channel_id=1, source_target_pairs={{0,8},{4,12},{8,0},{12,4},{16,24},{20,28},{24,16},{28,20},{1,9},{5... | collective-permute-start | bytes 589832 | tf_op jit(solution)/shard_map/ppermute | solution.py:38
  29.3 1.2 %collective-permute-start.4 = (bf16[6,32,128]{2,1,0:T(8,128)(2,1)S(1)}, bf16[6,32,128]{2,1,0:T(8,128)(2,1)S(1)}, u32[]{:S(2)}, u32[]{:S(2)}) collective-permute-start(bf16[6,32,128]{2,1,0:T(8,128)(2,1)S(1)} %get-tuple-element.22), channel_id=1, source_target_pairs={{0,2},{1,3},{2,0},{3,1},{4,6},{5,7},{6,4},{7,5},{8,10},{9,11},{10,... | collective-permute-start | bytes 147464 | tf_op jit(solution)/shard_map/ppermute | solution.py:38
  31.2 2.3 %collective-permute-done.4.refs_2_ = bf16[6,32,128]{2,1,0:T(8,128)(2,1)S(1)} collective-permute-done((bf16[6,32,128]{2,1,0:T(8,128)(2,1)S(1)}, bf16[6,32,128]{2,1,0:T(8,128)(2,1)S(1)}, u32[]{:S(2)}, u32[]{:S(2)}) %collective-permute-start.4) | collective-permute-done | bytes 49184 | tf_op jit(solution)/shard_map/ppermute | solution.py:38
  34.2 3.6 %shard_map.48 = (bf16[6,64,128]{2,1,0:T(8,128)(2,1)S(1)}, f32[4,4,32,256]{3,2,1,0:T(8,128)S(1)}) custom-call(s32[1]{0:T(128)} %bitcast.place, bf16[4,4,256,256]{3,2,1,0:T(8,128)(2,1)S(1)} %get-tuple-element.19.weights.refs_0_, bf16[6,32,128]{2,1,0:T(8,128)(2,1)S(1)} %get-tuple-element.20.refs_0_, bf16[6,32,128]{2,1,0:T(8,128)(2,1)S(1)} %collective-permute-done.3.refs_1_, ...), custom_call_target="tpu_custom_call" | custom-call | tf_op jit(solution)/shard_map/pallas_call | solution.py:422
  37.7 1.5 %collective-permute-start.9 = (bf16[6,64,128]{2,1,0:T(8,128)(2,1)S(1)}, bf16[6,64,128]{2,1,0:T(8,128)(2,1)S(1)}, u32[]{:S(2)}, u32[]{:S(2)}) collective-permute-start(bf16[6,64,128]{2,1,0:T(8,128)(2,1)S(1)} %get-tuple-element.26.own_offset), channel_id=1, source_target_pairs={{0,4},{4,0},{8,12},{12,8},{16,20},{20,16},{24,28},{28,24},{1,5},{5... | collective-permute-start | bytes 294920 | tf_op jit(solution)/shard_map/ppermute | solution.py:38
  39.5 3.4 %collective-permute-done.9.got_offset.refs_9_ = bf16[6,64,128]{2,1,0:T(8,128)(2,1)S(1)} collective-permute-done((bf16[6,64,128]{2,1,0:T(8,128)(2,1)S(1)}, bf16[6,64,128]{2,1,0:T(8,128)(2,1)S(1)}, u32[]{:S(2)}, u32[]{:S(2)}) %collective-permute-start.9) | collective-permute-done | bytes 98336 | tf_op jit(solution)/shard_map/ppermute | solution.py:38
  44.0 4.0 %collective-permute-done.10.entry.refs_2_ = bf16[6,64,128]{2,1,0:T(8,128)(2,1)S(1)} collective-permute-done((bf16[6,64,128]{2,1,0:T(8,128)(2,1)S(1)}, bf16[6,64,128]{2,1,0:T(8,128)(2,1)S(1)}, u32[]{:S(2)}, u32[]{:S(2)}) %collective-permute-start.10) | collective-permute-done | bytes 98336 | tf_op jit(solution)/shard_map/ppermute | solution.py:38
  48.3 1.6 %collective-permute-start.12 = (bf16[6,64,128]{2,1,0:T(8,128)(2,1)S(1)}, bf16[6,64,128]{2,1,0:T(8,128)(2,1)S(1)}, u32[]{:S(2)}, u32[]{:S(2)}) collective-permute-start(bf16[6,64,128]{2,1,0:T(8,128)(2,1)S(1)} %shard_map.51), channel_id=1, source_target_pairs={{0,4},{4,0},{8,16},{12,20},{16,8},{20,12},{24,28},{28,24},{1,5},{5... | collective-permute-start | bytes 294920 | tf_op jit(solution)/shard_map/ppermute | solution.py:518
  49.9 0.8 %collective-permute-start.13 = (bf16[6,64,128]{2,1,0:T(8,128)(2,1)S(1)}, bf16[6,64,128]{2,1,0:T(8,128)(2,1)S(1)}, u32[]{:S(2)}, u32[]{:S(2)}) collective-permute-start(bf16[6,64,128]{2,1,0:T(8,128)(2,1)S(1)} %shard_map.51), channel_id=1, source_target_pairs={{0,16},{4,20},{8,24},{12,28},{16,0},{20,4},{24,8},{28,12},{1,17},{... | collective-permute-start | bytes 294920 | tf_op jit(solution)/shard_map/ppermute | solution.py:38
  50.8 2.2 %collective-permute-done.12.refs_3_ = bf16[6,64,128]{2,1,0:T(8,128)(2,1)S(1)} collective-permute-done((bf16[6,64,128]{2,1,0:T(8,128)(2,1)S(1)}, bf16[6,64,128]{2,1,0:T(8,128)(2,1)S(1)}, u32[]{:S(2)}, u32[]{:S(2)}) %collective-permute-start.12) | collective-permute-done | bytes 98336 | tf_op jit(solution)/shard_map/ppermute | solution.py:518
  53.0 3.9 %collective-permute-done.13.refs_4_ = bf16[6,64,128]{2,1,0:T(8,128)(2,1)S(1)} collective-permute-done((bf16[6,64,128]{2,1,0:T(8,128)(2,1)S(1)}, bf16[6,64,128]{2,1,0:T(8,128)(2,1)S(1)}, u32[]{:S(2)}, u32[]{:S(2)}) %collective-permute-start.13) | collective-permute-done | bytes 98336 | tf_op jit(solution)/shard_map/ppermute | solution.py:38
  56.9 4.0 %shard_map.52 = (bf16[6,32,128]{2,1,0:T(8,128)(2,1)S(1)}, bf16[6,32,128]{2,1,0:T(8,128)(2,1)S(1)}, bf16[6,32,128]{2,1,0:T(8,128)(2,1)S(1)}, bf16[6,32,128]{2,1,0:T(8,128)(2,1)S(1)}) custom-call(s32[1]{0:T(128)} %bitcast.place, s32[1]{0:T(128)} %bitcast.5.line, bf16[4,4,256,256]{3,2,1,0:T(8,128)(2,1)S(1)} %get-tuple-element.19.weights.refs_0_, ...), custom_call_target="tpu_custom_call" | custom-call | tf_op jit(solution)/shard_map/pallas_call | solution.py:422
  61.0 1.1 %collective-permute-start.17 = (bf16[6,32,128]{2,1,0:T(8,128)(2,1)S(1)}, bf16[6,32,128]{2,1,0:T(8,128)(2,1)S(1)}, u32[]{:S(2)}, u32[]{:S(2)}) collective-permute-start(bf16[6,32,128]{2,1,0:T(8,128)(2,1)S(1)} %get-tuple-element.29), channel_id=1, source_target_pairs={{0,2},{1,3},{2,0},{3,1},{4,6},{5,7},{6,4},{7,5},{8,10},{9,11},{10,... | collective-permute-start | bytes 147464 | tf_op jit(solution)/shard_map/ppermute | solution.py:38
  62.1 0.7 %collective-permute-start.18 = (bf16[6,32,128]{2,1,0:T(8,128)(2,1)S(1)}, bf16[6,32,128]{2,1,0:T(8,128)(2,1)S(1)}, u32[]{:S(2)}, u32[]{:S(2)}) collective-permute-start(bf16[6,32,128]{2,1,0:T(8,128)(2,1)S(1)} %get-tuple-element.30), channel_id=1, source_target_pairs={{0,3},{1,2},{2,1},{3,0},{4,7},{5,6},{6,5},{7,4},{8,11},{9,10},{10,... | collective-permute-start | bytes 147464 | tf_op jit(solution)/shard_map/ppermute | solution.py:38
  62.9 2.4 %collective-permute-done.17.refs_2_ = bf16[6,32,128]{2,1,0:T(8,128)(2,1)S(1)} collective-permute-done((bf16[6,32,128]{2,1,0:T(8,128)(2,1)S(1)}, bf16[6,32,128]{2,1,0:T(8,128)(2,1)S(1)}, u32[]{:S(2)}, u32[]{:S(2)}) %collective-permute-start.17) | collective-permute-done | bytes 49184 | tf_op jit(solution)/shard_map/ppermute | solution.py:38
  66.0 2.6 %shard_map.53 = bf16[4,512,128]{2,1,0:T(8,128)(2,1)} custom-call(s32[1]{0:T(128)} %bitcast.place, s32[4]{0:T(128)S(1)} %bitcast.14, bf16[4,512,512]{2,1,0:T(8,128)(2,1)S(1)} %bitcast.8, bf16[4,192,512]{2,1,0:T(8,128)(2,1)S(1)} %bitcast.10, bf16[4,512,128]{2,1,0:T(8,128)(2,1)S(1)} %bitcast.12, bf16[6,32,128]{2,1,0:T(8,128)(2,1)S(1)} %get-tuple-element.27.refs_0_, ...), custom_call_target="tpu_custom_call" | custom-call | tf_op jit(solution)/shard_map/pallas_call | solution.py:422
  (30 shorter events, 4.0 us)
Async XLA Ops:
  3.1 10.1 %collective-permute-start = (bf16[1152,128]{1,0:T(8,128)(2,1)S(1)}, bf16[1152,128]{1,0:T(8,128)(2,1)S(1)}, u32[]{:S(2)}, u32[]{:S(2)}) collective-permute-start(bf16[1152,128]{1,0:T(8,128)(2,1)S(1)} %get-tuple-element.18.refs_0_), channel_id=1, source_target_pairs={{0,2},{1,3},{2,0},{3,1},{4,6},{5,7},{6,4},{7,5},{8,10},{9,11},{10,... | collective-permute-start | bytes 884744 | tf_op jit(solution)/shard_map/ppermute | solution.py:38
  5.9 7.4 %collective-permute-start.1 = (bf16[1152,128]{1,0:T(8,128)(2,1)S(1)}, bf16[1152,128]{1,0:T(8,128)(2,1)S(1)}, u32[]{:S(2)}, u32[]{:S(2)}) collective-permute-start(bf16[1152,128]{1,0:T(8,128)(2,1)S(1)} %get-tuple-element.18.refs_0_), channel_id=1, source_target_pairs={{0,1},{1,0},{2,3},{3,2},{4,5},{5,4},{6,7},{7,6},{8,9},{9,8},{10,11... | collective-permute-start | bytes 884744 | tf_op jit(solution)/shard_map/ppermute | solution.py:38
  13.3 1.6 %collective-permute-start.2 = (bf16[1152,128]{1,0:T(8,128)(2,1)S(1)}, bf16[1152,128]{1,0:T(8,128)(2,1)S(1)}, u32[]{:S(2)}, u32[]{:S(2)}) collective-permute-start(bf16[1152,128]{1,0:T(8,128)(2,1)S(1)} %collective-permute-done.refs_1_), channel_id=1, source_target_pairs={{0,1},{1,0},{2,3},{3,2},{4,5},{5,4},{6,7},{7,6},{8,9},{9,8},{10,11... | collective-permute-start | bytes 884744 | tf_op jit(solution)/shard_map/ppermute | solution.py:38
  18.3 7.3 %collective-permute-start.7 = (bf16[6,128,128]{2,1,0:T(8,128)(2,1)S(1)}, bf16[6,128,128]{2,1,0:T(8,128)(2,1)S(1)}, u32[]{:S(2)}, u32[]{:S(2)}) collective-permute-start(bf16[6,128,128]{2,1,0:T(8,128)(2,1)S(1)} %get-tuple-element.25.own), channel_id=1, source_target_pairs={{0,4},{4,0},{8,12},{12,8},{16,20},{20,16},{24,28},{28,24},{1,5},{5... | collective-permute-start | bytes 589832 | tf_op jit(solution)/shard_map/ppermute | solution.py:38
  20.4 5.2 %collective-permute-start.6 = (bf16[6,128,128]{2,1,0:T(8,128)(2,1)S(1)}, bf16[6,128,128]{2,1,0:T(8,128)(2,1)S(1)}, u32[]{:S(2)}, u32[]{:S(2)}) collective-permute-start(bf16[6,128,128]{2,1,0:T(8,128)(2,1)S(1)} %get-tuple-element.25.own), channel_id=1, source_target_pairs={{0,1},{1,0},{2,3},{3,2},{4,5},{5,4},{6,7},{7,6},{8,9},{9,8},{10,11... | collective-permute-start | bytes 589832 | tf_op jit(solution)/shard_map/ppermute | solution.py:38
  25.6 1.4 %collective-permute-start.8 = (bf16[6,128,128]{2,1,0:T(8,128)(2,1)S(1)}, bf16[6,128,128]{2,1,0:T(8,128)(2,1)S(1)}, u32[]{:S(2)}, u32[]{:S(2)}) collective-permute-start(bf16[6,128,128]{2,1,0:T(8,128)(2,1)S(1)} %collective-permute-done.7.got.refs_7_), channel_id=1, source_target_pairs={{0,1},{1,0},{2,3},{3,2},{4,5},{5,4},{6,7},{7,6},{8,9},{9,8},{10,11... | collective-permute-start | bytes 589832 | tf_op jit(solution)/shard_map/ppermute | solution.py:38
  27.4 16.5 %collective-permute-start.14 = (bf16[6,128,128]{2,1,0:T(8,128)(2,1)S(1)}, bf16[6,128,128]{2,1,0:T(8,128)(2,1)S(1)}, u32[]{:S(2)}, u32[]{:S(2)}) collective-permute-start(bf16[6,128,128]{2,1,0:T(8,128)(2,1)S(1)} %shard_map.50.even), channel_id=1, source_target_pairs={{0,8},{4,12},{8,0},{12,4},{16,24},{20,28},{24,16},{28,20},{1,9},{5... | collective-permute-start | bytes 589832 | tf_op jit(solution)/shard_map/ppermute | solution.py:38
  29.3 1.9 %collective-permute-start.3 = (bf16[6,32,128]{2,1,0:T(8,128)(2,1)S(1)}, bf16[6,32,128]{2,1,0:T(8,128)(2,1)S(1)}, u32[]{:S(2)}, u32[]{:S(2)}) collective-permute-start(bf16[6,32,128]{2,1,0:T(8,128)(2,1)S(1)} %get-tuple-element.21), channel_id=1, source_target_pairs={{0,1},{1,0},{2,3},{3,2},{4,5},{5,4},{6,7},{7,6},{8,9},{9,8},{10,11... | collective-permute-start | bytes 147464 | tf_op jit(solution)/shard_map/ppermute | solution.py:38
  29.3 4.2 %collective-permute-start.4 = (bf16[6,32,128]{2,1,0:T(8,128)(2,1)S(1)}, bf16[6,32,128]{2,1,0:T(8,128)(2,1)S(1)}, u32[]{:S(2)}, u32[]{:S(2)}) collective-permute-start(bf16[6,32,128]{2,1,0:T(8,128)(2,1)S(1)} %get-tuple-element.22), channel_id=1, source_target_pairs={{0,2},{1,3},{2,0},{3,1},{4,6},{5,7},{6,4},{7,5},{8,10},{9,11},{10,... | collective-permute-start | bytes 147464 | tf_op jit(solution)/shard_map/ppermute | solution.py:38
  30.5 3.6 %collective-permute-start.5 = (bf16[6,32,128]{2,1,0:T(8,128)(2,1)S(1)}, bf16[6,32,128]{2,1,0:T(8,128)(2,1)S(1)}, u32[]{:S(2)}, u32[]{:S(2)}) collective-permute-start(bf16[6,32,128]{2,1,0:T(8,128)(2,1)S(1)} %get-tuple-element.23), channel_id=1, source_target_pairs={{0,3},{1,2},{2,1},{3,0},{4,7},{5,6},{6,5},{7,4},{8,11},{9,10},{10,... | collective-permute-start | bytes 147464 | tf_op jit(solution)/shard_map/ppermute | solution.py:38
  37.7 5.2 %collective-permute-start.9 = (bf16[6,64,128]{2,1,0:T(8,128)(2,1)S(1)}, bf16[6,64,128]{2,1,0:T(8,128)(2,1)S(1)}, u32[]{:S(2)}, u32[]{:S(2)}) collective-permute-start(bf16[6,64,128]{2,1,0:T(8,128)(2,1)S(1)} %get-tuple-element.26.own_offset), channel_id=1, source_target_pairs={{0,4},{4,0},{8,12},{12,8},{16,20},{20,16},{24,28},{28,24},{1,5},{5... | collective-permute-start | bytes 294920 | tf_op jit(solution)/shard_map/ppermute | solution.py:38
  39.3 8.7 %collective-permute-start.11 = (bf16[6,128,128]{2,1,0:T(8,128)(2,1)S(1)}, bf16[6,128,128]{2,1,0:T(8,128)(2,1)S(1)}, u32[]{:S(2)}, u32[]{:S(2)}) collective-permute-start(bf16[6,128,128]{2,1,0:T(8,128)(2,1)S(1)} %shard_map.50.even), channel_id=1, source_target_pairs={{0,1},{1,0},{2,3},{3,2},{4,5},{5,4},{6,7},{7,6},{8,9},{9,8},{10,11... | collective-permute-start | bytes 589832 | tf_op jit(solution)/shard_map/ppermute | solution.py:38
  43.3 22.7 %copy-start = (bf16[1,1,4,512,512]{4,3,2,1,0:T(8,128)(2,1)S(1)}, bf16[1,1,4,512,512]{4,3,2,1,0:T(8,128)(2,1)}, u32[]{:S(2)}) copy-start(bf16[1,1,4,512,512]{4,3,2,1,0:T(8,128)(2,1)} %param.5) | copy-start | bytes 6291460
  43.3 22.7 %copy-start.1 = (bf16[1,1,4,3,64,512]{5,4,3,2,1,0:T(8,128)(2,1)S(1)}, bf16[1,1,4,3,64,512]{5,4,3,2,1,0:T(8,128)(2,1)}, u32[]{:S(2)}) copy-start(bf16[1,1,4,3,64,512]{5,4,3,2,1,0:T(8,128)(2,1)} %param.6) | copy-start | bytes 2359300
  43.3 22.7 %copy-start.2 = (bf16[1,1,4,512,128]{4,3,2,1,0:T(8,128)(2,1)S(1)}, bf16[1,1,4,512,128]{4,3,2,1,0:T(8,128)(2,1)}, u32[]{:S(2)}) copy-start(bf16[1,1,4,512,128]{4,3,2,1,0:T(8,128)(2,1)} %param.4) | copy-start | bytes 1572868
  43.3 22.7 %copy-start.3 = (s32[1,1,4]{2,1,0:T(1,128)S(1)}, s32[1,1,4]{2,1,0:T(1,128)}, u32[]{:S(2)}) copy-start(s32[1,1,4]{2,1,0:T(1,128)} %param.7) | copy-start | bytes 52
  43.3 4.7 %collective-permute-start.10 = (bf16[6,64,128]{2,1,0:T(8,128)(2,1)S(1)}, bf16[6,64,128]{2,1,0:T(8,128)(2,1)S(1)}, u32[]{:S(2)}, u32[]{:S(2)}) collective-permute-start(bf16[6,64,128]{2,1,0:T(8,128)(2,1)S(1)} %shard_map.49.own), channel_id=1, source_target_pairs={{0,8},{4,12},{8,0},{12,4},{16,24},{20,28},{24,16},{28,20},{1,9},{5... | collective-permute-start | bytes 294920 | tf_op jit(solution)/shard_map/ppermute | solution.py:38
  44.0 13.0 %collective-permute-start.15 = (bf16[6,128,128]{2,1,0:T(8,128)(2,1)S(1)}, bf16[6,128,128]{2,1,0:T(8,128)(2,1)S(1)}, u32[]{:S(2)}, u32[]{:S(2)}) collective-permute-start(bf16[6,128,128]{2,1,0:T(8,128)(2,1)S(1)} %collective-permute-done.14.refs_5_), channel_id=1, source_target_pairs={{0,1},{1,0},{2,3},{3,2},{4,5},{5,4},{6,7},{7,6},{8,9},{9,8},{10,11... | collective-permute-start | bytes 589832 | tf_op jit(solution)/shard_map/ppermute | solution.py:38
  48.3 4.7 %collective-permute-start.12 = (bf16[6,64,128]{2,1,0:T(8,128)(2,1)S(1)}, bf16[6,64,128]{2,1,0:T(8,128)(2,1)S(1)}, u32[]{:S(2)}, u32[]{:S(2)}) collective-permute-start(bf16[6,64,128]{2,1,0:T(8,128)(2,1)S(1)} %shard_map.51), channel_id=1, source_target_pairs={{0,4},{4,0},{8,16},{12,20},{16,8},{20,12},{24,28},{28,24},{1,5},{5... | collective-permute-start | bytes 294920 | tf_op jit(solution)/shard_map/ppermute | solution.py:518
  49.9 7.0 %collective-permute-start.13 = (bf16[6,64,128]{2,1,0:T(8,128)(2,1)S(1)}, bf16[6,64,128]{2,1,0:T(8,128)(2,1)S(1)}, u32[]{:S(2)}, u32[]{:S(2)}) collective-permute-start(bf16[6,64,128]{2,1,0:T(8,128)(2,1)S(1)} %shard_map.51), channel_id=1, source_target_pairs={{0,16},{4,20},{8,24},{12,28},{16,0},{20,4},{24,8},{28,12},{1,17},{... | collective-permute-start | bytes 294920 | tf_op jit(solution)/shard_map/ppermute | solution.py:38
  60.9 1.9 %collective-permute-start.16 = (bf16[6,32,128]{2,1,0:T(8,128)(2,1)S(1)}, bf16[6,32,128]{2,1,0:T(8,128)(2,1)S(1)}, u32[]{:S(2)}, u32[]{:S(2)}) collective-permute-start(bf16[6,32,128]{2,1,0:T(8,128)(2,1)S(1)} %get-tuple-element.28), channel_id=1, source_target_pairs={{0,1},{1,0},{2,3},{3,2},{4,5},{5,4},{6,7},{7,6},{8,9},{9,8},{10,11... | collective-permute-start | bytes 147464 | tf_op jit(solution)/shard_map/ppermute | solution.py:38
  61.0 4.2 %collective-permute-start.17 = (bf16[6,32,128]{2,1,0:T(8,128)(2,1)S(1)}, bf16[6,32,128]{2,1,0:T(8,128)(2,1)S(1)}, u32[]{:S(2)}, u32[]{:S(2)}) collective-permute-start(bf16[6,32,128]{2,1,0:T(8,128)(2,1)S(1)} %get-tuple-element.29), channel_id=1, source_target_pairs={{0,2},{1,3},{2,0},{3,1},{4,6},{5,7},{6,4},{7,5},{8,10},{9,11},{10,... | collective-permute-start | bytes 147464 | tf_op jit(solution)/shard_map/ppermute | solution.py:38
  62.1 3.8 %collective-permute-start.18 = (bf16[6,32,128]{2,1,0:T(8,128)(2,1)S(1)}, bf16[6,32,128]{2,1,0:T(8,128)(2,1)S(1)}, u32[]{:S(2)}, u32[]{:S(2)}) collective-permute-start(bf16[6,32,128]{2,1,0:T(8,128)(2,1)S(1)} %get-tuple-element.30), channel_id=1, source_target_pairs={{0,3},{1,2},{2,1},{3,0},{4,7},{5,6},{6,5},{7,4},{8,11},{9,10},{10,... | collective-permute-start | bytes 147464 | tf_op jit(solution)/shard_map/ppermute | solution.py:38

commit v2 on v1

--- a/solution.py
+++ b/solution.py
@@ -63,13 +63,36 @@
     return pltpu.roll(value.astype(F32), value.shape[-1] // 2, 1).astype(value.dtype)
 
 
-def facemap_kernel(place, order_far, inverse_far, coupling_far, given_far, maps, *refs):
-    gains = refs[:-7]
-    order, inverse, coupling, given, gathered, order_done, done = refs[-7:]
-    groups = len(gains)
-    count, nodes, width = given.shape
+def face_rows_of(inverse, slot, face):
+    nodes = inverse.shape[1]
+    part = nodes // NP
+    layer = part // NP
+    lower = []
+    upper = []
+    for a in range(NP):
+        head = inverse[slot, a * part : a * part + 2 * layer, :].astype(F32)
+        tail = inverse[slot, (a + 1) * part - 2 * layer : (a + 1) * part, :].astype(F32)
+        lower.append(head[:layer])
+        upper.append(tail[layer:])
+    faces = jnp.concatenate(lower + upper, axis=0).astype(BF16)
+    outflow = inverse[slot, nodes - face :, :]
+    return jnp.concatenate([faces, outflow, outflow], axis=0)
+
+
+def pair_maps(maps, coupling, slots, rows, face):
+    outs = []
+    for i, slot in enumerate(slots):
+        full = dot_nt(coupling[slot], rows[i])
+        full = jnp.concatenate([full[2 * face :], full[face : 2 * face], full[:face]], axis=0).astype(BF16)
+        maps[i * 3 * face : (i + 1) * 3 * face, :] = full[:, : 2 * face]
+        outs.append(full[:, 2 * face :])
+    maps[2 * 3 * face :, :] = by_half(outs[0], outs[1])
+
+
+def first_kernel(order_far, inverse_far, coupling_far, given_far, maps, inverse, coupling, given, *refs):
+    order, order_done, done = refs
+    count = inverse.shape[0]
     face = coupling.shape[1] // 3
-    part = nodes // NP
     first = pltpu.make_async_copy(order_far, order, order_done)
     first.start()
     pairs = ((inverse_far, inverse), (coupling_far, coupling), (given_far, given))
@@ -78,36 +101,32 @@
         far, near = pairs[kind]
         return pltpu.make_async_copy(far.at[slot], near.at[slot], done.at[kind, slot])
 
-    for slot in range(count):
-        for kind in range(3):
+    for kind in range(3):
+        for slot in range(count):
             fetch(kind, slot).start()
     first.wait()
-    layer = part // NP
+    for kind in range(2):
+        for slot in range(count):
+            fetch(kind, slot).wait()
+    slots = [order[p] for p in range(2)]
+    pair_maps(maps, coupling, slots, [face_rows_of(inverse, slot, face) for slot in slots], face)
+    for slot in range(count):
+        fetch(2, slot).wait()
+
+
+def rest_kernel(place, order, inverse, coupling, given, *refs):
+    count, _, width = given.shape
+    maps = refs[: count // 2 - 1]
+    gains = refs[count // 2 - 1 : -1]
+    gathered = refs[-1]
+    face = coupling.shape[1] // 3
+    groups = len(gains)
     share = width // groups
-    outs = []
-    every = []
-    for p in range(count):
-        slot = order[p]
-        for kind in range(3):
-            fetch(kind, slot).wait()
-        lower = []
-        upper = []
-        for a in range(NP):
-            head = inverse[slot, a * part : a * part + 2 * layer, :].astype(F32)
-            tail = inverse[slot, (a + 1) * part - 2 * layer : (a + 1) * part, :].astype(F32)
-            lower.append(head[:layer])
-            upper.append(tail[layer:])
-        faces = jnp.concatenate(lower + upper, axis=0).astype(BF16)
-        outflow = inverse[slot, nodes - face :, :]
-        rows = jnp.concatenate([faces, outflow, outflow], axis=0)
-        full = dot_nt(coupling[slot], rows)
-        full = jnp.concatenate([full[2 * face :], full[face : 2 * face], full[:face]], axis=0).astype(BF16)
-        maps[p * 3 * face : (p + 1) * 3 * face, :] = full[:, : 2 * face]
-        outs.append(full[:, 2 * face :])
-        if p % 2 == 1:
-            at = (count + p // 2) * 3 * face
-            maps[at : at + 3 * face, :] = by_half(outs[p - 1], outs[p])
-        every.append(dot(rows, given[slot]).T)
+    slots = [order[p] for p in range(count)]
+    rows = [face_rows_of(inverse, slot, face) for slot in slots]
+    for j, target in enumerate(maps):
+        pair_maps(target, coupling, slots[2 * j + 2 : 2 * j + 4], rows[2 * j + 2 : 2 * j + 4], face)
+    every = [dot(rows[p], given[slots[p]]).T for p in range(count)]
     tiles = [gain[:, : 2 * face] for gain in every]
     for p in range(0, count, 2):
         tiles.append(by_half(every[p][:, 2 * face :], every[p + 1][:, 2 * face :]))
@@ -119,17 +138,16 @@
             gains[rel][m] = gathered[m, pl.ds(at, share), :].astype(BF16)
 
 
-def unpack_maps(map_refs, weights, count, face):
-    for pos, ref in enumerate(map_refs):
-        for p in range(count):
-            sides = ref[p * 3 * face : (p + 1) * 3 * face, :]
-            at = (count + p // 2) * 3 * face
-            outs = ref[at : at + 3 * face, :]
+def unpack_maps(map_refs, weights, face):
+    for j, refs in enumerate(map_refs):
+        for pos, ref in enumerate(refs):
+            outs = ref[2 * 3 * face :, :]
             other = turned(outs)
-            outs = by_half(outs, other) if p % 2 == 0 else by_half(other, outs)
-            full = jnp.concatenate([sides, outs], axis=1)
-            weights[pos, p, : 3 * face, :] = full
-            weights[pos, p, 3 * face :, :] = full[2 * face :]
+            for i in range(2):
+                sides = ref[i * 3 * face : (i + 1) * 3 * face, :]
+                full = jnp.concatenate([sides, by_half(outs, other) if i == 0 else by_half(other, outs)], axis=1)
+                weights[pos, 2 * j + i, : 3 * face, :] = full
+                weights[pos, 2 * j + i, 3 * face :, :] = full[2 * face :]
 
 
 def unpack_gains(gain_refs, gains, count):
@@ -138,7 +156,7 @@
             outs = ref[count + p // 2]
             other = turned(outs)
             outs = by_half(outs, other) if p % 2 == 0 else by_half(other, outs)
-            gains[reversed_static(rel, len(gain_refs)), p] = jnp.concatenate([ref[p], outs], axis=1).astype(F32)
+            gains[reversed_static(rel, len(gain_refs)), p] = jnp.concatenate([ref[p], outs], axis=1)
 
 
 def neighbours(me, pos, groups):
@@ -182,7 +200,7 @@
         for i, pos in enumerate(chosen):
             result = dot(jnp.concatenate([lags[pos, p], entries[i]], axis=1), weights[pos, p])
             if gains is not None:
-                result = result + gains[pos, p]
+                result = result + gains[pos, p].astype(F32)
             states[pos, p] = result[:, : 2 * face].astype(BF16)
             outs[i].append(result[:, 2 * face :])
         if p < count - 1:
@@ -191,11 +209,12 @@
 
 
 def respond_kernel(place, *refs, groups, count, face):
-    map_refs = refs[:groups]
-    response, weights, states, lags, unit = refs[groups:]
+    pairs = count // 2
+    map_refs = [refs[j * groups : (j + 1) * groups] for j in range(pairs)]
+    response, weights, states, lags, unit = refs[pairs * groups :]
     me = place[0]
     half = groups // 2
-    unpack_maps(map_refs, weights, count, face)
+    unpack_maps(map_refs, weights, face)
     states[...] = jnp.zeros_like(states)
     unit[...] = jnp.zeros_like(unit)
     row = lax.broadcasted_iota(jnp.int32, unit.shape[2:], 0)
@@ -425,7 +444,7 @@
         in_specs=[SMEM] * len(scalars) + [VMEM] * (len(arrays) - far) + [HBM] * far,
         out_specs=[VMEM] * len(outs),
         scratch_shapes=[*others[:1], *[pltpu.VMEM(shape, kind) for shape, kind in scratch], *others[1:]],
-        compiler_params=pltpu.CompilerParams(vmem_limit_bytes=grant or min(held + (6 << 20), 60 << 20)),
+        compiler_params=pltpu.CompilerParams(vmem_limit_bytes=grant or min(held + (3 << 20), 60 << 20)),
     )(*scalars, *arrays)
 
 
@@ -444,17 +463,18 @@
     masks = bits_of(lax.axis_size("stream"))
     tiles = count + count // 2
     shape = jax.ShapeDtypeStruct
-    maps, *gains = call(
-        facemap_kernel,
-        [shape((tiles * 3 * face, 2 * face), BF16)] + [shape((tiles, share, 2 * face), BF16)] * groups,
+    far = [pltpu.with_memory_space_constraint(a, pltpu.HBM) for a in (order, inverse, coupling, given)]
+    maps, *near = call(
+        first_kernel,
         [
-            (inverse.shape, BF16),
-            (coupling.shape, BF16),
-            (given.shape, BF16),
-            ((tiles, width, 2 * face), F32),
+            shape((3 * 3 * face, 2 * face), BF16),
+            shape(inverse.shape, BF16),
+            shape(coupling.shape, BF16),
+            shape(given.shape, BF16),
         ],
-        [place],
-        [pltpu.with_memory_space_constraint(a, pltpu.HBM) for a in (order, inverse, coupling, given)],
+        [],
+        [],
+        far,
         4,
         (
             pltpu.SMEM(order.shape, order.dtype),
@@ -463,6 +483,16 @@
         ),
     )
     all_maps = gather_list(maps, "span")
+    outs = call(
+        rest_kernel,
+        [shape(maps.shape, BF16)] * (count // 2 - 1) + [shape((tiles, share, 2 * face), BF16)] * groups,
+        [((tiles, width, 2 * face), F32)],
+        [place, far[0]],
+        near,
+    )
+    gains = outs[count // 2 - 1 :]
+    for maps in outs[: count // 2 - 1]:
+        all_maps += gather_list(maps, "span")
     gains = exchange(gains, "span")
     sizes = dict(groups=groups, count=count, face=face)
     wide = half * face
@@ -484,7 +514,7 @@
         functools.partial(offset_kernel, **sizes),
         [
             shape((SWEEPS, 2 * share, wide), BF16),
-            shape((groups, count, share, 4 * face), F32),
+            shape((groups, count, share, 4 * face), BF16),
         ],
         [
             ((groups + 1, count, share, 2 * face), BF16),

time: 68.7 us -> 69 us (level)
  waiting for transfers between devices: 35.3 us -> 34.1 us
  starting transfers between devices: 15.3 us -> 16.4 us
    ppermute x18 -> x21, starting transfers between devices: 13.7 us -> 14.7 us  [swap(): return lax.ppermute(value, axis, [(i, i ^ mask) for i in range(count)])]
    ppermute x18 -> x21, waiting for transfers between devices: 33 us -> 32.2 us  [swap(): return lax.ppermute(value, axis, [(i, i ^ mask) for i in range(count)])]
    pallas_call x8 -> x9, Pallas kernels: 17.8 us -> 18.2 us  [call(): pl.pallas_call(kernel, out_shape=outs, in_specs=[SMEM] * len(scalars) + [...]
  transfers between devices with their start and end apart: 19 -> 22, of which waited for: 12 -> 13; matrix products, arithmetic and copies ran while one was open for 0% -> 0% of each run, Pallas kernels for 6% -> 6%
where the time goes in v2:
time: 69 us; the launch traced here: 68.8 us
  waiting for transfers between devices  34.1 us (49%)
  Pallas kernels  18.2 us (26%)
  starting transfers between devices  16.4 us (24%)
    ppermute x21, waiting for transfers between devices, swap(): return lax.ppermute(value, axis, [(i, i ^ mask) for i in range(count)])  32.2 us
    pallas_call x9, Pallas kernels, call(): pl.pallas_call(kernel, out_shape=outs, in_specs=[SMEM] * len(scalars) + [...  18.2 us
    ppermute x21, starting transfers between devices, swap(): return lax.ppermute(value, axis, [(i, i ^ mask) for i in range(count)])  14.7 us
    ppermute x1, waiting for transfers between devices, shards(): second = lax.ppermute(joined, 'stream', crossing(masks))  1.83 us
    ppermute x1, starting transfers between devices, shards(): second = lax.ppermute(joined, 'stream', crossing(masks))  1.7 us
  transfers between devices with their start and end apart: 22, of which 13 were waited for; matrix products, arithmetic and copies ran while one was open for 0% of the time, Pallas kernels for 6%

profile of v2, /device:TPU:0, one launch (start us, length us, event | category | flops | bytes accessed | tf_op | source)
XLA Modules:
  0.0 68.8 jit_solution(4372105553548081267)
XLA Ops:
  0.0 2.2 %shard_map.46 = (bf16[576,128]{1,0:T(8,128)(2,1)S(1)}, bf16[4,512,512]{2,1,0:T(8,128)(2,1)S(1)}, bf16[4,192,512]{2,1,0:T(8,128)(2,1)S(1)}, bf16[4,512,128]{2,1,0:T(8,128)(2,1)S(1)}) custom-call(s32[4]{0:T(128)} %bitcast.13, bf16[4,512,512]{2,1,0:T(8,128)(2,1)} %bitcast.7, bf16[4,192,512]{2,1,0:T(8,128)(2,1)} %bitcast.9, bf16[4,512,128]{2,1,0:T(8,128)(2,1)} %bitcast.11), custom_call_target="tpu_custom_call" | custom-call | tf_op jit(solution)/shard_map/pallas_call | solution.py:441
  2.2 1.4 %shard_map.47 = (bf16[576,128]{1,0:T(8,128)(2,1)S(1)}, bf16[6,32,128]{2,1,0:T(8,128)(2,1)S(1)}, bf16[6,32,128]{2,1,0:T(8,128)(2,1)S(1)}, bf16[6,32,128]{2,1,0:T(8,128)(2,1)S(1)}, bf16[6,32,128]{2,1,0:T(8,128)(2,1)S(1)}) custom-call(s32[1]{0:T(128)} %bitcast.place, s32[4]{0:T(128)} %bitcast.14, bf16[4,512,512]{2,1,0:T(8,128)(2,1)S(1)} %get-tuple-element.23.inverse, ...), custom_call_target="tpu_custom_call" | custom-call | tf_op jit(solution)/shard_map/pallas_call | solution.py:441
  3.6 3.0 %collective-permute-start.3 = (bf16[576,128]{1,0:T(8,128)(2,1)S(1)}, bf16[576,128]{1,0:T(8,128)(2,1)S(1)}, u32[]{:S(2)}, u32[]{:S(2)}) collective-permute-start(bf16[576,128]{1,0:T(8,128)(2,1)S(1)} %get-tuple-element.26.refs_4_), channel_id=1, source_target_pairs={{0,2},{1,3},{2,0},{3,1},{4,6},{5,7},{6,4},{7,5},{8,10},{9,11},{10,... | collective-permute-start | bytes 442376 | tf_op jit(solution)/shard_map/ppermute | solution.py:38
  7.2 4.1 %collective-permute-done.3.refs_5_ = bf16[576,128]{1,0:T(8,128)(2,1)S(1)} collective-permute-done((bf16[576,128]{1,0:T(8,128)(2,1)S(1)}, bf16[576,128]{1,0:T(8,128)(2,1)S(1)}, u32[]{:S(2)}, u32[]{:S(2)}) %collective-permute-start.3) | collective-permute-done | bytes 147488 | tf_op jit(solution)/shard_map/ppermute | solution.py:38
  11.3 2.3 %collective-permute-done.refs_1_ = bf16[576,128]{1,0:T(8,128)(2,1)S(1)} collective-permute-done((bf16[576,128]{1,0:T(8,128)(2,1)S(1)}, bf16[576,128]{1,0:T(8,128)(2,1)S(1)}, u32[]{:S(2)}, u32[]{:S(2)}) %collective-permute-start) | collective-permute-done | bytes 147488 | tf_op jit(solution)/shard_map/ppermute | solution.py:38
  13.6 1.3 %collective-permute-done.2.refs_3_ = bf16[576,128]{1,0:T(8,128)(2,1)S(1)} collective-permute-done((bf16[576,128]{1,0:T(8,128)(2,1)S(1)}, bf16[576,128]{1,0:T(8,128)(2,1)S(1)}, u32[]{:S(2)}, u32[]{:S(2)}) %collective-permute-start.2) | collective-permute-done | bytes 147488 | tf_op jit(solution)/shard_map/ppermute | solution.py:38
  15.0 3.5 %shard_map.48 = (bf16[6,128,128]{2,1,0:T(8,128)(2,1)S(1)}, bf16[4,4,256,256]{3,2,1,0:T(8,128)(2,1)S(1)}) custom-call(s32[1]{0:T(128)} %bitcast.place, bf16[576,128]{1,0:T(8,128)(2,1)S(1)} %get-tuple-element.22.refs_0_, bf16[576,128]{1,0:T(8,128)(2,1)S(1)} %collective-permute-done.refs_1_, bf16[576,128]{1,0:T(8,128)(2,1)S(1)} %collective-permute-done.1.refs_2_, ...), custom_call_target="tpu_custom_call" | custom-call | tf_op jit(solution)/shard_map/pallas_call | solution.py:441
  18.5 1.8 %collective-permute-start.10 = (bf16[6,128,128]{2,1,0:T(8,128)(2,1)S(1)}, bf16[6,128,128]{2,1,0:T(8,128)(2,1)S(1)}, u32[]{:S(2)}, u32[]{:S(2)}) collective-permute-start(bf16[6,128,128]{2,1,0:T(8,128)(2,1)S(1)} %get-tuple-element.33.own), channel_id=1, source_target_pairs={{0,4},{4,0},{8,12},{12,8},{16,20},{20,16},{24,28},{28,24},{1,5},{5... | collective-permute-start | bytes 589832 | tf_op jit(solution)/shard_map/ppermute | solution.py:38
  20.3 5.2 %collective-permute-done.10.got.refs_7_ = bf16[6,128,128]{2,1,0:T(8,128)(2,1)S(1)} collective-permute-done((bf16[6,128,128]{2,1,0:T(8,128)(2,1)S(1)}, bf16[6,128,128]{2,1,0:T(8,128)(2,1)S(1)}, u32[]{:S(2)}, u32[]{:S(2)}) %collective-permute-start.10) | collective-permute-done | bytes 196640 | tf_op jit(solution)/shard_map/ppermute | solution.py:38
  25.5 1.4 %collective-permute-done.11.got_other.refs_8_ = bf16[6,128,128]{2,1,0:T(8,128)(2,1)S(1)} collective-permute-done((bf16[6,128,128]{2,1,0:T(8,128)(2,1)S(1)}, bf16[6,128,128]{2,1,0:T(8,128)(2,1)S(1)}, u32[]{:S(2)}, u32[]{:S(2)}) %collective-permute-start.11) | collective-permute-done | bytes 196640 | tf_op jit(solution)/shard_map/ppermute | solution.py:38
  27.3 1.9 %collective-permute-start.17 = (bf16[6,128,128]{2,1,0:T(8,128)(2,1)S(1)}, bf16[6,128,128]{2,1,0:T(8,128)(2,1)S(1)}, u32[]{:S(2)}, u32[]{:S(2)}) collective-permute-start(bf16[6,128,128]{2,1,0:T(8,128)(2,1)S(1)} %shard_map.51.even), channel_id=1, source_target_pairs={{0,8},{4,12},{8,0},{12,4},{16,24},{20,28},{24,16},{28,20},{1,9},{5... | collective-permute-start | bytes 589832 | tf_op jit(solution)/shard_map/ppermute | solution.py:38
  29.2 1.5 %collective-permute-start.7 = (bf16[6,32,128]{2,1,0:T(8,128)(2,1)S(1)}, bf16[6,32,128]{2,1,0:T(8,128)(2,1)S(1)}, u32[]{:S(2)}, u32[]{:S(2)}) collective-permute-start(bf16[6,32,128]{2,1,0:T(8,128)(2,1)S(1)} %get-tuple-element.30), channel_id=1, source_target_pairs={{0,2},{1,3},{2,0},{3,1},{4,6},{5,7},{6,4},{7,5},{8,10},{9,11},{10,... | collective-permute-start | bytes 147464 | tf_op jit(solution)/shard_map/ppermute | solution.py:38
  31.0 2.3 %collective-permute-done.7.refs_2_ = bf16[6,32,128]{2,1,0:T(8,128)(2,1)S(1)} collective-permute-done((bf16[6,32,128]{2,1,0:T(8,128)(2,1)S(1)}, bf16[6,32,128]{2,1,0:T(8,128)(2,1)S(1)}, u32[]{:S(2)}, u32[]{:S(2)}) %collective-permute-start.7) | collective-permute-done | bytes 49184 | tf_op jit(solution)/shard_map/ppermute | solution.py:38
  34.3 3.5 %shard_map.49 = (bf16[6,64,128]{2,1,0:T(8,128)(2,1)S(1)}, bf16[4,4,32,256]{3,2,1,0:T(8,128)(2,1)S(1)}) custom-call(s32[1]{0:T(128)} %bitcast.place, bf16[4,4,256,256]{3,2,1,0:T(8,128)(2,1)S(1)} %get-tuple-element.27.weights.refs_0_, bf16[6,32,128]{2,1,0:T(8,128)(2,1)S(1)} %get-tuple-element.28.refs_0_, ...), custom_call_target="tpu_custom_call" | custom-call | tf_op jit(solution)/shard_map/pallas_call | solution.py:441
  37.8 1.6 %collective-permute-start.12 = (bf16[6,64,128]{2,1,0:T(8,128)(2,1)S(1)}, bf16[6,64,128]{2,1,0:T(8,128)(2,1)S(1)}, u32[]{:S(2)}, u32[]{:S(2)}) collective-permute-start(bf16[6,64,128]{2,1,0:T(8,128)(2,1)S(1)} %get-tuple-element.34.own_offset), channel_id=1, source_target_pairs={{0,4},{4,0},{8,12},{12,8},{16,20},{20,16},{24,28},{28,24},{1,5},{5... | collective-permute-start | bytes 294920 | tf_op jit(solution)/shard_map/ppermute | solution.py:38
  39.5 3.3 %collective-permute-done.12.got_offset.refs_9_ = bf16[6,64,128]{2,1,0:T(8,128)(2,1)S(1)} collective-permute-done((bf16[6,64,128]{2,1,0:T(8,128)(2,1)S(1)}, bf16[6,64,128]{2,1,0:T(8,128)(2,1)S(1)}, u32[]{:S(2)}, u32[]{:S(2)}) %collective-permute-start.12) | collective-permute-done | bytes 98336 | tf_op jit(solution)/shard_map/ppermute | solution.py:38
  44.0 3.9 %collective-permute-done.13.entry.refs_2_ = bf16[6,64,128]{2,1,0:T(8,128)(2,1)S(1)} collective-permute-done((bf16[6,64,128]{2,1,0:T(8,128)(2,1)S(1)}, bf16[6,64,128]{2,1,0:T(8,128)(2,1)S(1)}, u32[]{:S(2)}, u32[]{:S(2)}) %collective-permute-start.13) | collective-permute-done | bytes 98336 | tf_op jit(solution)/shard_map/ppermute | solution.py:38
  48.2 1.7 %collective-permute-start.15 = (bf16[6,64,128]{2,1,0:T(8,128)(2,1)S(1)}, bf16[6,64,128]{2,1,0:T(8,128)(2,1)S(1)}, u32[]{:S(2)}, u32[]{:S(2)}) collective-permute-start(bf16[6,64,128]{2,1,0:T(8,128)(2,1)S(1)} %shard_map.52), channel_id=1, source_target_pairs={{0,4},{4,0},{8,16},{12,20},{16,8},{20,12},{24,28},{28,24},{1,5},{5... | collective-permute-start | bytes 294920 | tf_op jit(solution)/shard_map/ppermute | solution.py:548
  51.1 1.8 %collective-permute-done.15.refs_3_ = bf16[6,64,128]{2,1,0:T(8,128)(2,1)S(1)} collective-permute-done((bf16[6,64,128]{2,1,0:T(8,128)(2,1)S(1)}, bf16[6,64,128]{2,1,0:T(8,128)(2,1)S(1)}, u32[]{:S(2)}, u32[]{:S(2)}) %collective-permute-start.15) | collective-permute-done | bytes 98336 | tf_op jit(solution)/shard_map/ppermute | solution.py:548
  52.9 3.8 %collective-permute-done.16.refs_4_ = bf16[6,64,128]{2,1,0:T(8,128)(2,1)S(1)} collective-permute-done((bf16[6,64,128]{2,1,0:T(8,128)(2,1)S(1)}, bf16[6,64,128]{2,1,0:T(8,128)(2,1)S(1)}, u32[]{:S(2)}, u32[]{:S(2)}) %collective-permute-start.16) | collective-permute-done | bytes 98336 | tf_op jit(solution)/shard_map/ppermute | solution.py:38
  56.7 4.0 %shard_map.53 = (bf16[6,32,128]{2,1,0:T(8,128)(2,1)S(1)}, bf16[6,32,128]{2,1,0:T(8,128)(2,1)S(1)}, bf16[6,32,128]{2,1,0:T(8,128)(2,1)S(1)}, bf16[6,32,128]{2,1,0:T(8,128)(2,1)S(1)}) custom-call(s32[1]{0:T(128)} %bitcast.place, s32[1]{0:T(128)} %bitcast.5.line, bf16[4,4,256,256]{3,2,1,0:T(8,128)(2,1)S(1)} %get-tuple-element.27.weights.refs_0_, ...), custom_call_target="tpu_custom_call" | custom-call | tf_op jit(solution)/shard_map/pallas_call | solution.py:441
  60.8 1.6 %collective-permute-start.20 = (bf16[6,32,128]{2,1,0:T(8,128)(2,1)S(1)}, bf16[6,32,128]{2,1,0:T(8,128)(2,1)S(1)}, u32[]{:S(2)}, u32[]{:S(2)}) collective-permute-start(bf16[6,32,128]{2,1,0:T(8,128)(2,1)S(1)} %get-tuple-element.37), channel_id=1, source_target_pairs={{0,2},{1,3},{2,0},{3,1},{4,6},{5,7},{6,4},{7,5},{8,10},{9,11},{10,... | collective-permute-start | bytes 147464 | tf_op jit(solution)/shard_map/ppermute | solution.py:38
  62.7 2.3 %collective-permute-done.20.refs_2_ = bf16[6,32,128]{2,1,0:T(8,128)(2,1)S(1)} collective-permute-done((bf16[6,32,128]{2,1,0:T(8,128)(2,1)S(1)}, bf16[6,32,128]{2,1,0:T(8,128)(2,1)S(1)}, u32[]{:S(2)}, u32[]{:S(2)}) %collective-permute-start.20) | collective-permute-done | bytes 49184 | tf_op jit(solution)/shard_map/ppermute | solution.py:38
  66.2 2.6 %shard_map.54 = bf16[4,512,128]{2,1,0:T(8,128)(2,1)} custom-call(s32[1]{0:T(128)} %bitcast.place, s32[4]{0:T(128)S(1)} %bitcast.15, bf16[4,512,512]{2,1,0:T(8,128)(2,1)S(1)} %bitcast.8, bf16[4,192,512]{2,1,0:T(8,128)(2,1)S(1)} %bitcast.10, bf16[4,512,128]{2,1,0:T(8,128)(2,1)S(1)} %bitcast.12, bf16[6,32,128]{2,1,0:T(8,128)(2,1)S(1)} %get-tuple-element.35.refs_0_, ...), custom_call_target="tpu_custom_call" | custom-call | tf_op jit(solution)/shard_map/pallas_call | solution.py:441
  (37 shorter events, 6.5 us)
Async XLA Ops:
  3.6 7.7 %collective-permute-start.3 = (bf16[576,128]{1,0:T(8,128)(2,1)S(1)}, bf16[576,128]{1,0:T(8,128)(2,1)S(1)}, u32[]{:S(2)}, u32[]{:S(2)}) collective-permute-start(bf16[576,128]{1,0:T(8,128)(2,1)S(1)} %get-tuple-element.26.refs_4_), channel_id=1, source_target_pairs={{0,2},{1,3},{2,0},{3,1},{4,6},{5,7},{6,4},{7,5},{8,10},{9,11},{10,... | collective-permute-start | bytes 442376 | tf_op jit(solution)/shard_map/ppermute | solution.py:38
  6.6 7.0 %collective-permute-start = (bf16[576,128]{1,0:T(8,128)(2,1)S(1)}, bf16[576,128]{1,0:T(8,128)(2,1)S(1)}, u32[]{:S(2)}, u32[]{:S(2)}) collective-permute-start(bf16[576,128]{1,0:T(8,128)(2,1)S(1)} %get-tuple-element.22.refs_0_), channel_id=1, source_target_pairs={{0,2},{1,3},{2,0},{3,1},{4,6},{5,7},{6,4},{7,5},{8,10},{9,11},{10,... | collective-permute-start | bytes 442376 | tf_op jit(solution)/shard_map/ppermute | solution.py:38
  6.7 6.9 %collective-permute-start.4 = (bf16[576,128]{1,0:T(8,128)(2,1)S(1)}, bf16[576,128]{1,0:T(8,128)(2,1)S(1)}, u32[]{:S(2)}, u32[]{:S(2)}) collective-permute-start(bf16[576,128]{1,0:T(8,128)(2,1)S(1)} %get-tuple-element.26.refs_4_), channel_id=1, source_target_pairs={{0,1},{1,0},{2,3},{3,2},{4,5},{5,4},{6,7},{7,6},{8,9},{9,8},{10,11... | collective-permute-start | bytes 442376 | tf_op jit(solution)/shard_map/ppermute | solution.py:38
  6.7 6.9 %collective-permute-start.1 = (bf16[576,128]{1,0:T(8,128)(2,1)S(1)}, bf16[576,128]{1,0:T(8,128)(2,1)S(1)}, u32[]{:S(2)}, u32[]{:S(2)}) collective-permute-start(bf16[576,128]{1,0:T(8,128)(2,1)S(1)} %get-tuple-element.22.refs_0_), channel_id=1, source_target_pairs={{0,1},{1,0},{2,3},{3,2},{4,5},{5,4},{6,7},{7,6},{8,9},{9,8},{10,11... | collective-permute-start | bytes 442376 | tf_op jit(solution)/shard_map/ppermute | solution.py:38
  11.3 2.3 %collective-permute-start.5 = (bf16[576,128]{1,0:T(8,128)(2,1)S(1)}, bf16[576,128]{1,0:T(8,128)(2,1)S(1)}, u32[]{:S(2)}, u32[]{:S(2)}) collective-permute-start(bf16[576,128]{1,0:T(8,128)(2,1)S(1)} %collective-permute-done.3.refs_5_), channel_id=1, source_target_pairs={{0,1},{1,0},{2,3},{3,2},{4,5},{5,4},{6,7},{7,6},{8,9},{9,8},{10,11... | collective-permute-start | bytes 442376 | tf_op jit(solution)/shard_map/ppermute | solution.py:38
  13.6 1.4 %collective-permute-start.2 = (bf16[576,128]{1,0:T(8,128)(2,1)S(1)}, bf16[576,128]{1,0:T(8,128)(2,1)S(1)}, u32[]{:S(2)}, u32[]{:S(2)}) collective-permute-start(bf16[576,128]{1,0:T(8,128)(2,1)S(1)} %collective-permute-done.refs_1_), channel_id=1, source_target_pairs={{0,1},{1,0},{2,3},{3,2},{4,5},{5,4},{6,7},{7,6},{8,9},{9,8},{10,11... | collective-permute-start | bytes 442376 | tf_op jit(solution)/shard_map/ppermute | solution.py:38
  18.5 7.0 %collective-permute-start.10 = (bf16[6,128,128]{2,1,0:T(8,128)(2,1)S(1)}, bf16[6,128,128]{2,1,0:T(8,128)(2,1)S(1)}, u32[]{:S(2)}, u32[]{:S(2)}) collective-permute-start(bf16[6,128,128]{2,1,0:T(8,128)(2,1)S(1)} %get-tuple-element.33.own), channel_id=1, source_target_pairs={{0,4},{4,0},{8,12},{12,8},{16,20},{20,16},{24,28},{28,24},{1,5},{5... | collective-permute-start | bytes 589832 | tf_op jit(solution)/shard_map/ppermute | solution.py:38
  20.3 5.2 %collective-permute-start.9 = (bf16[6,128,128]{2,1,0:T(8,128)(2,1)S(1)}, bf16[6,128,128]{2,1,0:T(8,128)(2,1)S(1)}, u32[]{:S(2)}, u32[]{:S(2)}) collective-permute-start(bf16[6,128,128]{2,1,0:T(8,128)(2,1)S(1)} %get-tuple-element.33.own), channel_id=1, source_target_pairs={{0,1},{1,0},{2,3},{3,2},{4,5},{5,4},{6,7},{7,6},{8,9},{9,8},{10,11... | collective-permute-start | bytes 589832 | tf_op jit(solution)/shard_map/ppermute | solution.py:38
  25.5 1.4 %collective-permute-start.11 = (bf16[6,128,128]{2,1,0:T(8,128)(2,1)S(1)}, bf16[6,128,128]{2,1,0:T(8,128)(2,1)S(1)}, u32[]{:S(2)}, u32[]{:S(2)}) collective-permute-start(bf16[6,128,128]{2,1,0:T(8,128)(2,1)S(1)} %collective-permute-done.10.got.refs_7_), channel_id=1, source_target_pairs={{0,1},{1,0},{2,3},{3,2},{4,5},{5,4},{6,7},{7,6},{8,9},{9,8},{10,11... | collective-permute-start | bytes 589832 | tf_op jit(solution)/shard_map/ppermute | solution.py:38
  27.3 16.7 %collective-permute-start.17 = (bf16[6,128,128]{2,1,0:T(8,128)(2,1)S(1)}, bf16[6,128,128]{2,1,0:T(8,128)(2,1)S(1)}, u32[]{:S(2)}, u32[]{:S(2)}) collective-permute-start(bf16[6,128,128]{2,1,0:T(8,128)(2,1)S(1)} %shard_map.51.even), channel_id=1, source_target_pairs={{0,8},{4,12},{8,0},{12,4},{16,24},{20,28},{24,16},{28,20},{1,9},{5... | collective-permute-start | bytes 589832 | tf_op jit(solution)/shard_map/ppermute | solution.py:38
  29.1 1.9 %collective-permute-start.6 = (bf16[6,32,128]{2,1,0:T(8,128)(2,1)S(1)}, bf16[6,32,128]{2,1,0:T(8,128)(2,1)S(1)}, u32[]{:S(2)}, u32[]{:S(2)}) collective-permute-start(bf16[6,32,128]{2,1,0:T(8,128)(2,1)S(1)} %get-tuple-element.29), channel_id=1, source_target_pairs={{0,1},{1,0},{2,3},{3,2},{4,5},{5,4},{6,7},{7,6},{8,9},{9,8},{10,11... | collective-permute-start | bytes 147464 | tf_op jit(solution)/shard_map/ppermute | solution.py:38
  29.2 4.2 %collective-permute-start.7 = (bf16[6,32,128]{2,1,0:T(8,128)(2,1)S(1)}, bf16[6,32,128]{2,1,0:T(8,128)(2,1)S(1)}, u32[]{:S(2)}, u32[]{:S(2)}) collective-permute-start(bf16[6,32,128]{2,1,0:T(8,128)(2,1)S(1)} %get-tuple-element.30), channel_id=1, source_target_pairs={{0,2},{1,3},{2,0},{3,1},{4,6},{5,7},{6,4},{7,5},{8,10},{9,11},{10,... | collective-permute-start | bytes 147464 | tf_op jit(solution)/shard_map/ppermute | solution.py:38
  30.6 3.6 %collective-permute-start.8 = (bf16[6,32,128]{2,1,0:T(8,128)(2,1)S(1)}, bf16[6,32,128]{2,1,0:T(8,128)(2,1)S(1)}, u32[]{:S(2)}, u32[]{:S(2)}) collective-permute-start(bf16[6,32,128]{2,1,0:T(8,128)(2,1)S(1)} %get-tuple-element.31), channel_id=1, source_target_pairs={{0,3},{1,2},{2,1},{3,0},{4,7},{5,6},{6,5},{7,4},{8,11},{9,10},{10,... | collective-permute-start | bytes 147464 | tf_op jit(solution)/shard_map/ppermute | solution.py:38
  37.8 5.0 %collective-permute-start.12 = (bf16[6,64,128]{2,1,0:T(8,128)(2,1)S(1)}, bf16[6,64,128]{2,1,0:T(8,128)(2,1)S(1)}, u32[]{:S(2)}, u32[]{:S(2)}) collective-permute-start(bf16[6,64,128]{2,1,0:T(8,128)(2,1)S(1)} %get-tuple-element.34.own_offset), channel_id=1, source_target_pairs={{0,4},{4,0},{8,12},{12,8},{16,20},{20,16},{24,28},{28,24},{1,5},{5... | collective-permute-start | bytes 294920 | tf_op jit(solution)/shard_map/ppermute | solution.py:38
  39.4 8.5 %collective-permute-start.14 = (bf16[6,128,128]{2,1,0:T(8,128)(2,1)S(1)}, bf16[6,128,128]{2,1,0:T(8,128)(2,1)S(1)}, u32[]{:S(2)}, u32[]{:S(2)}) collective-permute-start(bf16[6,128,128]{2,1,0:T(8,128)(2,1)S(1)} %shard_map.51.even), channel_id=1, source_target_pairs={{0,1},{1,0},{2,3},{3,2},{4,5},{5,4},{6,7},{7,6},{8,9},{9,8},{10,11... | collective-permute-start | bytes 589832 | tf_op jit(solution)/shard_map/ppermute | solution.py:38
  43.1 23.0 %copy-start = (bf16[1,1,4,512,512]{4,3,2,1,0:T(8,128)(2,1)S(1)}, bf16[1,1,4,512,512]{4,3,2,1,0:T(8,128)(2,1)}, u32[]{:S(2)}) copy-start(bf16[1,1,4,512,512]{4,3,2,1,0:T(8,128)(2,1)} %param.5) | copy-start | bytes 6291460
  43.2 23.0 %copy-start.1 = (bf16[1,1,4,3,64,512]{5,4,3,2,1,0:T(8,128)(2,1)S(1)}, bf16[1,1,4,3,64,512]{5,4,3,2,1,0:T(8,128)(2,1)}, u32[]{:S(2)}) copy-start(bf16[1,1,4,3,64,512]{5,4,3,2,1,0:T(8,128)(2,1)} %param.6) | copy-start | bytes 2359300
  43.2 4.7 %collective-permute-start.13 = (bf16[6,64,128]{2,1,0:T(8,128)(2,1)S(1)}, bf16[6,64,128]{2,1,0:T(8,128)(2,1)S(1)}, u32[]{:S(2)}, u32[]{:S(2)}) collective-permute-start(bf16[6,64,128]{2,1,0:T(8,128)(2,1)S(1)} %shard_map.50.own), channel_id=1, source_target_pairs={{0,8},{4,12},{8,0},{12,4},{16,24},{20,28},{24,16},{28,20},{1,9},{5... | collective-permute-start | bytes 294920 | tf_op jit(solution)/shard_map/ppermute | solution.py:38
  44.0 12.7 %collective-permute-start.18 = (bf16[6,128,128]{2,1,0:T(8,128)(2,1)S(1)}, bf16[6,128,128]{2,1,0:T(8,128)(2,1)S(1)}, u32[]{:S(2)}, u32[]{:S(2)}) collective-permute-start(bf16[6,128,128]{2,1,0:T(8,128)(2,1)S(1)} %collective-permute-done.17.refs_5_), channel_id=1, source_target_pairs={{0,1},{1,0},{2,3},{3,2},{4,5},{5,4},{6,7},{7,6},{8,9},{9,8},{10,11... | collective-permute-start | bytes 589832 | tf_op jit(solution)/shard_map/ppermute | solution.py:38
  48.2 4.7 %collective-permute-start.15 = (bf16[6,64,128]{2,1,0:T(8,128)(2,1)S(1)}, bf16[6,64,128]{2,1,0:T(8,128)(2,1)S(1)}, u32[]{:S(2)}, u32[]{:S(2)}) collective-permute-start(bf16[6,64,128]{2,1,0:T(8,128)(2,1)S(1)} %shard_map.52), channel_id=1, source_target_pairs={{0,4},{4,0},{8,16},{12,20},{16,8},{20,12},{24,28},{28,24},{1,5},{5... | collective-permute-start | bytes 294920 | tf_op jit(solution)/shard_map/ppermute | solution.py:548
  49.9 6.8 %collective-permute-start.16 = (bf16[6,64,128]{2,1,0:T(8,128)(2,1)S(1)}, bf16[6,64,128]{2,1,0:T(8,128)(2,1)S(1)}, u32[]{:S(2)}, u32[]{:S(2)}) collective-permute-start(bf16[6,64,128]{2,1,0:T(8,128)(2,1)S(1)} %shard_map.52), channel_id=1, source_target_pairs={{0,16},{4,20},{8,24},{12,28},{16,0},{20,4},{24,8},{28,12},{1,17},{... | collective-permute-start | bytes 294920 | tf_op jit(solution)/shard_map/ppermute | solution.py:38
  60.8 1.9 %collective-permute-start.19 = (bf16[6,32,128]{2,1,0:T(8,128)(2,1)S(1)}, bf16[6,32,128]{2,1,0:T(8,128)(2,1)S(1)}, u32[]{:S(2)}, u32[]{:S(2)}) collective-permute-start(bf16[6,32,128]{2,1,0:T(8,128)(2,1)S(1)} %get-tuple-element.36), channel_id=1, source_target_pairs={{0,1},{1,0},{2,3},{3,2},{4,5},{5,4},{6,7},{7,6},{8,9},{9,8},{10,11... | collective-permute-start | bytes 147464 | tf_op jit(solution)/shard_map/ppermute | solution.py:38
  60.8 4.2 %collective-permute-start.20 = (bf16[6,32,128]{2,1,0:T(8,128)(2,1)S(1)}, bf16[6,32,128]{2,1,0:T(8,128)(2,1)S(1)}, u32[]{:S(2)}, u32[]{:S(2)}) collective-permute-start(bf16[6,32,128]{2,1,0:T(8,128)(2,1)S(1)} %get-tuple-element.37), channel_id=1, source_target_pairs={{0,2},{1,3},{2,0},{3,1},{4,6},{5,7},{6,4},{7,5},{8,10},{9,11},{10,... | collective-permute-start | bytes 147464 | tf_op jit(solution)/shard_map/ppermute | solution.py:38
  62.5 3.7 %collective-permute-start.21 = (bf16[6,32,128]{2,1,0:T(8,128)(2,1)S(1)}, bf16[6,32,128]{2,1,0:T(8,128)(2,1)S(1)}, u32[]{:S(2)}, u32[]{:S(2)}) collective-permute-start(bf16[6,32,128]{2,1,0:T(8,128)(2,1)S(1)} %get-tuple-element.38), channel_id=1, source_target_pairs={{0,3},{1,2},{2,1},{3,0},{4,7},{5,6},{6,5},{7,4},{8,11},{9,10},{10,... | collective-permute-start | bytes 147464 | tf_op jit(solution)/shard_map/ppermute | solution.py:38
  (2 other events, 46.0 us)

commit v3 on v2

--- a/solution.py
+++ b/solution.py
@@ -89,32 +89,49 @@
     maps[2 * 3 * face :, :] = by_half(outs[0], outs[1])
 
 
-def first_kernel(order_far, inverse_far, coupling_far, given_far, maps, inverse, coupling, given, *refs):
-    order, order_done, done = refs
+def first_kernel(order_far, inverse_far, coupling_far, given_far, *refs):
+    maps, rows, inverse_near, coupling_near, given_near = refs[:5]
+    inverse, coupling, order, order_done, done, near_done = refs[5:]
     count = inverse.shape[0]
     face = coupling.shape[1] // 3
     first = pltpu.make_async_copy(order_far, order, order_done)
     first.start()
-    pairs = ((inverse_far, inverse), (coupling_far, coupling), (given_far, given))
+    pairs = ((inverse_far, inverse), (coupling_far, coupling))
 
     def fetch(kind, slot):
         far, near = pairs[kind]
         return pltpu.make_async_copy(far.at[slot], near.at[slot], done.at[kind, slot])
 
-    for kind in range(3):
+    for kind in range(2):
         for slot in range(count):
             fetch(kind, slot).start()
     first.wait()
+    slots = [order[p] for p in range(count)]
+    later = [
+        pltpu.make_async_copy(given_far.at[slots[p]], given_near.at[p], near_done.at[0, p]) for p in range(count)
+    ]
+    for p in range(2, count):
+        later.append(
+            pltpu.make_async_copy(inverse_far.at[slots[p]], inverse_near.at[p - 2], near_done.at[1, p])
+        )
+        later.append(
+            pltpu.make_async_copy(coupling_far.at[slots[p]], coupling_near.at[p - 2], near_done.at[2, p])
+        )
+    for copy in later:
+        copy.start()
     for kind in range(2):
         for slot in range(count):
             fetch(kind, slot).wait()
-    slots = [order[p] for p in range(2)]
-    pair_maps(maps, coupling, slots, [face_rows_of(inverse, slot, face) for slot in slots], face)
-    for slot in range(count):
-        fetch(2, slot).wait()
-
-
-def rest_kernel(place, order, inverse, coupling, given, *refs):
+    values = []
+    for p in range(2):
+        values.append(face_rows_of(inverse, slots[p], face))
+        rows[p] = values[p]
+    pair_maps(maps, coupling, slots[:2], values, face)
+    for copy in later:
+        copy.wait()
+
+
+def rest_kernel(place, early_rows, inverse, coupling, given, *refs):
     count, _, width = given.shape
     maps = refs[: count // 2 - 1]
     gains = refs[count // 2 - 1 : -1]
@@ -122,11 +139,11 @@
     face = coupling.shape[1] // 3
     groups = len(gains)
     share = width // groups
-    slots = [order[p] for p in range(count)]
-    rows = [face_rows_of(inverse, slot, face) for slot in slots]
+    rows = [face_rows_of(inverse, p, face) for p in range(count - 2)]
     for j, target in enumerate(maps):
-        pair_maps(target, coupling, slots[2 * j + 2 : 2 * j + 4], rows[2 * j + 2 : 2 * j + 4], face)
-    every = [dot(rows[p], given[slots[p]]).T for p in range(count)]
+        pair_maps(target, coupling, (2 * j, 2 * j + 1), rows[2 * j : 2 * j + 2], face)
+    rows = [early_rows[0], early_rows[1]] + rows
+    every = [dot(rows[p], given[p]).T for p in range(count)]
     tiles = [gain[:, : 2 * face] for gain in every]
     for p in range(0, count, 2):
         tiles.append(by_half(every[p][:, 2 * face :], every[p + 1][:, 2 * face :]))
@@ -166,14 +183,13 @@
     return below, above
 
 
-def read_lags(me, states, lags, groups, count, first=0, live=None):
-    def read(i):
-        pos = first + i
+def read_lags(me, states, lags, groups, count):
+    def read(pos):
         below, above = neighbours(me, pos, groups)
         for p in range(count):
             lags[pos, p] = by_half(states[above, p], states[below, p])
 
-    over(live or groups, read)
+    over(groups, read)
 
 
 def over(count, body, limit=4):
@@ -195,13 +211,15 @@
 
 
 def run_chains(chosen, entries, lags, weights, gains, states, count, face):
+    share = gains.shape[2]
     outs = [[] for _ in chosen]
     for p in range(count):
         for i, pos in enumerate(chosen):
-            result = dot(jnp.concatenate([lags[pos, p], entries[i]], axis=1), weights[pos, p])
-            if gains is not None:
-                result = result + gains[pos, p].astype(F32)
-            states[pos, p] = result[:, : 2 * face].astype(BF16)
+            rows = entries[i].shape[0]
+            result = dot(jnp.concatenate([lags[pos, p, :rows], entries[i]], axis=1), weights[pos, p])
+            first = result[:share] + gains[pos, p].astype(F32)
+            result = first if rows == share else jnp.concatenate([first, result[share:]], axis=0)
+            states[pos, p, :rows] = result[:, : 2 * face].astype(BF16)
             outs[i].append(result[:, 2 * face :])
         if p < count - 1:
             entries = [split_trace(o[p])[0] for o in outs]
@@ -211,27 +229,36 @@
 def respond_kernel(place, *refs, groups, count, face):
     pairs = count // 2
     map_refs = [refs[j * groups : (j + 1) * groups] for j in range(pairs)]
-    response, weights, states, lags, unit = refs[pairs * groups :]
+    gain_refs = refs[pairs * groups : (pairs + 1) * groups]
+    response, offset, weights, gains, states, lags, unit = refs[(pairs + 1) * groups :]
     me = place[0]
     half = groups // 2
+    share = gains.shape[2]
     unpack_maps(map_refs, weights, face)
+    unpack_gains(gain_refs, gains, count)
     states[...] = jnp.zeros_like(states)
     unit[...] = jnp.zeros_like(unit)
-    row = lax.broadcasted_iota(jnp.int32, unit.shape[2:], 0)
+    row = lax.broadcasted_iota(jnp.int32, unit.shape[2:], 0) - share
     lane = lax.broadcasted_iota(jnp.int32, unit.shape[2:], 1)
     for pos in range(half):
         hit = jnp.logical_and(lane < face, row == lane + pos * face)
         unit[0, pos] = jnp.where(hit, 1.0, 0.0).astype(BF16)
 
     def sweep(k, parity):
-        read_lags(me, states, lags, groups, count, half * parity, half)
+        read_lags(me, states, lags, groups, count)
 
         def block(t):
-            chosen = [2 * t + half * parity, 2 * t + 1 + half * parity]
-            entries = [unit[jnp.minimum(k, 1), pos] for pos in chosen]
-            ends = [outs[-1] for outs in run_chains(chosen, entries, lags, weights, None, states, count, face)]
+            live = [2 * t + half * parity, 2 * t + 1 + half * parity]
+            bare = [2 * t + half * (1 - parity), 2 * t + 1 + half * (1 - parity)]
+            entries = [unit[jnp.minimum(k, 1), pos] for pos in live]
+            entries += [jnp.zeros((share, 2 * face), BF16)] * 2
+            chains = run_chains(live + bare, entries, lags, weights, gains, states, count, face)
+            ends = [outs[-1] for outs in chains]
             at = pl.ds(pl.multiple_of(t * 2 * face, 2 * face), 2 * face)
-            response[k, :, at] = by_half(ends[0], ends[1]).astype(BF16)
+            full = by_half(ends[0], ends[1])
+            response[k, :, at] = full[share:].astype(BF16)
+            for target, tile in ((parity, full[:share]), (1 - parity, by_half(ends[2], ends[3]))):
+                offset[k, target * share : (target + 1) * share, at] = tile.astype(BF16)
 
         over(groups // 4, block, 1)
 
@@ -241,33 +268,6 @@
         return carry
 
     lax.fori_loop(0, SWEEPS // 2, both, 0)
-
-
-def offset_kernel(place, weights, *refs, groups, count, face):
-    gain_refs = refs[:groups]
-    offset, gains, states, lags = refs[groups:]
-    me = place[0]
-    half = groups // 2
-    unpack_gains(gain_refs, gains, count)
-    states[...] = jnp.zeros_like(states)
-    share = gains.shape[2]
-    blank = jnp.zeros((share, 2 * face), BF16)
-
-    def sweep(k, carry):
-        read_lags(me, states, lags, groups, count)
-
-        def block(t):
-            chosen = [2 * t, 2 * t + 1, 2 * t + half, 2 * t + 1 + half]
-            outs = run_chains(chosen, [blank] * 4, lags, weights, gains, states, count, face)
-            ends = [out[-1] for out in outs]
-            at = pl.ds(pl.multiple_of(t * 2 * face, 2 * face), 2 * face)
-            offset[k, :share, at] = by_half(ends[0], ends[1]).astype(BF16)
-            offset[k, share:, at] = by_half(ends[2], ends[3]).astype(BF16)
-
-        over(groups // 4, block, 1)
-        return carry
-
-    lax.fori_loop(0, SWEEPS, sweep, 0)
 
 
 def pick(flag, first, second):
@@ -317,23 +317,48 @@
     return pair
 
 
-def join_kernel(even, odd, entry, own, joined):
+def add_own(values, maps, own):
+    moved = []
+    for k in range(SWEEPS):
+        pair = zip(moved_by(values, maps, k), own[k])
+        moved.append([(total + added.astype(F32)).astype(BF16) for total, added in pair])
+    return moved
+
+
+def put_halves(ref, values):
+    share = ref.shape[1] // 2
+    for k in range(SWEEPS):
+        for target in (0, 1):
+            ref[k, target * share : (target + 1) * share] = values[k][target]
+
+
+def opening_kernel(even, odd, entry, own, opened):
     maps = [(even[k], odd[k]) for k in range(SWEEPS)]
     values = [halves_of(entry, k) for k in range(SWEEPS)]
-    share = own.shape[1] // 2
-    for k in range(SWEEPS):
-        added = halves_of(own, k)
-        for target, total in enumerate(moved_by(values, maps, k)):
-            total = total + added[target].astype(F32)
-            joined[k, target * share : (target + 1) * share] = total.astype(BF16)
+    put_halves(opened, add_own(values, maps, [halves_of(own, k) for k in range(SWEEPS)]))
+
+
+def join_kernel(line, own, other, got, got_other, own_offset, got_offset, near, across, joined, *, mask):
+    down = (line[0] // mask) % 2
+    values = [
+        [pick(down, a, b) for a, b in zip(halves_of(near, k), halves_of(across, k))] for k in range(SWEEPS)
+    ]
+    for turn in (down, 1 - down):
+        maps = [(pick(turn, got[k], own[k]), pick(turn, got_other[k], other[k])) for k in range(SWEEPS)]
+        added = [
+            [pick(turn, a, b) for a, b in zip(halves_of(got_offset, k), halves_of(own_offset, k))]
+            for k in range(SWEEPS)
+        ]
+        values = add_own(values, maps, added)
+    put_halves(joined, values)
 
 
 def resolve_kernel(place, line, *refs, groups, count, face, masks):
-    weights, gains, ahead, second, third, ahead_even, ahead_odd = refs[:7]
+    weights, gains, near, across, second, third, ahead_even, ahead_odd = refs[:8]
     levels = len(masks) - 2
-    lower = refs[7 : 7 + 3 * levels]
-    wanted = refs[7 + 3 * levels : 7 + 3 * levels + groups]
-    states, lags, inflows = refs[7 + 3 * levels + groups :]
+    lower = refs[8 : 8 + 3 * levels]
+    wanted = refs[8 + 3 * levels : 8 + 3 * levels + groups]
+    states, lags, inflows = refs[8 + 3 * levels + groups :]
     me = place[0]
     half = groups // 2
     states[...] = jnp.zeros_like(states)
@@ -344,7 +369,7 @@
     for k in range(SWEEPS):
         pair = []
         for target, total in enumerate(moved_by(given, maps, k)):
-            own = halves_of(ahead, k)[target]
+            own = pick(flags[-3], halves_of(near, k)[target], halves_of(across, k)[target])
             last = (total + own.astype(F32)).astype(BF16)
             upper = pick(flags[-2], last, halves_of(second, k)[target])
             pair.append(pick(flags[-1], upper, pick(flags[-2], own, jnp.zeros_like(own))))
@@ -443,7 +468,7 @@
         out_shape=outs,
         in_specs=[SMEM] * len(scalars) + [VMEM] * (len(arrays) - far) + [HBM] * far,
         out_specs=[VMEM] * len(outs),
-        scratch_shapes=[*others[:1], *[pltpu.VMEM(shape, kind) for shape, kind in scratch], *others[1:]],
+        scratch_shapes=[*[pltpu.VMEM(shape, kind) for shape, kind in scratch], *others],
         compiler_params=pltpu.CompilerParams(vmem_limit_bytes=grant or min(held + (3 << 20), 60 << 20)),
     )(*scalars, *arrays)
 
@@ -468,17 +493,19 @@
         first_kernel,
         [
             shape((3 * 3 * face, 2 * face), BF16),
-            shape(inverse.shape, BF16),
-            shape(coupling.shape, BF16),
+            shape((2, 4 * face, nodes), BF16),
+            shape((count - 2,) + inverse.shape[1:], BF16),
+            shape((count - 2,) + coupling.shape[1:], BF16),
             shape(given.shape, BF16),
         ],
-        [],
+        [(inverse.shape, BF16), (coupling.shape, BF16)],
         [],
         far,
         4,
         (
             pltpu.SMEM(order.shape, order.dtype),
             pltpu.SemaphoreType.DMA,
+            pltpu.SemaphoreType.DMA((2, count)),
             pltpu.SemaphoreType.DMA((3, count)),
         ),
     )
@@ -487,7 +514,7 @@
         rest_kernel,
         [shape(maps.shape, BF16)] * (count // 2 - 1) + [shape((tiles, share, 2 * face), BF16)] * groups,
         [((tiles, width, 2 * face), F32)],
-        [place, far[0]],
+        [place],
         near,
     )
     gains = outs[count // 2 - 1 :]
@@ -496,55 +523,45 @@
     gains = exchange(gains, "span")
     sizes = dict(groups=groups, count=count, face=face)
     wide = half * face
-    response, weights = call(
+    response, offset, weights, gains = call(
         functools.partial(respond_kernel, **sizes),
         [
             shape((SWEEPS, wide, wide), BF16),
+            shape((SWEEPS, 2 * share, wide), BF16),
             shape((groups, count, 4 * face, 4 * face), BF16),
-        ],
-        [
-            ((groups + 1, count, wide, 2 * face), BF16),
-            ((groups, count, wide, 2 * face), BF16),
-            ((2, groups, wide, 2 * face), BF16),
-        ],
-        [place],
-        all_maps,
-    )
-    offset, gains = call(
-        functools.partial(offset_kernel, **sizes),
-        [
-            shape((SWEEPS, 2 * share, wide), BF16),
             shape((groups, count, share, 4 * face), BF16),
         ],
         [
-            ((groups + 1, count, share, 2 * face), BF16),
-            ((groups, count, share, 2 * face), BF16),
+            ((groups + 1, count, share + wide, 2 * face), BF16),
+            ((groups, count, share + wide, 2 * face), BF16),
+            ((2, groups, share + wide, 2 * face), BF16),
         ],
         [place],
-        [weights, *gains],
+        [*all_maps, *gains],
     )
     levels = []
     for mask in masks[:-2]:
+        got_offset = swap(offset, "stream", mask)
+        other = swap(response, "span", 1)
         got = swap(response, "stream", mask)
-        other = swap(response, "span", 1)
         got_other = swap(got, "span", 1)
-        got_offset = swap(offset, "stream", mask)
         levels += [got, got_other, got_offset]
         arrays = [response, other, got, got_other]
-        (offset,) = call(
-            functools.partial(pair_offset_kernel, mask=mask),
-            [shape(offset.shape, BF16)],
-            [],
-            [line],
-            arrays + [offset, got_offset],
-        )
+        same = shape(offset.shape, BF16)
+        if mask == masks[-3]:
+            (opened,) = call(opening_kernel, [same], [], [], [response, other, got_offset, offset])
+            near = swap(opened, "stream", masks[-2])
+            across = swap(opened, "stream", masks[-2] | mask)
+            joining = arrays + [offset, got_offset, near, across]
+        else:
+            (offset,) = call(
+                functools.partial(pair_offset_kernel, mask=mask), [same], [], [line], arrays + [offset, got_offset]
+            )
         (response,) = call(
             functools.partial(pair_map_kernel, mask=mask), [shape(response.shape, BF16)], [], [line], arrays
         )
-    ahead = swap(offset, "stream", masks[-2])
-    other = swap(response, "span", 1)
     ahead_even = swap(response, "stream", masks[-2])
-    (joined,) = call(join_kernel, [shape(offset.shape, BF16)], [], [], [response, other, ahead, offset])
+    (joined,) = call(functools.partial(join_kernel, mask=masks[-3]), [same], [], [line], joining)
     second = lax.ppermute(joined, "stream", crossing(masks))
     third = swap(joined, "stream", masks[-1])
     ahead_odd = swap(ahead_even, "span", 1)
@@ -557,7 +574,7 @@
             ((SWEEPS, groups, share, 2 * face), BF16),
         ],
         [place, line],
-        [weights, gains, ahead, second, third, ahead_even, ahead_odd, *levels],
+        [weights, gains, near, across, second, third, ahead_even, ahead_odd, *levels],
     )
     wanted = exchange(wanted, "span")
     (placed,) = call(

time: 69 us -> 68 us (0.986)
  starting transfers between devices: 16.4 us -> 20 us
  Pallas kernels: 18.2 us -> 15.5 us
  waiting for transfers between devices: 34.1 us -> 32.3 us
    ppermute x21, starting transfers between devices: 14.7 us -> 19.5 us  [swap(): return lax.ppermute(value, axis, [(i, i ^ mask) for i in range(count)])]
    pallas_call x9 -> x8, Pallas kernels: 18.2 us -> 15.5 us  [call(): pl.pallas_call(kernel, out_shape=outs, in_specs=[SMEM] * len(scalars) + [...]
    ppermute x1, waiting for transfers between devices: 1.83 us -> 0.3 us  [shards(): second = lax.ppermute(joined, 'stream', crossing(masks))]
    ppermute x1, starting transfers between devices: 1.7 us -> 0.5 us  [shards(): second = lax.ppermute(joined, 'stream', crossing(masks))]
  transfers between devices with their start and end apart: 22 -> 22, of which waited for: 13 -> 13; matrix products, arithmetic and copies ran while one was open for 0% -> 0% of each run, Pallas kernels for 6% -> 1%
where the time goes in v3:
time: 68 us; the launch traced here: 67.9 us
  waiting for transfers between devices  32.3 us (47%)
  starting transfers between devices  20 us (29%)
  Pallas kernels  15.5 us (23%)
    ppermute x21, waiting for transfers between devices, swap(): return lax.ppermute(value, axis, [(i, i ^ mask) for i in range(count)])  32 us
    ppermute x21, starting transfers between devices, swap(): return lax.ppermute(value, axis, [(i, i ^ mask) for i in range(count)])  19.5 us
    pallas_call x8, Pallas kernels, call(): pl.pallas_call(kernel, out_shape=outs, in_specs=[SMEM] * len(scalars) + [...  15.5 us
  transfers between devices with their start and end apart: 22, of which 13 were waited for; matrix products, arithmetic and copies ran while one was open for 0% of the time, Pallas kernels for 1%

profile of v3, /device:TPU:0, one launch (start us, length us, event | category | flops | bytes accessed | tf_op | source)
XLA Modules:
  0.0 67.9 jit_solution(4994343894941647379)
XLA Ops:
  0.0 2.7 %shard_map.46 = (bf16[576,128]{1,0:T(8,128)(2,1)S(1)}, bf16[2,256,512]{2,1,0:T(8,128)(2,1)S(1)}, bf16[2,512,512]{2,1,0:T(8,128)(2,1)S(1)}, bf16[2,192,512]{2,1,0:T(8,128)(2,1)S(1)}, bf16[4,512,128]{2,1,0:T(8,128)(2,1)S(1)}) custom-call(s32[4]{0:T(128)} %bitcast.13, bf16[4,512,512]{2,1,0:T(8,128)(2,1)} %bitcast.7, bf16[4,192,512]{2,1,0:T(8,128)(2,1)} %bitcast.9, ...), custom_call_target="tpu_custom_call" | custom-call | tf_op jit(solution)/shard_map/pallas_call | solution.py:466
  3.4 3.0 %collective-permute-start.3 = (bf16[576,128]{1,0:T(8,128)(2,1)S(1)}, bf16[576,128]{1,0:T(8,128)(2,1)S(1)}, u32[]{:S(2)}, u32[]{:S(2)}) collective-permute-start(bf16[576,128]{1,0:T(8,128)(2,1)S(1)} %get-tuple-element.28.refs_4_), channel_id=1, source_target_pairs={{0,2},{1,3},{2,0},{3,1},{4,6},{5,7},{6,4},{7,5},{8,10},{9,11},{10,... | collective-permute-start | bytes 442376 | tf_op jit(solution)/shard_map/ppermute | solution.py:38
  7.1 4.1 %collective-permute-done.3.refs_5_ = bf16[576,128]{1,0:T(8,128)(2,1)S(1)} collective-permute-done((bf16[576,128]{1,0:T(8,128)(2,1)S(1)}, bf16[576,128]{1,0:T(8,128)(2,1)S(1)}, u32[]{:S(2)}, u32[]{:S(2)}) %collective-permute-start.3) | collective-permute-done | bytes 147488 | tf_op jit(solution)/shard_map/ppermute | solution.py:38
  11.2 2.3 %collective-permute-done.refs_1_ = bf16[576,128]{1,0:T(8,128)(2,1)S(1)} collective-permute-done((bf16[576,128]{1,0:T(8,128)(2,1)S(1)}, bf16[576,128]{1,0:T(8,128)(2,1)S(1)}, u32[]{:S(2)}, u32[]{:S(2)}) %collective-permute-start) | collective-permute-done | bytes 147488 | tf_op jit(solution)/shard_map/ppermute | solution.py:38
  13.5 1.7 %collective-permute-start.7 = (bf16[6,32,128]{2,1,0:T(8,128)(2,1)S(1)}, bf16[6,32,128]{2,1,0:T(8,128)(2,1)S(1)}, u32[]{:S(2)}, u32[]{:S(2)}) collective-permute-start(bf16[6,32,128]{2,1,0:T(8,128)(2,1)S(1)} %get-tuple-element.31), channel_id=1, source_target_pairs={{0,2},{1,3},{2,0},{3,1},{4,6},{5,7},{6,4},{7,5},{8,10},{9,11},{10,... | collective-permute-start | bytes 147464 | tf_op jit(solution)/shard_map/ppermute | solution.py:38
  15.2 2.4 %collective-permute-done.7.refs_10_ = bf16[6,32,128]{2,1,0:T(8,128)(2,1)S(1)} collective-permute-done((bf16[6,32,128]{2,1,0:T(8,128)(2,1)S(1)}, bf16[6,32,128]{2,1,0:T(8,128)(2,1)S(1)}, u32[]{:S(2)}, u32[]{:S(2)}) %collective-permute-start.7) | collective-permute-done | bytes 49184 | tf_op jit(solution)/shard_map/ppermute | solution.py:38
  18.6 2.8 %collective-permute-done.8.refs_11_ = bf16[6,32,128]{2,1,0:T(8,128)(2,1)S(1)} collective-permute-done((bf16[6,32,128]{2,1,0:T(8,128)(2,1)S(1)}, bf16[6,32,128]{2,1,0:T(8,128)(2,1)S(1)}, u32[]{:S(2)}, u32[]{:S(2)}) %collective-permute-start.8) | collective-permute-done | bytes 49184 | tf_op jit(solution)/shard_map/ppermute | solution.py:38
  21.4 4.2 %shard_map.48 = (bf16[6,128,128]{2,1,0:T(8,128)(2,1)S(1)}, bf16[6,64,128]{2,1,0:T(8,128)(2,1)S(1)}, bf16[4,4,256,256]{3,2,1,0:T(8,128)(2,1)S(1)}, bf16[4,4,32,256]{3,2,1,0:T(8,128)(2,1)S(1)}) custom-call(s32[1]{0:T(128)} %bitcast.place, bf16[576,128]{1,0:T(8,128)(2,1)S(1)} %get-tuple-element.23.refs_0_, bf16[576,128]{1,0:T(8,128)(2,1)S(1)} %collective-permute-done.refs_1_, ...), custom_call_target="tpu_custom_call" | custom-call | tf_op jit(solution)/shard_map/pallas_call | solution.py:466
  25.6 2.1 %collective-permute-start.13 = (bf16[6,128,128]{2,1,0:T(8,128)(2,1)S(1)}, bf16[6,128,128]{2,1,0:T(8,128)(2,1)S(1)}, u32[]{:S(2)}, u32[]{:S(2)}) collective-permute-start(bf16[6,128,128]{2,1,0:T(8,128)(2,1)S(1)} %get-tuple-element.35.even.own), channel_id=1, source_target_pairs={{0,4},{4,0},{8,12},{12,8},{16,20},{20,16},{24,28},{28,24},{1,5},{5... | collective-permute-start | bytes 589832 | tf_op jit(solution)/shard_map/ppermute | solution.py:38
  27.7 5.2 %collective-permute-done.13.got.refs_8_ = bf16[6,128,128]{2,1,0:T(8,128)(2,1)S(1)} collective-permute-done((bf16[6,128,128]{2,1,0:T(8,128)(2,1)S(1)}, bf16[6,128,128]{2,1,0:T(8,128)(2,1)S(1)}, u32[]{:S(2)}, u32[]{:S(2)}) %collective-permute-start.13) | collective-permute-done | bytes 196640 | tf_op jit(solution)/shard_map/ppermute | solution.py:38
  32.9 1.4 %collective-permute-done.14.got_other.refs_9_ = bf16[6,128,128]{2,1,0:T(8,128)(2,1)S(1)} collective-permute-done((bf16[6,128,128]{2,1,0:T(8,128)(2,1)S(1)}, bf16[6,128,128]{2,1,0:T(8,128)(2,1)S(1)}, u32[]{:S(2)}, u32[]{:S(2)}) %collective-permute-start.14) | collective-permute-done | bytes 196640 | tf_op jit(solution)/shard_map/ppermute | solution.py:38
  34.7 1.9 %collective-permute-start.17 = (bf16[6,128,128]{2,1,0:T(8,128)(2,1)S(1)}, bf16[6,128,128]{2,1,0:T(8,128)(2,1)S(1)}, u32[]{:S(2)}, u32[]{:S(2)}) collective-permute-start(bf16[6,128,128]{2,1,0:T(8,128)(2,1)S(1)} %shard_map.51), channel_id=1, source_target_pairs={{0,8},{4,12},{8,0},{12,4},{16,24},{20,28},{24,16},{28,20},{1,9},{5... | collective-permute-start | bytes 589832 | tf_op jit(solution)/shard_map/ppermute | solution.py:38
  36.5 1.5 %collective-permute-start.10 = (bf16[6,64,128]{2,1,0:T(8,128)(2,1)S(1)}, bf16[6,64,128]{2,1,0:T(8,128)(2,1)S(1)}, u32[]{:S(2)}, u32[]{:S(2)}) collective-permute-start(bf16[6,64,128]{2,1,0:T(8,128)(2,1)S(1)} %get-tuple-element.36.own.own_offset), channel_id=1, source_target_pairs={{0,4},{4,0},{8,12},{12,8},{16,20},{20,16},{24,28},{28,24},{1,5},{5... | collective-permute-start | bytes 294920 | tf_op jit(solution)/shard_map/ppermute | solution.py:38
  38.1 3.1 %collective-permute-done.10.entry.got_offset.refs_10_ = bf16[6,64,128]{2,1,0:T(8,128)(2,1)S(1)} collective-permute-done((bf16[6,64,128]{2,1,0:T(8,128)(2,1)S(1)}, bf16[6,64,128]{2,1,0:T(8,128)(2,1)S(1)}, u32[]{:S(2)}, u32[]{:S(2)}) %collective-permute-start.10) | collective-permute-done | bytes 98336 | tf_op jit(solution)/shard_map/ppermute | solution.py:38
  41.5 1.5 %collective-permute-start.12 = (bf16[6,64,128]{2,1,0:T(8,128)(2,1)S(1)}, bf16[6,64,128]{2,1,0:T(8,128)(2,1)S(1)}, u32[]{:S(2)}, u32[]{:S(2)}) collective-permute-start(bf16[6,64,128]{2,1,0:T(8,128)(2,1)S(1)} %shard_map.49), channel_id=1, source_target_pairs={{0,12},{4,8},{8,4},{12,0},{16,28},{20,24},{24,20},{28,16},{1,13},{... | collective-permute-start | bytes 294920 | tf_op jit(solution)/shard_map/ppermute | solution.py:38
  43.0 1.6 %collective-permute-start.11 = (bf16[6,64,128]{2,1,0:T(8,128)(2,1)S(1)}, bf16[6,64,128]{2,1,0:T(8,128)(2,1)S(1)}, u32[]{:S(2)}, u32[]{:S(2)}) collective-permute-start(bf16[6,64,128]{2,1,0:T(8,128)(2,1)S(1)} %shard_map.49), channel_id=1, source_target_pairs={{0,8},{4,12},{8,0},{12,4},{16,24},{20,28},{24,16},{28,20},{1,9},{5... | collective-permute-start | bytes 294920 | tf_op jit(solution)/shard_map/ppermute | solution.py:38
  44.6 2.6 %collective-permute-done.12.across.refs_3_ = bf16[6,64,128]{2,1,0:T(8,128)(2,1)S(1)} collective-permute-done((bf16[6,64,128]{2,1,0:T(8,128)(2,1)S(1)}, bf16[6,64,128]{2,1,0:T(8,128)(2,1)S(1)}, u32[]{:S(2)}, u32[]{:S(2)}) %collective-permute-start.12) | collective-permute-done | bytes 98336 | tf_op jit(solution)/shard_map/ppermute | solution.py:38
  47.2 1.1 %collective-permute-done.11.near.refs_2_ = bf16[6,64,128]{2,1,0:T(8,128)(2,1)S(1)} collective-permute-done((bf16[6,64,128]{2,1,0:T(8,128)(2,1)S(1)}, bf16[6,64,128]{2,1,0:T(8,128)(2,1)S(1)}, u32[]{:S(2)}, u32[]{:S(2)}) %collective-permute-start.11) | collective-permute-done | bytes 98336 | tf_op jit(solution)/shard_map/ppermute | solution.py:38
  48.9 2.6 %collective-permute-start.16 = (bf16[6,64,128]{2,1,0:T(8,128)(2,1)S(1)}, bf16[6,64,128]{2,1,0:T(8,128)(2,1)S(1)}, u32[]{:S(2)}, u32[]{:S(2)}) collective-permute-start(bf16[6,64,128]{2,1,0:T(8,128)(2,1)S(1)} %shard_map.50), channel_id=1, source_target_pairs={{0,16},{4,20},{8,24},{12,28},{16,0},{20,4},{24,8},{28,12},{1,17},{... | collective-permute-start | bytes 294920 | tf_op jit(solution)/shard_map/ppermute | solution.py:38
  52.1 3.8 %collective-permute-done.16.refs_5_ = bf16[6,64,128]{2,1,0:T(8,128)(2,1)S(1)} collective-permute-done((bf16[6,64,128]{2,1,0:T(8,128)(2,1)S(1)}, bf16[6,64,128]{2,1,0:T(8,128)(2,1)S(1)}, u32[]{:S(2)}, u32[]{:S(2)}) %collective-permute-start.16) | collective-permute-done | bytes 98336 | tf_op jit(solution)/shard_map/ppermute | solution.py:38
  56.2 4.0 %shard_map.52 = (bf16[6,32,128]{2,1,0:T(8,128)(2,1)S(1)}, bf16[6,32,128]{2,1,0:T(8,128)(2,1)S(1)}, bf16[6,32,128]{2,1,0:T(8,128)(2,1)S(1)}, bf16[6,32,128]{2,1,0:T(8,128)(2,1)S(1)}) custom-call(s32[1]{0:T(128)} %bitcast.place, s32[1]{0:T(128)} %bitcast.5.line, bf16[4,4,256,256]{3,2,1,0:T(8,128)(2,1)S(1)} %get-tuple-element.33.refs_0_, ...), custom_call_target="tpu_custom_call" | custom-call | tf_op jit(solution)/shard_map/pallas_call | solution.py:466
  60.3 1.3 %collective-permute-start.20 = (bf16[6,32,128]{2,1,0:T(8,128)(2,1)S(1)}, bf16[6,32,128]{2,1,0:T(8,128)(2,1)S(1)}, u32[]{:S(2)}, u32[]{:S(2)}) collective-permute-start(bf16[6,32,128]{2,1,0:T(8,128)(2,1)S(1)} %get-tuple-element.39), channel_id=1, source_target_pairs={{0,2},{1,3},{2,0},{3,1},{4,6},{5,7},{6,4},{7,5},{8,10},{9,11},{10,... | collective-permute-start | bytes 147464 | tf_op jit(solution)/shard_map/ppermute | solution.py:38
  62.1 2.3 %collective-permute-done.20.refs_2_ = bf16[6,32,128]{2,1,0:T(8,128)(2,1)S(1)} collective-permute-done((bf16[6,32,128]{2,1,0:T(8,128)(2,1)S(1)}, bf16[6,32,128]{2,1,0:T(8,128)(2,1)S(1)}, u32[]{:S(2)}, u32[]{:S(2)}) %collective-permute-start.20) | collective-permute-done | bytes 49184 | tf_op jit(solution)/shard_map/ppermute | solution.py:38
  65.3 2.6 %shard_map.53 = bf16[4,512,128]{2,1,0:T(8,128)(2,1)} custom-call(s32[1]{0:T(128)} %bitcast.place, s32[4]{0:T(128)S(1)} %bitcast.14, bf16[4,512,512]{2,1,0:T(8,128)(2,1)S(1)} %bitcast.8, bf16[4,192,512]{2,1,0:T(8,128)(2,1)S(1)} %bitcast.10, bf16[4,512,128]{2,1,0:T(8,128)(2,1)S(1)} %bitcast.12, bf16[6,32,128]{2,1,0:T(8,128)(2,1)S(1)} %get-tuple-element.37.refs_0_, ...), custom_call_target="tpu_custom_call" | custom-call | tf_op jit(solution)/shard_map/pallas_call | solution.py:466
  (36 shorter events, 5.8 us)
Async XLA Ops:
  3.4 7.7 %collective-permute-start.3 = (bf16[576,128]{1,0:T(8,128)(2,1)S(1)}, bf16[576,128]{1,0:T(8,128)(2,1)S(1)}, u32[]{:S(2)}, u32[]{:S(2)}) collective-permute-start(bf16[576,128]{1,0:T(8,128)(2,1)S(1)} %get-tuple-element.28.refs_4_), channel_id=1, source_target_pairs={{0,2},{1,3},{2,0},{3,1},{4,6},{5,7},{6,4},{7,5},{8,10},{9,11},{10,... | collective-permute-start | bytes 442376 | tf_op jit(solution)/shard_map/ppermute | solution.py:38
  6.5 7.0 %collective-permute-start = (bf16[576,128]{1,0:T(8,128)(2,1)S(1)}, bf16[576,128]{1,0:T(8,128)(2,1)S(1)}, u32[]{:S(2)}, u32[]{:S(2)}) collective-permute-start(bf16[576,128]{1,0:T(8,128)(2,1)S(1)} %get-tuple-element.23.refs_0_), channel_id=1, source_target_pairs={{0,2},{1,3},{2,0},{3,1},{4,6},{5,7},{6,4},{7,5},{8,10},{9,11},{10,... | collective-permute-start | bytes 442376 | tf_op jit(solution)/shard_map/ppermute | solution.py:38
  6.5 6.9 %collective-permute-start.6 = (bf16[6,32,128]{2,1,0:T(8,128)(2,1)S(1)}, bf16[6,32,128]{2,1,0:T(8,128)(2,1)S(1)}, u32[]{:S(2)}, u32[]{:S(2)}) collective-permute-start(bf16[6,32,128]{2,1,0:T(8,128)(2,1)S(1)} %get-tuple-element.30), channel_id=1, source_target_pairs={{0,1},{1,0},{2,3},{3,2},{4,5},{5,4},{6,7},{7,6},{8,9},{9,8},{10,11... | collective-permute-start | bytes 147464 | tf_op jit(solution)/shard_map/ppermute | solution.py:38
  6.5 14.8 %collective-permute-start.4 = (bf16[576,128]{1,0:T(8,128)(2,1)S(1)}, bf16[576,128]{1,0:T(8,128)(2,1)S(1)}, u32[]{:S(2)}, u32[]{:S(2)}) collective-permute-start(bf16[576,128]{1,0:T(8,128)(2,1)S(1)} %get-tuple-element.28.refs_4_), channel_id=1, source_target_pairs={{0,1},{1,0},{2,3},{3,2},{4,5},{5,4},{6,7},{7,6},{8,9},{9,8},{10,11... | collective-permute-start | bytes 442376 | tf_op jit(solution)/shard_map/ppermute | solution.py:38
  7.1 14.3 %collective-permute-start.1 = (bf16[576,128]{1,0:T(8,128)(2,1)S(1)}, bf16[576,128]{1,0:T(8,128)(2,1)S(1)}, u32[]{:S(2)}, u32[]{:S(2)}) collective-permute-start(bf16[576,128]{1,0:T(8,128)(2,1)S(1)} %get-tuple-element.23.refs_0_), channel_id=1, source_target_pairs={{0,1},{1,0},{2,3},{3,2},{4,5},{5,4},{6,7},{7,6},{8,9},{9,8},{10,11... | collective-permute-start | bytes 442376 | tf_op jit(solution)/shard_map/ppermute | solution.py:38
  11.2 10.2 %collective-permute-start.5 = (bf16[576,128]{1,0:T(8,128)(2,1)S(1)}, bf16[576,128]{1,0:T(8,128)(2,1)S(1)}, u32[]{:S(2)}, u32[]{:S(2)}) collective-permute-start(bf16[576,128]{1,0:T(8,128)(2,1)S(1)} %collective-permute-done.3.refs_5_), channel_id=1, source_target_pairs={{0,1},{1,0},{2,3},{3,2},{4,5},{5,4},{6,7},{7,6},{8,9},{9,8},{10,11... | collective-permute-start | bytes 442376 | tf_op jit(solution)/shard_map/ppermute | solution.py:38
  13.5 7.9 %collective-permute-start.2 = (bf16[576,128]{1,0:T(8,128)(2,1)S(1)}, bf16[576,128]{1,0:T(8,128)(2,1)S(1)}, u32[]{:S(2)}, u32[]{:S(2)}) collective-permute-start(bf16[576,128]{1,0:T(8,128)(2,1)S(1)} %collective-permute-done.refs_1_), channel_id=1, source_target_pairs={{0,1},{1,0},{2,3},{3,2},{4,5},{5,4},{6,7},{7,6},{8,9},{9,8},{10,11... | collective-permute-start | bytes 442376 | tf_op jit(solution)/shard_map/ppermute | solution.py:38
  13.5 4.2 %collective-permute-start.7 = (bf16[6,32,128]{2,1,0:T(8,128)(2,1)S(1)}, bf16[6,32,128]{2,1,0:T(8,128)(2,1)S(1)}, u32[]{:S(2)}, u32[]{:S(2)}) collective-permute-start(bf16[6,32,128]{2,1,0:T(8,128)(2,1)S(1)} %get-tuple-element.31), channel_id=1, source_target_pairs={{0,2},{1,3},{2,0},{3,1},{4,6},{5,7},{6,4},{7,5},{8,10},{9,11},{10,... | collective-permute-start | bytes 147464 | tf_op jit(solution)/shard_map/ppermute | solution.py:38
  17.6 3.7 %collective-permute-start.8 = (bf16[6,32,128]{2,1,0:T(8,128)(2,1)S(1)}, bf16[6,32,128]{2,1,0:T(8,128)(2,1)S(1)}, u32[]{:S(2)}, u32[]{:S(2)}) collective-permute-start(bf16[6,32,128]{2,1,0:T(8,128)(2,1)S(1)} %get-tuple-element.32), channel_id=1, source_target_pairs={{0,3},{1,2},{2,1},{3,0},{4,7},{5,6},{6,5},{7,4},{8,11},{9,10},{10,... | collective-permute-start | bytes 147464 | tf_op jit(solution)/shard_map/ppermute | solution.py:38
  25.6 7.2 %collective-permute-start.13 = (bf16[6,128,128]{2,1,0:T(8,128)(2,1)S(1)}, bf16[6,128,128]{2,1,0:T(8,128)(2,1)S(1)}, u32[]{:S(2)}, u32[]{:S(2)}) collective-permute-start(bf16[6,128,128]{2,1,0:T(8,128)(2,1)S(1)} %get-tuple-element.35.even.own), channel_id=1, source_target_pairs={{0,4},{4,0},{8,12},{12,8},{16,20},{20,16},{24,28},{28,24},{1,5},{5... | collective-permute-start | bytes 589832 | tf_op jit(solution)/shard_map/ppermute | solution.py:38
  27.7 5.2 %collective-permute-start.9 = (bf16[6,128,128]{2,1,0:T(8,128)(2,1)S(1)}, bf16[6,128,128]{2,1,0:T(8,128)(2,1)S(1)}, u32[]{:S(2)}, u32[]{:S(2)}) collective-permute-start(bf16[6,128,128]{2,1,0:T(8,128)(2,1)S(1)} %get-tuple-element.35.even.own), channel_id=1, source_target_pairs={{0,1},{1,0},{2,3},{3,2},{4,5},{5,4},{6,7},{7,6},{8,9},{9,8},{10,11... | collective-permute-start | bytes 589832 | tf_op jit(solution)/shard_map/ppermute | solution.py:38
  32.9 1.4 %collective-permute-start.14 = (bf16[6,128,128]{2,1,0:T(8,128)(2,1)S(1)}, bf16[6,128,128]{2,1,0:T(8,128)(2,1)S(1)}, u32[]{:S(2)}, u32[]{:S(2)}) collective-permute-start(bf16[6,128,128]{2,1,0:T(8,128)(2,1)S(1)} %collective-permute-done.13.got.refs_8_), channel_id=1, source_target_pairs={{0,1},{1,0},{2,3},{3,2},{4,5},{5,4},{6,7},{7,6},{8,9},{9,8},{10,11... | collective-permute-start | bytes 589832 | tf_op jit(solution)/shard_map/ppermute | solution.py:38
  34.7 9.9 %collective-permute-start.17 = (bf16[6,128,128]{2,1,0:T(8,128)(2,1)S(1)}, bf16[6,128,128]{2,1,0:T(8,128)(2,1)S(1)}, u32[]{:S(2)}, u32[]{:S(2)}) collective-permute-start(bf16[6,128,128]{2,1,0:T(8,128)(2,1)S(1)} %shard_map.51), channel_id=1, source_target_pairs={{0,8},{4,12},{8,0},{12,4},{16,24},{20,28},{24,16},{28,20},{1,9},{5... | collective-permute-start | bytes 589832 | tf_op jit(solution)/shard_map/ppermute | solution.py:38
  36.5 4.6 %collective-permute-start.10 = (bf16[6,64,128]{2,1,0:T(8,128)(2,1)S(1)}, bf16[6,64,128]{2,1,0:T(8,128)(2,1)S(1)}, u32[]{:S(2)}, u32[]{:S(2)}) collective-permute-start(bf16[6,64,128]{2,1,0:T(8,128)(2,1)S(1)} %get-tuple-element.36.own.own_offset), channel_id=1, source_target_pairs={{0,4},{4,0},{8,12},{12,8},{16,20},{20,16},{24,28},{28,24},{1,5},{5... | collective-permute-start | bytes 294920 | tf_op jit(solution)/shard_map/ppermute | solution.py:38
  41.5 5.7 %collective-permute-start.12 = (bf16[6,64,128]{2,1,0:T(8,128)(2,1)S(1)}, bf16[6,64,128]{2,1,0:T(8,128)(2,1)S(1)}, u32[]{:S(2)}, u32[]{:S(2)}) collective-permute-start(bf16[6,64,128]{2,1,0:T(8,128)(2,1)S(1)} %shard_map.49), channel_id=1, source_target_pairs={{0,12},{4,8},{8,4},{12,0},{16,28},{20,24},{24,20},{28,16},{1,13},{... | collective-permute-start | bytes 294920 | tf_op jit(solution)/shard_map/ppermute | solution.py:38
  43.0 5.4 %collective-permute-start.11 = (bf16[6,64,128]{2,1,0:T(8,128)(2,1)S(1)}, bf16[6,64,128]{2,1,0:T(8,128)(2,1)S(1)}, u32[]{:S(2)}, u32[]{:S(2)}) collective-permute-start(bf16[6,64,128]{2,1,0:T(8,128)(2,1)S(1)} %shard_map.49), channel_id=1, source_target_pairs={{0,8},{4,12},{8,0},{12,4},{16,24},{20,28},{24,16},{28,20},{1,9},{5... | collective-permute-start | bytes 294920 | tf_op jit(solution)/shard_map/ppermute | solution.py:38
  44.6 11.6 %collective-permute-start.18 = (bf16[6,128,128]{2,1,0:T(8,128)(2,1)S(1)}, bf16[6,128,128]{2,1,0:T(8,128)(2,1)S(1)}, u32[]{:S(2)}, u32[]{:S(2)}) collective-permute-start(bf16[6,128,128]{2,1,0:T(8,128)(2,1)S(1)} %collective-permute-done.17.refs_6_), channel_id=1, source_target_pairs={{0,1},{1,0},{2,3},{3,2},{4,5},{5,4},{6,7},{7,6},{8,9},{9,8},{10,11... | collective-permute-start | bytes 589832 | tf_op jit(solution)/shard_map/ppermute | solution.py:38
  48.9 16.4 %copy-start = (bf16[1,1,4,512,512]{4,3,2,1,0:T(8,128)(2,1)S(1)}, bf16[1,1,4,512,512]{4,3,2,1,0:T(8,128)(2,1)}, u32[]{:S(2)}) copy-start(bf16[1,1,4,512,512]{4,3,2,1,0:T(8,128)(2,1)} %param.5) | copy-start | bytes 6291460
  48.9 16.4 %copy-start.1 = (bf16[1,1,4,3,64,512]{5,4,3,2,1,0:T(8,128)(2,1)S(1)}, bf16[1,1,4,3,64,512]{5,4,3,2,1,0:T(8,128)(2,1)}, u32[]{:S(2)}) copy-start(bf16[1,1,4,3,64,512]{5,4,3,2,1,0:T(8,128)(2,1)} %param.6) | copy-start | bytes 2359300
  48.9 7.0 %collective-permute-start.16 = (bf16[6,64,128]{2,1,0:T(8,128)(2,1)S(1)}, bf16[6,64,128]{2,1,0:T(8,128)(2,1)S(1)}, u32[]{:S(2)}, u32[]{:S(2)}) collective-permute-start(bf16[6,64,128]{2,1,0:T(8,128)(2,1)S(1)} %shard_map.50), channel_id=1, source_target_pairs={{0,16},{4,20},{8,24},{12,28},{16,0},{20,4},{24,8},{28,12},{1,17},{... | collective-permute-start | bytes 294920 | tf_op jit(solution)/shard_map/ppermute | solution.py:38
  51.6 4.6 %collective-permute-start.15 = (bf16[6,64,128]{2,1,0:T(8,128)(2,1)S(1)}, bf16[6,64,128]{2,1,0:T(8,128)(2,1)S(1)}, u32[]{:S(2)}, u32[]{:S(2)}) collective-permute-start(bf16[6,64,128]{2,1,0:T(8,128)(2,1)S(1)} %shard_map.50), channel_id=1, source_target_pairs={{0,4},{4,0},{8,16},{12,20},{16,8},{20,12},{24,28},{28,24},{1,5},{5... | collective-permute-start | bytes 294920 | tf_op jit(solution)/shard_map/ppermute | solution.py:565
  60.2 1.9 %collective-permute-start.19 = (bf16[6,32,128]{2,1,0:T(8,128)(2,1)S(1)}, bf16[6,32,128]{2,1,0:T(8,128)(2,1)S(1)}, u32[]{:S(2)}, u32[]{:S(2)}) collective-permute-start(bf16[6,32,128]{2,1,0:T(8,128)(2,1)S(1)} %get-tuple-element.38), channel_id=1, source_target_pairs={{0,1},{1,0},{2,3},{3,2},{4,5},{5,4},{6,7},{7,6},{8,9},{9,8},{10,11... | collective-permute-start | bytes 147464 | tf_op jit(solution)/shard_map/ppermute | solution.py:38
  60.3 4.2 %collective-permute-start.20 = (bf16[6,32,128]{2,1,0:T(8,128)(2,1)S(1)}, bf16[6,32,128]{2,1,0:T(8,128)(2,1)S(1)}, u32[]{:S(2)}, u32[]{:S(2)}) collective-permute-start(bf16[6,32,128]{2,1,0:T(8,128)(2,1)S(1)} %get-tuple-element.39), channel_id=1, source_target_pairs={{0,2},{1,3},{2,0},{3,1},{4,6},{5,7},{6,4},{7,5},{8,10},{9,11},{10,... | collective-permute-start | bytes 147464 | tf_op jit(solution)/shard_map/ppermute | solution.py:38
  61.5 3.7 %collective-permute-start.21 = (bf16[6,32,128]{2,1,0:T(8,128)(2,1)S(1)}, bf16[6,32,128]{2,1,0:T(8,128)(2,1)S(1)}, u32[]{:S(2)}, u32[]{:S(2)}) collective-permute-start(bf16[6,32,128]{2,1,0:T(8,128)(2,1)S(1)} %get-tuple-element.40), channel_id=1, source_target_pairs={{0,3},{1,2},{2,1},{3,0},{4,7},{5,6},{6,5},{7,4},{8,11},{9,10},{10,... | collective-permute-start | bytes 147464 | tf_op jit(solution)/shard_map/ppermute | solution.py:38
  (2 other events, 32.7 us)

commit v4 on v3

--- a/solution.py
+++ b/solution.py
@@ -91,42 +91,30 @@
 
 def first_kernel(order_far, inverse_far, coupling_far, given_far, *refs):
     maps, rows, inverse_near, coupling_near, given_near = refs[:5]
-    inverse, coupling, order, order_done, done, near_done = refs[5:]
-    count = inverse.shape[0]
+    inverse, coupling, order, order_done, done = refs[5:]
+    count = given_near.shape[0]
     face = coupling.shape[1] // 3
     first = pltpu.make_async_copy(order_far, order, order_done)
     first.start()
-    pairs = ((inverse_far, inverse), (coupling_far, coupling))
-
-    def fetch(kind, slot):
-        far, near = pairs[kind]
-        return pltpu.make_async_copy(far.at[slot], near.at[slot], done.at[kind, slot])
-
-    for kind in range(2):
-        for slot in range(count):
-            fetch(kind, slot).start()
     first.wait()
-    slots = [order[p] for p in range(count)]
-    later = [
-        pltpu.make_async_copy(given_far.at[slots[p]], given_near.at[p], near_done.at[0, p]) for p in range(count)
-    ]
-    for p in range(2, count):
-        later.append(
-            pltpu.make_async_copy(inverse_far.at[slots[p]], inverse_near.at[p - 2], near_done.at[1, p])
-        )
-        later.append(
-            pltpu.make_async_copy(coupling_far.at[slots[p]], coupling_near.at[p - 2], near_done.at[2, p])
-        )
-    for copy in later:
+    early = []
+    later = []
+    for p in range(count):
+        slot = order[p]
+        near = (inverse.at[p], coupling.at[p]) if p < 2 else (inverse_near.at[p - 2], coupling_near.at[p - 2])
+        copies = early if p < 2 else later
+        copies.append(pltpu.make_async_copy(inverse_far.at[slot], near[0], done.at[0, p]))
+        copies.append(pltpu.make_async_copy(coupling_far.at[slot], near[1], done.at[1, p]))
+        later.append(pltpu.make_async_copy(given_far.at[slot], given_near.at[p], done.at[2, p]))
+    for copy in early + later:
         copy.start()
-    for kind in range(2):
-        for slot in range(count):
-            fetch(kind, slot).wait()
     values = []
     for p in range(2):
-        values.append(face_rows_of(inverse, slots[p], face))
+        early[2 * p].wait()
+        early[2 * p + 1].wait()
+        values.append(face_rows_of(inverse, p, face))
         rows[p] = values[p]
-    pair_maps(maps, coupling, slots[:2], values, face)
+    pair_maps(maps, coupling, (0, 1), values, face)
     for copy in later:
         copy.wait()
 
@@ -210,15 +198,18 @@
     return by_half(high, (out - high.astype(F32)).astype(BF16)), high
 
 
-def run_chains(chosen, entries, lags, weights, gains, states, count, face):
+def run_chains(chosen, entries, lags, weights, gains, states, count, face, first):
     share = gains.shape[2]
     outs = [[] for _ in chosen]
     for p in range(count):
         for i, pos in enumerate(chosen):
             rows = entries[i].shape[0]
-            result = dot(jnp.concatenate([lags[pos, p, :rows], entries[i]], axis=1), weights[pos, p])
-            first = result[:share] + gains[pos, p].astype(F32)
-            result = first if rows == share else jnp.concatenate([first, result[share:]], axis=0)
+            if first:
+                result = dot(entries[i], weights[pos, p, 2 * face :])
+            else:
+                result = dot(jnp.concatenate([lags[pos, p, :rows], entries[i]], axis=1), weights[pos, p])
+            head = result[:share] + gains[pos, p].astype(F32)
+            result = head if rows == share else jnp.concatenate([head, result[share:]], axis=0)
             states[pos, p, :rows] = result[:, : 2 * face].astype(BF16)
             outs[i].append(result[:, 2 * face :])
         if p < count - 1:
@@ -236,23 +227,23 @@
     share = gains.shape[2]
     unpack_maps(map_refs, weights, face)
     unpack_gains(gain_refs, gains, count)
-    states[...] = jnp.zeros_like(states)
-    unit[...] = jnp.zeros_like(unit)
-    row = lax.broadcasted_iota(jnp.int32, unit.shape[2:], 0) - share
-    lane = lax.broadcasted_iota(jnp.int32, unit.shape[2:], 1)
+    states[groups] = jnp.zeros_like(states[groups])
+    row = lax.broadcasted_iota(jnp.int32, unit.shape[1:], 0) - share
+    lane = lax.broadcasted_iota(jnp.int32, unit.shape[1:], 1)
     for pos in range(half):
         hit = jnp.logical_and(lane < face, row == lane + pos * face)
-        unit[0, pos] = jnp.where(hit, 1.0, 0.0).astype(BF16)
-
-    def sweep(k, parity):
-        read_lags(me, states, lags, groups, count)
+        unit[pos] = jnp.where(hit, 1.0, 0.0).astype(BF16)
+
+    def sweep(k, parity, first=False):
+        if not first:
+            read_lags(me, states, lags, groups, count)
 
         def block(t):
             live = [2 * t + half * parity, 2 * t + 1 + half * parity]
             bare = [2 * t + half * (1 - parity), 2 * t + 1 + half * (1 - parity)]
-            entries = [unit[jnp.minimum(k, 1), pos] for pos in live]
+            entries = [unit[pos] if first else jnp.zeros_like(unit[pos]) for pos in live]
             entries += [jnp.zeros((share, 2 * face), BF16)] * 2
-            chains = run_chains(live + bare, entries, lags, weights, gains, states, count, face)
+            chains = run_chains(live + bare, entries, lags, weights, gains, states, count, face, first)
             ends = [outs[-1] for outs in chains]
             at = pl.ds(pl.multiple_of(t * 2 * face, 2 * face), 2 * face)
             full = by_half(ends[0], ends[1])
@@ -267,7 +258,9 @@
         sweep(2 * i + 1, 1)
         return carry
 
-    lax.fori_loop(0, SWEEPS // 2, both, 0)
+    sweep(0, 0, True)
+    sweep(1, 1)
+    lax.fori_loop(1, SWEEPS // 2, both, 0)
 
 
 def pick(flag, first, second):
@@ -361,7 +354,7 @@
     states, lags, inflows = refs[8 + 3 * levels + groups :]
     me = place[0]
     half = groups // 2
-    states[...] = jnp.zeros_like(states)
+    states[groups] = jnp.zeros_like(states[groups])
     flags = [(line[0] // mask) % 2 for mask in masks]
     maps = [(ahead_even[k], ahead_odd[k]) for k in range(SWEEPS)]
     given = [halves_of(third, k) for k in range(SWEEPS)]
@@ -392,45 +385,64 @@
             both = values[k][pos // half][:, tile * 2 * face : (tile + 1) * 2 * face]
             inflows[k, pos] = by_half(both if pos % 2 == 0 else turned(both), blank)
 
+    def chains(k, t, stage):
+        chosen = tuple(4 * t + i for i in range(4))
+        entries = [inflows[k, pos] for pos in chosen]
+        every = [[entry] for entry in entries]
+        for p in range(count - (stage == 2)):
+            for i, pos in enumerate(chosen):
+                left = every[i][p][:, :face]
+                right = weights[pos, p, 2 * face : 3 * face]
+                added = gains[pos, p].astype(F32)
+                if stage > 0:
+                    left = jnp.concatenate([lags[pos, p], left], axis=1)
+                    right = weights[pos, p, : 3 * face]
+                if stage == 2:
+                    right = right[:, 2 * face :]
+                    added = added[:, 2 * face :]
+                result = dot(left, right) + added
+                if stage < 2:
+                    states[pos, p] = result[:, : 2 * face].astype(BF16)
+                    result = result[:, 2 * face :]
+                every[i].append(result.astype(BF16))
+        return chosen, every
+
+    def blocks(k, stage):
+        over(groups // 4, lambda t: chains(k, t, stage), 1)
+
+    blocks(0, 0)
+
     def sweep(k, carry):
         read_lags(me, states, lags, groups, count)
-
-        def block(t):
-            chosen = tuple(4 * t + i for i in range(4))
-            run_chains(
-                chosen, [inflows[k, pos] for pos in chosen], lags, weights, gains, states, count, face
-            )
-
-        over(groups // 4, block, 1)
+        blocks(k, 1)
         return carry
 
-    lax.fori_loop(0, SWEEPS - 1, sweep, 0)
+    lax.fori_loop(1, SWEEPS - 1, sweep, 0)
     read_lags(me, states, lags, groups, count)
     for t in range(groups // 4):
-        chosen = tuple(4 * t + i for i in range(4))
-        entries = [inflows[SWEEPS - 1, pos] for pos in chosen]
-        outs = run_chains(chosen, entries, lags, weights, gains, states, count, face)
+        chosen, every = chains(SWEEPS - 1, t, 2)
         for i, pos in enumerate(chosen):
             target = wanted[reversed_static(pos, groups)]
-            traces = [entries[i]] + [o.astype(BF16) for o in outs[i][:-1]]
+            traces = every[i]
             for p in range(count):
                 target[p] = lags[pos, p]
-            target[count] = by_half(traces[0], traces[-1])
+            target[count] = by_half(traces[0], traces[count - 1])
             for m in range(1, count // 2):
                 target[count + m] = by_half(traces[2 * m - 1], traces[2 * m])
 
 
 def final_kernel(place, order, inverse, coupling, given, *refs):
-    wanted = refs[:-2]
-    placed, gathered = refs[-2:]
+    wanted = refs[:-4]
+    placed, solved, gathered, done = refs[-4:]
     count, nodes, width = given.shape
     face = coupling.shape[1] // 3
     share = width // len(wanted)
     for rel, ref in enumerate(wanted):
         at = pl.multiple_of((place[0] ^ rel) * share, share)
         for m in range(ref.shape[0]):
-            gathered[m, pl.ds(at, share), :] = ref[m].astype(F32)
+            gathered[m, pl.ds(at, share), :] = ref[m].astype(gathered.dtype)
     blank = jnp.zeros((face, nodes), BF16)
+    copies = []
     for p in range(count):
         slot = order[p]
         rows = coupling[slot]
@@ -440,7 +452,11 @@
         sides = jnp.concatenate([rows[2 * face :], rows[face : 2 * face]] + pair, axis=0)
         traces = jnp.concatenate([gathered[p], gathered[count + tile]], axis=1).astype(BF16)
         source = given[slot].astype(F32) + dot(traces, sides).T
-        placed[slot] = dot(inverse[slot], source.astype(BF16)).astype(BF16)
+        solved[p] = dot(inverse[slot], source.astype(BF16)).astype(BF16)
+        copies.append(pltpu.make_async_copy(solved.at[p], placed.at[slot], done.at[p]))
+        copies[p].start()
+    for copy in copies:
+        copy.wait()
 
 
 def gather_list(value, axis):
@@ -454,7 +470,7 @@
     return [v if rel == 0 else swap(v, axis, rel) for rel, v in enumerate(values)]
 
 
-def call(kernel, outs, scratch, scalars, arrays, far=0, others=(), grant=0):
+def call(kernel, outs, scratch, scalars, arrays, far=0, others=(), space=VMEM):
     def size(shape, kind):
         total = jnp.dtype(kind).itemsize
         for extent in shape:
@@ -467,9 +483,9 @@
         kernel,
         out_shape=outs,
         in_specs=[SMEM] * len(scalars) + [VMEM] * (len(arrays) - far) + [HBM] * far,
-        out_specs=[VMEM] * len(outs),
+        out_specs=[space] * len(outs),
         scratch_shapes=[*[pltpu.VMEM(shape, kind) for shape, kind in scratch], *others],
-        compiler_params=pltpu.CompilerParams(vmem_limit_bytes=grant or min(held + (3 << 20), 60 << 20)),
+        compiler_params=pltpu.CompilerParams(vmem_limit_bytes=min(held + (3 << 20), 60 << 20)),
     )(*scalars, *arrays)
 
 
@@ -498,14 +514,13 @@
             shape((count - 2,) + coupling.shape[1:], BF16),
             shape(given.shape, BF16),
         ],
-        [(inverse.shape, BF16), (coupling.shape, BF16)],
+        [((2,) + inverse.shape[1:], BF16), ((2,) + coupling.shape[1:], BF16)],
         [],
         far,
         4,
         (
             pltpu.SMEM(order.shape, order.dtype),
             pltpu.SemaphoreType.DMA,
-            pltpu.SemaphoreType.DMA((2, count)),
             pltpu.SemaphoreType.DMA((3, count)),
         ),
     )
@@ -534,7 +549,7 @@
         [
             ((groups + 1, count, share + wide, 2 * face), BF16),
             ((groups, count, share + wide, 2 * face), BF16),
-            ((2, groups, share + wide, 2 * face), BF16),
+            ((half, share + wide, 2 * face), BF16),
         ],
         [place],
         [*all_maps, *gains],
@@ -580,9 +595,12 @@
     (placed,) = call(
         final_kernel,
         [shape((count, nodes, width), BF16)],
-        [((tiles, width, 2 * face), F32)],
+        [((count, nodes, width), BF16), ((tiles, width, 2 * face), BF16 if share % 16 == 0 else F32)],
         [place, order],
         [inverse, coupling, given, *wanted],
+        0,
+        (pltpu.SemaphoreType.DMA((count,)),),
+        HBM,
     )
     return placed[None, None]
 

time: 68 us -> 67 us (0.985)
  Pallas kernels: 15.5 us -> 14.4 us
    pallas_call x8, Pallas kernels: 15.5 us -> 14.4 us  [call(): pl.pallas_call(kernel, out_shape=outs, in_specs=[SMEM] * len(scalars) + [...]
where the time goes in v4:
time: 67 us; the launch traced here: 66.8 us
  waiting for transfers between devices  32.3 us (48%)
  starting transfers between devices  20 us (30%)
  Pallas kernels  14.4 us (21%)
    ppermute x21, waiting for transfers between devices, swap(): return lax.ppermute(value, axis, [(i, i ^ mask) for i in range(count)])  32 us
    ppermute x21, starting transfers between devices, swap(): return lax.ppermute(value, axis, [(i, i ^ mask) for i in range(count)])  19.5 us
    pallas_call x8, Pallas kernels, call(): pl.pallas_call(kernel, out_shape=outs, in_specs=[SMEM] * len(scalars) + [...  14.4 us
  transfers between devices with their start and end apart: 22, of which 13 were waited for; matrix products, arithmetic and copies ran while one was open for 0% of the time, Pallas kernels for 1%

profile of v4, /device:TPU:0, one launch (start us, length us, event | category | flops | bytes accessed | tf_op | source)
XLA Modules:
  0.0 66.8 jit_solution(17039777262714670239)
XLA Ops:
  0.0 2.7 %shard_map.46 = (bf16[576,128]{1,0:T(8,128)(2,1)S(1)}, bf16[2,256,512]{2,1,0:T(8,128)(2,1)S(1)}, bf16[2,512,512]{2,1,0:T(8,128)(2,1)S(1)}, bf16[2,192,512]{2,1,0:T(8,128)(2,1)S(1)}, bf16[4,512,128]{2,1,0:T(8,128)(2,1)S(1)}) custom-call(s32[4]{0:T(128)} %bitcast.13, bf16[4,512,512]{2,1,0:T(8,128)(2,1)} %bitcast.7, bf16[4,192,512]{2,1,0:T(8,128)(2,1)} %bitcast.9, ...), custom_call_target="tpu_custom_call" | custom-call | tf_op jit(solution)/shard_map/pallas_call | solution.py:482
  3.4 3.0 %collective-permute-start.3 = (bf16[576,128]{1,0:T(8,128)(2,1)S(1)}, bf16[576,128]{1,0:T(8,128)(2,1)S(1)}, u32[]{:S(2)}, u32[]{:S(2)}) collective-permute-start(bf16[576,128]{1,0:T(8,128)(2,1)S(1)} %get-tuple-element.28.refs_4_), channel_id=1, source_target_pairs={{0,2},{1,3},{2,0},{3,1},{4,6},{5,7},{6,4},{7,5},{8,10},{9,11},{10,... | collective-permute-start | bytes 442376 | tf_op jit(solution)/shard_map/ppermute | solution.py:38
  7.0 4.1 %collective-permute-done.3.refs_5_ = bf16[576,128]{1,0:T(8,128)(2,1)S(1)} collective-permute-done((bf16[576,128]{1,0:T(8,128)(2,1)S(1)}, bf16[576,128]{1,0:T(8,128)(2,1)S(1)}, u32[]{:S(2)}, u32[]{:S(2)}) %collective-permute-start.3) | collective-permute-done | bytes 147488 | tf_op jit(solution)/shard_map/ppermute | solution.py:38
  11.1 2.3 %collective-permute-done.refs_1_ = bf16[576,128]{1,0:T(8,128)(2,1)S(1)} collective-permute-done((bf16[576,128]{1,0:T(8,128)(2,1)S(1)}, bf16[576,128]{1,0:T(8,128)(2,1)S(1)}, u32[]{:S(2)}, u32[]{:S(2)}) %collective-permute-start) | collective-permute-done | bytes 147488 | tf_op jit(solution)/shard_map/ppermute | solution.py:38
  13.4 1.7 %collective-permute-start.7 = (bf16[6,32,128]{2,1,0:T(8,128)(2,1)S(1)}, bf16[6,32,128]{2,1,0:T(8,128)(2,1)S(1)}, u32[]{:S(2)}, u32[]{:S(2)}) collective-permute-start(bf16[6,32,128]{2,1,0:T(8,128)(2,1)S(1)} %get-tuple-element.31), channel_id=1, source_target_pairs={{0,2},{1,3},{2,0},{3,1},{4,6},{5,7},{6,4},{7,5},{8,10},{9,11},{10,... | collective-permute-start | bytes 147464 | tf_op jit(solution)/shard_map/ppermute | solution.py:38
  15.2 2.4 %collective-permute-done.7.refs_10_ = bf16[6,32,128]{2,1,0:T(8,128)(2,1)S(1)} collective-permute-done((bf16[6,32,128]{2,1,0:T(8,128)(2,1)S(1)}, bf16[6,32,128]{2,1,0:T(8,128)(2,1)S(1)}, u32[]{:S(2)}, u32[]{:S(2)}) %collective-permute-start.7) | collective-permute-done | bytes 49184 | tf_op jit(solution)/shard_map/ppermute | solution.py:38
  18.6 2.8 %collective-permute-done.8.refs_11_ = bf16[6,32,128]{2,1,0:T(8,128)(2,1)S(1)} collective-permute-done((bf16[6,32,128]{2,1,0:T(8,128)(2,1)S(1)}, bf16[6,32,128]{2,1,0:T(8,128)(2,1)S(1)}, u32[]{:S(2)}, u32[]{:S(2)}) %collective-permute-start.8) | collective-permute-done | bytes 49184 | tf_op jit(solution)/shard_map/ppermute | solution.py:38
  21.4 3.8 %shard_map.48 = (bf16[6,128,128]{2,1,0:T(8,128)(2,1)S(1)}, bf16[6,64,128]{2,1,0:T(8,128)(2,1)S(1)}, bf16[4,4,256,256]{3,2,1,0:T(8,128)(2,1)S(1)}, bf16[4,4,32,256]{3,2,1,0:T(8,128)(2,1)S(1)}) custom-call(s32[1]{0:T(128)} %bitcast.place, bf16[576,128]{1,0:T(8,128)(2,1)S(1)} %get-tuple-element.23.refs_0_, bf16[576,128]{1,0:T(8,128)(2,1)S(1)} %collective-permute-done.refs_1_, ...), custom_call_target="tpu_custom_call" | custom-call | tf_op jit(solution)/shard_map/pallas_call | solution.py:482
  25.1 2.1 %collective-permute-start.13 = (bf16[6,128,128]{2,1,0:T(8,128)(2,1)S(1)}, bf16[6,128,128]{2,1,0:T(8,128)(2,1)S(1)}, u32[]{:S(2)}, u32[]{:S(2)}) collective-permute-start(bf16[6,128,128]{2,1,0:T(8,128)(2,1)S(1)} %get-tuple-element.35.even.own), channel_id=1, source_target_pairs={{0,4},{4,0},{8,12},{12,8},{16,20},{20,16},{24,28},{28,24},{1,5},{5... | collective-permute-start | bytes 589832 | tf_op jit(solution)/shard_map/ppermute | solution.py:38
  27.2 5.2 %collective-permute-done.13.got.refs_8_ = bf16[6,128,128]{2,1,0:T(8,128)(2,1)S(1)} collective-permute-done((bf16[6,128,128]{2,1,0:T(8,128)(2,1)S(1)}, bf16[6,128,128]{2,1,0:T(8,128)(2,1)S(1)}, u32[]{:S(2)}, u32[]{:S(2)}) %collective-permute-start.13) | collective-permute-done | bytes 196640 | tf_op jit(solution)/shard_map/ppermute | solution.py:38
  32.4 1.4 %collective-permute-done.14.got_other.refs_9_ = bf16[6,128,128]{2,1,0:T(8,128)(2,1)S(1)} collective-permute-done((bf16[6,128,128]{2,1,0:T(8,128)(2,1)S(1)}, bf16[6,128,128]{2,1,0:T(8,128)(2,1)S(1)}, u32[]{:S(2)}, u32[]{:S(2)}) %collective-permute-start.14) | collective-permute-done | bytes 196640 | tf_op jit(solution)/shard_map/ppermute | solution.py:38
  34.2 1.9 %collective-permute-start.17 = (bf16[6,128,128]{2,1,0:T(8,128)(2,1)S(1)}, bf16[6,128,128]{2,1,0:T(8,128)(2,1)S(1)}, u32[]{:S(2)}, u32[]{:S(2)}) collective-permute-start(bf16[6,128,128]{2,1,0:T(8,128)(2,1)S(1)} %shard_map.51), channel_id=1, source_target_pairs={{0,8},{4,12},{8,0},{12,4},{16,24},{20,28},{24,16},{28,20},{1,9},{5... | collective-permute-start | bytes 589832 | tf_op jit(solution)/shard_map/ppermute | solution.py:38
  36.0 1.5 %collective-permute-start.10 = (bf16[6,64,128]{2,1,0:T(8,128)(2,1)S(1)}, bf16[6,64,128]{2,1,0:T(8,128)(2,1)S(1)}, u32[]{:S(2)}, u32[]{:S(2)}) collective-permute-start(bf16[6,64,128]{2,1,0:T(8,128)(2,1)S(1)} %get-tuple-element.36.own.own_offset), channel_id=1, source_target_pairs={{0,4},{4,0},{8,12},{12,8},{16,20},{20,16},{24,28},{28,24},{1,5},{5... | collective-permute-start | bytes 294920 | tf_op jit(solution)/shard_map/ppermute | solution.py:38
  37.6 3.1 %collective-permute-done.10.entry.got_offset.refs_10_ = bf16[6,64,128]{2,1,0:T(8,128)(2,1)S(1)} collective-permute-done((bf16[6,64,128]{2,1,0:T(8,128)(2,1)S(1)}, bf16[6,64,128]{2,1,0:T(8,128)(2,1)S(1)}, u32[]{:S(2)}, u32[]{:S(2)}) %collective-permute-start.10) | collective-permute-done | bytes 98336 | tf_op jit(solution)/shard_map/ppermute | solution.py:38
  41.0 1.5 %collective-permute-start.12 = (bf16[6,64,128]{2,1,0:T(8,128)(2,1)S(1)}, bf16[6,64,128]{2,1,0:T(8,128)(2,1)S(1)}, u32[]{:S(2)}, u32[]{:S(2)}) collective-permute-start(bf16[6,64,128]{2,1,0:T(8,128)(2,1)S(1)} %shard_map.49), channel_id=1, source_target_pairs={{0,12},{4,8},{8,4},{12,0},{16,28},{20,24},{24,20},{28,16},{1,13},{... | collective-permute-start | bytes 294920 | tf_op jit(solution)/shard_map/ppermute | solution.py:38
  42.4 1.6 %collective-permute-start.11 = (bf16[6,64,128]{2,1,0:T(8,128)(2,1)S(1)}, bf16[6,64,128]{2,1,0:T(8,128)(2,1)S(1)}, u32[]{:S(2)}, u32[]{:S(2)}) collective-permute-start(bf16[6,64,128]{2,1,0:T(8,128)(2,1)S(1)} %shard_map.49), channel_id=1, source_target_pairs={{0,8},{4,12},{8,0},{12,4},{16,24},{20,28},{24,16},{28,20},{1,9},{5... | collective-permute-start | bytes 294920 | tf_op jit(solution)/shard_map/ppermute | solution.py:38
  44.0 2.7 %collective-permute-done.12.across.refs_3_ = bf16[6,64,128]{2,1,0:T(8,128)(2,1)S(1)} collective-permute-done((bf16[6,64,128]{2,1,0:T(8,128)(2,1)S(1)}, bf16[6,64,128]{2,1,0:T(8,128)(2,1)S(1)}, u32[]{:S(2)}, u32[]{:S(2)}) %collective-permute-start.12) | collective-permute-done | bytes 98336 | tf_op jit(solution)/shard_map/ppermute | solution.py:38
  46.7 1.1 %collective-permute-done.11.near.refs_2_ = bf16[6,64,128]{2,1,0:T(8,128)(2,1)S(1)} collective-permute-done((bf16[6,64,128]{2,1,0:T(8,128)(2,1)S(1)}, bf16[6,64,128]{2,1,0:T(8,128)(2,1)S(1)}, u32[]{:S(2)}, u32[]{:S(2)}) %collective-permute-start.11) | collective-permute-done | bytes 98336 | tf_op jit(solution)/shard_map/ppermute | solution.py:38
  48.4 2.7 %collective-permute-start.16 = (bf16[6,64,128]{2,1,0:T(8,128)(2,1)S(1)}, bf16[6,64,128]{2,1,0:T(8,128)(2,1)S(1)}, u32[]{:S(2)}, u32[]{:S(2)}) collective-permute-start(bf16[6,64,128]{2,1,0:T(8,128)(2,1)S(1)} %shard_map.50), channel_id=1, source_target_pairs={{0,16},{4,20},{8,24},{12,28},{16,0},{20,4},{24,8},{28,12},{1,17},{... | collective-permute-start | bytes 294920 | tf_op jit(solution)/shard_map/ppermute | solution.py:38
  51.6 3.8 %collective-permute-done.16.refs_5_ = bf16[6,64,128]{2,1,0:T(8,128)(2,1)S(1)} collective-permute-done((bf16[6,64,128]{2,1,0:T(8,128)(2,1)S(1)}, bf16[6,64,128]{2,1,0:T(8,128)(2,1)S(1)}, u32[]{:S(2)}, u32[]{:S(2)}) %collective-permute-start.16) | collective-permute-done | bytes 98336 | tf_op jit(solution)/shard_map/ppermute | solution.py:38
  55.7 3.5 %shard_map.52 = (bf16[6,32,128]{2,1,0:T(8,128)(2,1)S(1)}, bf16[6,32,128]{2,1,0:T(8,128)(2,1)S(1)}, bf16[6,32,128]{2,1,0:T(8,128)(2,1)S(1)}, bf16[6,32,128]{2,1,0:T(8,128)(2,1)S(1)}) custom-call(s32[1]{0:T(128)} %bitcast.place, s32[1]{0:T(128)} %bitcast.5.line, bf16[4,4,256,256]{3,2,1,0:T(8,128)(2,1)S(1)} %get-tuple-element.33.refs_0_, ...), custom_call_target="tpu_custom_call" | custom-call | tf_op jit(solution)/shard_map/pallas_call | solution.py:482
  59.3 1.2 %collective-permute-start.20 = (bf16[6,32,128]{2,1,0:T(8,128)(2,1)S(1)}, bf16[6,32,128]{2,1,0:T(8,128)(2,1)S(1)}, u32[]{:S(2)}, u32[]{:S(2)}) collective-permute-start(bf16[6,32,128]{2,1,0:T(8,128)(2,1)S(1)} %get-tuple-element.39), channel_id=1, source_target_pairs={{0,2},{1,3},{2,0},{3,1},{4,6},{5,7},{6,4},{7,5},{8,10},{9,11},{10,... | collective-permute-start | bytes 147464 | tf_op jit(solution)/shard_map/ppermute | solution.py:38
  61.2 2.3 %collective-permute-done.20.refs_2_ = bf16[6,32,128]{2,1,0:T(8,128)(2,1)S(1)} collective-permute-done((bf16[6,32,128]{2,1,0:T(8,128)(2,1)S(1)}, bf16[6,32,128]{2,1,0:T(8,128)(2,1)S(1)}, u32[]{:S(2)}, u32[]{:S(2)}) %collective-permute-start.20) | collective-permute-done | bytes 49184 | tf_op jit(solution)/shard_map/ppermute | solution.py:38
  64.3 2.5 %shard_map.53 = bf16[4,512,128]{2,1,0:T(8,128)(2,1)} custom-call(s32[1]{0:T(128)} %bitcast.place, s32[4]{0:T(128)S(1)} %bitcast.14, bf16[4,512,512]{2,1,0:T(8,128)(2,1)S(1)} %bitcast.8, bf16[4,192,512]{2,1,0:T(8,128)(2,1)S(1)} %bitcast.10, bf16[4,512,128]{2,1,0:T(8,128)(2,1)S(1)} %bitcast.12, bf16[6,32,128]{2,1,0:T(8,128)(2,1)S(1)} %get-tuple-element.37.refs_0_, ...), custom_call_target="tpu_custom_call" | custom-call | tf_op jit(solution)/shard_map/pallas_call | solution.py:482
  (36 shorter events, 5.8 us)
Async XLA Ops:
  3.4 7.7 %collective-permute-start.3 = (bf16[576,128]{1,0:T(8,128)(2,1)S(1)}, bf16[576,128]{1,0:T(8,128)(2,1)S(1)}, u32[]{:S(2)}, u32[]{:S(2)}) collective-permute-start(bf16[576,128]{1,0:T(8,128)(2,1)S(1)} %get-tuple-element.28.refs_4_), channel_id=1, source_target_pairs={{0,2},{1,3},{2,0},{3,1},{4,6},{5,7},{6,4},{7,5},{8,10},{9,11},{10,... | collective-permute-start | bytes 442376 | tf_op jit(solution)/shard_map/ppermute | solution.py:38
  6.4 7.0 %collective-permute-start = (bf16[576,128]{1,0:T(8,128)(2,1)S(1)}, bf16[576,128]{1,0:T(8,128)(2,1)S(1)}, u32[]{:S(2)}, u32[]{:S(2)}) collective-permute-start(bf16[576,128]{1,0:T(8,128)(2,1)S(1)} %get-tuple-element.23.refs_0_), channel_id=1, source_target_pairs={{0,2},{1,3},{2,0},{3,1},{4,6},{5,7},{6,4},{7,5},{8,10},{9,11},{10,... | collective-permute-start | bytes 442376 | tf_op jit(solution)/shard_map/ppermute | solution.py:38
  6.5 6.9 %collective-permute-start.6 = (bf16[6,32,128]{2,1,0:T(8,128)(2,1)S(1)}, bf16[6,32,128]{2,1,0:T(8,128)(2,1)S(1)}, u32[]{:S(2)}, u32[]{:S(2)}) collective-permute-start(bf16[6,32,128]{2,1,0:T(8,128)(2,1)S(1)} %get-tuple-element.30), channel_id=1, source_target_pairs={{0,1},{1,0},{2,3},{3,2},{4,5},{5,4},{6,7},{7,6},{8,9},{9,8},{10,11... | collective-permute-start | bytes 147464 | tf_op jit(solution)/shard_map/ppermute | solution.py:38
  6.5 14.8 %collective-permute-start.4 = (bf16[576,128]{1,0:T(8,128)(2,1)S(1)}, bf16[576,128]{1,0:T(8,128)(2,1)S(1)}, u32[]{:S(2)}, u32[]{:S(2)}) collective-permute-start(bf16[576,128]{1,0:T(8,128)(2,1)S(1)} %get-tuple-element.28.refs_4_), channel_id=1, source_target_pairs={{0,1},{1,0},{2,3},{3,2},{4,5},{5,4},{6,7},{7,6},{8,9},{9,8},{10,11... | collective-permute-start | bytes 442376 | tf_op jit(solution)/shard_map/ppermute | solution.py:38
  7.0 14.3 %collective-permute-start.1 = (bf16[576,128]{1,0:T(8,128)(2,1)S(1)}, bf16[576,128]{1,0:T(8,128)(2,1)S(1)}, u32[]{:S(2)}, u32[]{:S(2)}) collective-permute-start(bf16[576,128]{1,0:T(8,128)(2,1)S(1)} %get-tuple-element.23.refs_0_), channel_id=1, source_target_pairs={{0,1},{1,0},{2,3},{3,2},{4,5},{5,4},{6,7},{7,6},{8,9},{9,8},{10,11... | collective-permute-start | bytes 442376 | tf_op jit(solution)/shard_map/ppermute | solution.py:38
  11.1 10.2 %collective-permute-start.5 = (bf16[576,128]{1,0:T(8,128)(2,1)S(1)}, bf16[576,128]{1,0:T(8,128)(2,1)S(1)}, u32[]{:S(2)}, u32[]{:S(2)}) collective-permute-start(bf16[576,128]{1,0:T(8,128)(2,1)S(1)} %collective-permute-done.3.refs_5_), channel_id=1, source_target_pairs={{0,1},{1,0},{2,3},{3,2},{4,5},{5,4},{6,7},{7,6},{8,9},{9,8},{10,11... | collective-permute-start | bytes 442376 | tf_op jit(solution)/shard_map/ppermute | solution.py:38
  13.4 7.9 %collective-permute-start.2 = (bf16[576,128]{1,0:T(8,128)(2,1)S(1)}, bf16[576,128]{1,0:T(8,128)(2,1)S(1)}, u32[]{:S(2)}, u32[]{:S(2)}) collective-permute-start(bf16[576,128]{1,0:T(8,128)(2,1)S(1)} %collective-permute-done.refs_1_), channel_id=1, source_target_pairs={{0,1},{1,0},{2,3},{3,2},{4,5},{5,4},{6,7},{7,6},{8,9},{9,8},{10,11... | collective-permute-start | bytes 442376 | tf_op jit(solution)/shard_map/ppermute | solution.py:38
  13.4 4.2 %collective-permute-start.7 = (bf16[6,32,128]{2,1,0:T(8,128)(2,1)S(1)}, bf16[6,32,128]{2,1,0:T(8,128)(2,1)S(1)}, u32[]{:S(2)}, u32[]{:S(2)}) collective-permute-start(bf16[6,32,128]{2,1,0:T(8,128)(2,1)S(1)} %get-tuple-element.31), channel_id=1, source_target_pairs={{0,2},{1,3},{2,0},{3,1},{4,6},{5,7},{6,4},{7,5},{8,10},{9,11},{10,... | collective-permute-start | bytes 147464 | tf_op jit(solution)/shard_map/ppermute | solution.py:38
  17.6 3.7 %collective-permute-start.8 = (bf16[6,32,128]{2,1,0:T(8,128)(2,1)S(1)}, bf16[6,32,128]{2,1,0:T(8,128)(2,1)S(1)}, u32[]{:S(2)}, u32[]{:S(2)}) collective-permute-start(bf16[6,32,128]{2,1,0:T(8,128)(2,1)S(1)} %get-tuple-element.32), channel_id=1, source_target_pairs={{0,3},{1,2},{2,1},{3,0},{4,7},{5,6},{6,5},{7,4},{8,11},{9,10},{10,... | collective-permute-start | bytes 147464 | tf_op jit(solution)/shard_map/ppermute | solution.py:38
  25.1 7.2 %collective-permute-start.13 = (bf16[6,128,128]{2,1,0:T(8,128)(2,1)S(1)}, bf16[6,128,128]{2,1,0:T(8,128)(2,1)S(1)}, u32[]{:S(2)}, u32[]{:S(2)}) collective-permute-start(bf16[6,128,128]{2,1,0:T(8,128)(2,1)S(1)} %get-tuple-element.35.even.own), channel_id=1, source_target_pairs={{0,4},{4,0},{8,12},{12,8},{16,20},{20,16},{24,28},{28,24},{1,5},{5... | collective-permute-start | bytes 589832 | tf_op jit(solution)/shard_map/ppermute | solution.py:38
  27.2 5.2 %collective-permute-start.9 = (bf16[6,128,128]{2,1,0:T(8,128)(2,1)S(1)}, bf16[6,128,128]{2,1,0:T(8,128)(2,1)S(1)}, u32[]{:S(2)}, u32[]{:S(2)}) collective-permute-start(bf16[6,128,128]{2,1,0:T(8,128)(2,1)S(1)} %get-tuple-element.35.even.own), channel_id=1, source_target_pairs={{0,1},{1,0},{2,3},{3,2},{4,5},{5,4},{6,7},{7,6},{8,9},{9,8},{10,11... | collective-permute-start | bytes 589832 | tf_op jit(solution)/shard_map/ppermute | solution.py:38
  32.4 1.4 %collective-permute-start.14 = (bf16[6,128,128]{2,1,0:T(8,128)(2,1)S(1)}, bf16[6,128,128]{2,1,0:T(8,128)(2,1)S(1)}, u32[]{:S(2)}, u32[]{:S(2)}) collective-permute-start(bf16[6,128,128]{2,1,0:T(8,128)(2,1)S(1)} %collective-permute-done.13.got.refs_8_), channel_id=1, source_target_pairs={{0,1},{1,0},{2,3},{3,2},{4,5},{5,4},{6,7},{7,6},{8,9},{9,8},{10,11... | collective-permute-start | bytes 589832 | tf_op jit(solution)/shard_map/ppermute | solution.py:38
  34.2 9.9 %collective-permute-start.17 = (bf16[6,128,128]{2,1,0:T(8,128)(2,1)S(1)}, bf16[6,128,128]{2,1,0:T(8,128)(2,1)S(1)}, u32[]{:S(2)}, u32[]{:S(2)}) collective-permute-start(bf16[6,128,128]{2,1,0:T(8,128)(2,1)S(1)} %shard_map.51), channel_id=1, source_target_pairs={{0,8},{4,12},{8,0},{12,4},{16,24},{20,28},{24,16},{28,20},{1,9},{5... | collective-permute-start | bytes 589832 | tf_op jit(solution)/shard_map/ppermute | solution.py:38
  36.0 4.6 %collective-permute-start.10 = (bf16[6,64,128]{2,1,0:T(8,128)(2,1)S(1)}, bf16[6,64,128]{2,1,0:T(8,128)(2,1)S(1)}, u32[]{:S(2)}, u32[]{:S(2)}) collective-permute-start(bf16[6,64,128]{2,1,0:T(8,128)(2,1)S(1)} %get-tuple-element.36.own.own_offset), channel_id=1, source_target_pairs={{0,4},{4,0},{8,12},{12,8},{16,20},{20,16},{24,28},{28,24},{1,5},{5... | collective-permute-start | bytes 294920 | tf_op jit(solution)/shard_map/ppermute | solution.py:38
  41.0 5.7 %collective-permute-start.12 = (bf16[6,64,128]{2,1,0:T(8,128)(2,1)S(1)}, bf16[6,64,128]{2,1,0:T(8,128)(2,1)S(1)}, u32[]{:S(2)}, u32[]{:S(2)}) collective-permute-start(bf16[6,64,128]{2,1,0:T(8,128)(2,1)S(1)} %shard_map.49), channel_id=1, source_target_pairs={{0,12},{4,8},{8,4},{12,0},{16,28},{20,24},{24,20},{28,16},{1,13},{... | collective-permute-start | bytes 294920 | tf_op jit(solution)/shard_map/ppermute | solution.py:38
  42.4 5.4 %collective-permute-start.11 = (bf16[6,64,128]{2,1,0:T(8,128)(2,1)S(1)}, bf16[6,64,128]{2,1,0:T(8,128)(2,1)S(1)}, u32[]{:S(2)}, u32[]{:S(2)}) collective-permute-start(bf16[6,64,128]{2,1,0:T(8,128)(2,1)S(1)} %shard_map.49), channel_id=1, source_target_pairs={{0,8},{4,12},{8,0},{12,4},{16,24},{20,28},{24,16},{28,20},{1,9},{5... | collective-permute-start | bytes 294920 | tf_op jit(solution)/shard_map/ppermute | solution.py:38
  44.0 11.7 %collective-permute-start.18 = (bf16[6,128,128]{2,1,0:T(8,128)(2,1)S(1)}, bf16[6,128,128]{2,1,0:T(8,128)(2,1)S(1)}, u32[]{:S(2)}, u32[]{:S(2)}) collective-permute-start(bf16[6,128,128]{2,1,0:T(8,128)(2,1)S(1)} %collective-permute-done.17.refs_6_), channel_id=1, source_target_pairs={{0,1},{1,0},{2,3},{3,2},{4,5},{5,4},{6,7},{7,6},{8,9},{9,8},{10,11... | collective-permute-start | bytes 589832 | tf_op jit(solution)/shard_map/ppermute | solution.py:38
  48.4 15.9 %copy-start = (bf16[1,1,4,512,512]{4,3,2,1,0:T(8,128)(2,1)S(1)}, bf16[1,1,4,512,512]{4,3,2,1,0:T(8,128)(2,1)}, u32[]{:S(2)}) copy-start(bf16[1,1,4,512,512]{4,3,2,1,0:T(8,128)(2,1)} %param.5) | copy-start | bytes 6291460
  48.4 15.9 %copy-start.1 = (bf16[1,1,4,3,64,512]{5,4,3,2,1,0:T(8,128)(2,1)S(1)}, bf16[1,1,4,3,64,512]{5,4,3,2,1,0:T(8,128)(2,1)}, u32[]{:S(2)}) copy-start(bf16[1,1,4,3,64,512]{5,4,3,2,1,0:T(8,128)(2,1)} %param.6) | copy-start | bytes 2359300
  48.4 7.0 %collective-permute-start.16 = (bf16[6,64,128]{2,1,0:T(8,128)(2,1)S(1)}, bf16[6,64,128]{2,1,0:T(8,128)(2,1)S(1)}, u32[]{:S(2)}, u32[]{:S(2)}) collective-permute-start(bf16[6,64,128]{2,1,0:T(8,128)(2,1)S(1)} %shard_map.50), channel_id=1, source_target_pairs={{0,16},{4,20},{8,24},{12,28},{16,0},{20,4},{24,8},{28,12},{1,17},{... | collective-permute-start | bytes 294920 | tf_op jit(solution)/shard_map/ppermute | solution.py:38
  51.1 4.6 %collective-permute-start.15 = (bf16[6,64,128]{2,1,0:T(8,128)(2,1)S(1)}, bf16[6,64,128]{2,1,0:T(8,128)(2,1)S(1)}, u32[]{:S(2)}, u32[]{:S(2)}) collective-permute-start(bf16[6,64,128]{2,1,0:T(8,128)(2,1)S(1)} %shard_map.50), channel_id=1, source_target_pairs={{0,4},{4,0},{8,16},{12,20},{16,8},{20,12},{24,28},{28,24},{1,5},{5... | collective-permute-start | bytes 294920 | tf_op jit(solution)/shard_map/ppermute | solution.py:580
  59.2 1.9 %collective-permute-start.19 = (bf16[6,32,128]{2,1,0:T(8,128)(2,1)S(1)}, bf16[6,32,128]{2,1,0:T(8,128)(2,1)S(1)}, u32[]{:S(2)}, u32[]{:S(2)}) collective-permute-start(bf16[6,32,128]{2,1,0:T(8,128)(2,1)S(1)} %get-tuple-element.38), channel_id=1, source_target_pairs={{0,1},{1,0},{2,3},{3,2},{4,5},{5,4},{6,7},{7,6},{8,9},{9,8},{10,11... | collective-permute-start | bytes 147464 | tf_op jit(solution)/shard_map/ppermute | solution.py:38
  59.3 4.2 %collective-permute-start.20 = (bf16[6,32,128]{2,1,0:T(8,128)(2,1)S(1)}, bf16[6,32,128]{2,1,0:T(8,128)(2,1)S(1)}, u32[]{:S(2)}, u32[]{:S(2)}) collective-permute-start(bf16[6,32,128]{2,1,0:T(8,128)(2,1)S(1)} %get-tuple-element.39), channel_id=1, source_target_pairs={{0,2},{1,3},{2,0},{3,1},{4,6},{5,7},{6,4},{7,5},{8,10},{9,11},{10,... | collective-permute-start | bytes 147464 | tf_op jit(solution)/shard_map/ppermute | solution.py:38
  60.6 3.7 %collective-permute-start.21 = (bf16[6,32,128]{2,1,0:T(8,128)(2,1)S(1)}, bf16[6,32,128]{2,1,0:T(8,128)(2,1)S(1)}, u32[]{:S(2)}, u32[]{:S(2)}) collective-permute-start(bf16[6,32,128]{2,1,0:T(8,128)(2,1)S(1)} %get-tuple-element.40), channel_id=1, source_target_pairs={{0,3},{1,2},{2,1},{3,0},{4,7},{5,6},{6,5},{7,4},{8,11},{9,10},{10,... | collective-permute-start | bytes 147464 | tf_op jit(solution)/shard_map/ppermute | solution.py:38
  (2 other events, 31.7 us)

commit v5 on v4

--- a/solution.py
+++ b/solution.py
@@ -38,11 +38,12 @@
     return lax.ppermute(value, axis, [(i, i ^ mask) for i in range(count)])
 
 
-def crossing(masks):
+def crossing(masks, first, second):
     pairs = []
     for i in range(2 * masks[-1]):
-        inner = bool(i & masks[-1]) != bool(i & masks[-2])
-        pairs.append((i, i ^ (masks[-1] | masks[-2] if inner else 1)))
+        quarter = i // masks[-2]
+        inner = quarter in (first, second)
+        pairs.append((i, i ^ ((first ^ second) * masks[-2] if inner else 1)))
     return pairs
 
 
@@ -577,8 +578,8 @@
         )
     ahead_even = swap(response, "stream", masks[-2])
     (joined,) = call(functools.partial(join_kernel, mask=masks[-3]), [same], [], [line], joining)
-    second = lax.ppermute(joined, "stream", crossing(masks))
-    third = swap(joined, "stream", masks[-1])
+    second = lax.ppermute(joined, "stream", crossing(masks, 1, 2))
+    third = lax.ppermute(joined, "stream", crossing(masks, 1, 3))
     ahead_odd = swap(ahead_even, "span", 1)
     wanted = call(
         functools.partial(resolve_kernel, masks=masks, **sizes),

time: 67 us -> 65.4 us (0.976)
  starting transfers between devices: 20 us -> 18.9 us
    ppermute x21 -> x20, waiting for transfers between devices: 32 us -> 28.2 us  [swap(): return lax.ppermute(value, axis, [(i, i ^ mask) for i in range(count)])]
    ppermute x1 -> x2, waiting for transfers between devices: 0.31 us -> 3.64 us  [the longest x1 2.59 us: shards(): third = lax.ppermute(joined, 'stream', crossing(masks, 1, 3))]
    ppermute x21 -> x20, starting transfers between devices: 19.5 us -> 16.8 us  [swap(): return lax.ppermute(value, axis, [(i, i ^ mask) for i in range(count)])]
    ppermute x1 -> x2, starting transfers between devices: 0.5 us -> 2.09 us  [the longest x1 1.52 us: shards(): second = lax.ppermute(joined, 'stream', crossing(masks, 1, 2))]
where the time goes in v5:
time: 65.4 us; the launch traced here: 65.3 us
  waiting for transfers between devices  31.8 us (49%)
  starting transfers between devices  18.9 us (29%)
  Pallas kernels  14.4 us (22%)
    ppermute x20, waiting for transfers between devices, swap(): return lax.ppermute(value, axis, [(i, i ^ mask) for i in range(count)])  28.2 us
    ppermute x20, starting transfers between devices, swap(): return lax.ppermute(value, axis, [(i, i ^ mask) for i in range(count)])  16.8 us
    pallas_call x8, Pallas kernels, call(): pl.pallas_call(kernel, out_shape=outs, in_specs=[SMEM] * len(scalars) + [...  14.4 us
    ppermute x1, waiting for transfers between devices, shards(): third = lax.ppermute(joined, 'stream', crossing(masks, 1, 3))  2.59 us
    ppermute x1, starting transfers between devices, shards(): second = lax.ppermute(joined, 'stream', crossing(masks, 1, 2))  1.52 us
  transfers between devices with their start and end apart: 22, of which 13 were waited for; matrix products, arithmetic and copies ran while one was open for 0% of the time, Pallas kernels for 1%

profile of v5, /device:TPU:0, one launch (start us, length us, event | category | flops | bytes accessed | tf_op | source)
XLA Modules:
  0.0 65.3 jit_solution(9186952379321109301)
XLA Ops:
  0.0 2.7 %shard_map.46 = (bf16[576,128]{1,0:T(8,128)(2,1)S(1)}, bf16[2,256,512]{2,1,0:T(8,128)(2,1)S(1)}, bf16[2,512,512]{2,1,0:T(8,128)(2,1)S(1)}, bf16[2,192,512]{2,1,0:T(8,128)(2,1)S(1)}, bf16[4,512,128]{2,1,0:T(8,128)(2,1)S(1)}) custom-call(s32[4]{0:T(128)} %bitcast.13, bf16[4,512,512]{2,1,0:T(8,128)(2,1)} %bitcast.7, bf16[4,192,512]{2,1,0:T(8,128)(2,1)} %bitcast.9, ...), custom_call_target="tpu_custom_call" | custom-call | tf_op jit(solution)/shard_map/pallas_call | solution.py:483
  3.4 3.0 %collective-permute-start.3 = (bf16[576,128]{1,0:T(8,128)(2,1)S(1)}, bf16[576,128]{1,0:T(8,128)(2,1)S(1)}, u32[]{:S(2)}, u32[]{:S(2)}) collective-permute-start(bf16[576,128]{1,0:T(8,128)(2,1)S(1)} %get-tuple-element.28.refs_4_), channel_id=1, source_target_pairs={{0,2},{1,3},{2,0},{3,1},{4,6},{5,7},{6,4},{7,5},{8,10},{9,11},{10,... | collective-permute-start | bytes 442376 | tf_op jit(solution)/shard_map/ppermute | solution.py:38
  7.0 4.1 %collective-permute-done.3.refs_5_ = bf16[576,128]{1,0:T(8,128)(2,1)S(1)} collective-permute-done((bf16[576,128]{1,0:T(8,128)(2,1)S(1)}, bf16[576,128]{1,0:T(8,128)(2,1)S(1)}, u32[]{:S(2)}, u32[]{:S(2)}) %collective-permute-start.3) | collective-permute-done | bytes 147488 | tf_op jit(solution)/shard_map/ppermute | solution.py:38
  11.1 2.3 %collective-permute-done.refs_1_ = bf16[576,128]{1,0:T(8,128)(2,1)S(1)} collective-permute-done((bf16[576,128]{1,0:T(8,128)(2,1)S(1)}, bf16[576,128]{1,0:T(8,128)(2,1)S(1)}, u32[]{:S(2)}, u32[]{:S(2)}) %collective-permute-start) | collective-permute-done | bytes 147488 | tf_op jit(solution)/shard_map/ppermute | solution.py:38
  13.4 1.7 %collective-permute-start.7 = (bf16[6,32,128]{2,1,0:T(8,128)(2,1)S(1)}, bf16[6,32,128]{2,1,0:T(8,128)(2,1)S(1)}, u32[]{:S(2)}, u32[]{:S(2)}) collective-permute-start(bf16[6,32,128]{2,1,0:T(8,128)(2,1)S(1)} %get-tuple-element.31), channel_id=1, source_target_pairs={{0,2},{1,3},{2,0},{3,1},{4,6},{5,7},{6,4},{7,5},{8,10},{9,11},{10,... | collective-permute-start | bytes 147464 | tf_op jit(solution)/shard_map/ppermute | solution.py:38
  15.2 2.4 %collective-permute-done.7.refs_10_ = bf16[6,32,128]{2,1,0:T(8,128)(2,1)S(1)} collective-permute-done((bf16[6,32,128]{2,1,0:T(8,128)(2,1)S(1)}, bf16[6,32,128]{2,1,0:T(8,128)(2,1)S(1)}, u32[]{:S(2)}, u32[]{:S(2)}) %collective-permute-start.7) | collective-permute-done | bytes 49184 | tf_op jit(solution)/shard_map/ppermute | solution.py:38
  18.6 2.8 %collective-permute-done.8.refs_11_ = bf16[6,32,128]{2,1,0:T(8,128)(2,1)S(1)} collective-permute-done((bf16[6,32,128]{2,1,0:T(8,128)(2,1)S(1)}, bf16[6,32,128]{2,1,0:T(8,128)(2,1)S(1)}, u32[]{:S(2)}, u32[]{:S(2)}) %collective-permute-start.8) | collective-permute-done | bytes 49184 | tf_op jit(solution)/shard_map/ppermute | solution.py:38
  21.4 3.8 %shard_map.48 = (bf16[6,128,128]{2,1,0:T(8,128)(2,1)S(1)}, bf16[6,64,128]{2,1,0:T(8,128)(2,1)S(1)}, bf16[4,4,256,256]{3,2,1,0:T(8,128)(2,1)S(1)}, bf16[4,4,32,256]{3,2,1,0:T(8,128)(2,1)S(1)}) custom-call(s32[1]{0:T(128)} %bitcast.place, bf16[576,128]{1,0:T(8,128)(2,1)S(1)} %get-tuple-element.23.refs_0_, bf16[576,128]{1,0:T(8,128)(2,1)S(1)} %collective-permute-done.refs_1_, ...), custom_call_target="tpu_custom_call" | custom-call | tf_op jit(solution)/shard_map/pallas_call | solution.py:483
  25.1 2.1 %collective-permute-start.13 = (bf16[6,128,128]{2,1,0:T(8,128)(2,1)S(1)}, bf16[6,128,128]{2,1,0:T(8,128)(2,1)S(1)}, u32[]{:S(2)}, u32[]{:S(2)}) collective-permute-start(bf16[6,128,128]{2,1,0:T(8,128)(2,1)S(1)} %get-tuple-element.35.even.own), channel_id=1, source_target_pairs={{0,4},{4,0},{8,12},{12,8},{16,20},{20,16},{24,28},{28,24},{1,5},{5... | collective-permute-start | bytes 589832 | tf_op jit(solution)/shard_map/ppermute | solution.py:38
  27.2 5.2 %collective-permute-done.13.got.refs_8_ = bf16[6,128,128]{2,1,0:T(8,128)(2,1)S(1)} collective-permute-done((bf16[6,128,128]{2,1,0:T(8,128)(2,1)S(1)}, bf16[6,128,128]{2,1,0:T(8,128)(2,1)S(1)}, u32[]{:S(2)}, u32[]{:S(2)}) %collective-permute-start.13) | collective-permute-done | bytes 196640 | tf_op jit(solution)/shard_map/ppermute | solution.py:38
  32.4 1.4 %collective-permute-done.14.got_other.refs_9_ = bf16[6,128,128]{2,1,0:T(8,128)(2,1)S(1)} collective-permute-done((bf16[6,128,128]{2,1,0:T(8,128)(2,1)S(1)}, bf16[6,128,128]{2,1,0:T(8,128)(2,1)S(1)}, u32[]{:S(2)}, u32[]{:S(2)}) %collective-permute-start.14) | collective-permute-done | bytes 196640 | tf_op jit(solution)/shard_map/ppermute | solution.py:38
  34.2 1.9 %collective-permute-start.17 = (bf16[6,128,128]{2,1,0:T(8,128)(2,1)S(1)}, bf16[6,128,128]{2,1,0:T(8,128)(2,1)S(1)}, u32[]{:S(2)}, u32[]{:S(2)}) collective-permute-start(bf16[6,128,128]{2,1,0:T(8,128)(2,1)S(1)} %shard_map.51), channel_id=1, source_target_pairs={{0,8},{4,12},{8,0},{12,4},{16,24},{20,28},{24,16},{28,20},{1,9},{5... | collective-permute-start | bytes 589832 | tf_op jit(solution)/shard_map/ppermute | solution.py:38
  36.0 1.5 %collective-permute-start.10 = (bf16[6,64,128]{2,1,0:T(8,128)(2,1)S(1)}, bf16[6,64,128]{2,1,0:T(8,128)(2,1)S(1)}, u32[]{:S(2)}, u32[]{:S(2)}) collective-permute-start(bf16[6,64,128]{2,1,0:T(8,128)(2,1)S(1)} %get-tuple-element.36.own.own_offset), channel_id=1, source_target_pairs={{0,4},{4,0},{8,12},{12,8},{16,20},{20,16},{24,28},{28,24},{1,5},{5... | collective-permute-start | bytes 294920 | tf_op jit(solution)/shard_map/ppermute | solution.py:38
  37.6 3.1 %collective-permute-done.10.entry.got_offset.refs_10_ = bf16[6,64,128]{2,1,0:T(8,128)(2,1)S(1)} collective-permute-done((bf16[6,64,128]{2,1,0:T(8,128)(2,1)S(1)}, bf16[6,64,128]{2,1,0:T(8,128)(2,1)S(1)}, u32[]{:S(2)}, u32[]{:S(2)}) %collective-permute-start.10) | collective-permute-done | bytes 98336 | tf_op jit(solution)/shard_map/ppermute | solution.py:38
  41.0 1.5 %collective-permute-start.12 = (bf16[6,64,128]{2,1,0:T(8,128)(2,1)S(1)}, bf16[6,64,128]{2,1,0:T(8,128)(2,1)S(1)}, u32[]{:S(2)}, u32[]{:S(2)}) collective-permute-start(bf16[6,64,128]{2,1,0:T(8,128)(2,1)S(1)} %shard_map.49), channel_id=1, source_target_pairs={{0,12},{4,8},{8,4},{12,0},{16,28},{20,24},{24,20},{28,16},{1,13},{... | collective-permute-start | bytes 294920 | tf_op jit(solution)/shard_map/ppermute | solution.py:38
  42.4 1.6 %collective-permute-start.11 = (bf16[6,64,128]{2,1,0:T(8,128)(2,1)S(1)}, bf16[6,64,128]{2,1,0:T(8,128)(2,1)S(1)}, u32[]{:S(2)}, u32[]{:S(2)}) collective-permute-start(bf16[6,64,128]{2,1,0:T(8,128)(2,1)S(1)} %shard_map.49), channel_id=1, source_target_pairs={{0,8},{4,12},{8,0},{12,4},{16,24},{20,28},{24,16},{28,20},{1,9},{5... | collective-permute-start | bytes 294920 | tf_op jit(solution)/shard_map/ppermute | solution.py:38
  44.0 2.7 %collective-permute-done.12.across.refs_3_ = bf16[6,64,128]{2,1,0:T(8,128)(2,1)S(1)} collective-permute-done((bf16[6,64,128]{2,1,0:T(8,128)(2,1)S(1)}, bf16[6,64,128]{2,1,0:T(8,128)(2,1)S(1)}, u32[]{:S(2)}, u32[]{:S(2)}) %collective-permute-start.12) | collective-permute-done | bytes 98336 | tf_op jit(solution)/shard_map/ppermute | solution.py:38
  46.7 1.1 %collective-permute-done.11.near.refs_2_ = bf16[6,64,128]{2,1,0:T(8,128)(2,1)S(1)} collective-permute-done((bf16[6,64,128]{2,1,0:T(8,128)(2,1)S(1)}, bf16[6,64,128]{2,1,0:T(8,128)(2,1)S(1)}, u32[]{:S(2)}, u32[]{:S(2)}) %collective-permute-start.11) | collective-permute-done | bytes 98336 | tf_op jit(solution)/shard_map/ppermute | solution.py:38
  49.0 1.5 %collective-permute-start.15 = (bf16[6,64,128]{2,1,0:T(8,128)(2,1)S(1)}, bf16[6,64,128]{2,1,0:T(8,128)(2,1)S(1)}, u32[]{:S(2)}, u32[]{:S(2)}) collective-permute-start(bf16[6,64,128]{2,1,0:T(8,128)(2,1)S(1)} %shard_map.50), channel_id=1, source_target_pairs={{0,4},{4,0},{8,16},{12,20},{16,8},{20,12},{24,28},{28,24},{1,5},{5... | collective-permute-start | bytes 294920 | tf_op jit(solution)/shard_map/ppermute | solution.py:581
  50.5 2.6 %collective-permute-done.16.refs_5_ = bf16[6,64,128]{2,1,0:T(8,128)(2,1)S(1)} collective-permute-done((bf16[6,64,128]{2,1,0:T(8,128)(2,1)S(1)}, bf16[6,64,128]{2,1,0:T(8,128)(2,1)S(1)}, u32[]{:S(2)}, u32[]{:S(2)}) %collective-permute-start.16) | collective-permute-done | bytes 98336 | tf_op jit(solution)/shard_map/ppermute | solution.py:582
  54.2 3.5 %shard_map.52 = (bf16[6,32,128]{2,1,0:T(8,128)(2,1)S(1)}, bf16[6,32,128]{2,1,0:T(8,128)(2,1)S(1)}, bf16[6,32,128]{2,1,0:T(8,128)(2,1)S(1)}, bf16[6,32,128]{2,1,0:T(8,128)(2,1)S(1)}) custom-call(s32[1]{0:T(128)} %bitcast.place, s32[1]{0:T(128)} %bitcast.5.line, bf16[4,4,256,256]{3,2,1,0:T(8,128)(2,1)S(1)} %get-tuple-element.33.refs_0_, ...), custom_call_target="tpu_custom_call" | custom-call | tf_op jit(solution)/shard_map/pallas_call | solution.py:483
  57.8 1.3 %collective-permute-start.20 = (bf16[6,32,128]{2,1,0:T(8,128)(2,1)S(1)}, bf16[6,32,128]{2,1,0:T(8,128)(2,1)S(1)}, u32[]{:S(2)}, u32[]{:S(2)}) collective-permute-start(bf16[6,32,128]{2,1,0:T(8,128)(2,1)S(1)} %get-tuple-element.39), channel_id=1, source_target_pairs={{0,2},{1,3},{2,0},{3,1},{4,6},{5,7},{6,4},{7,5},{8,10},{9,11},{10,... | collective-permute-start | bytes 147464 | tf_op jit(solution)/shard_map/ppermute | solution.py:38
  59.6 2.3 %collective-permute-done.20.refs_2_ = bf16[6,32,128]{2,1,0:T(8,128)(2,1)S(1)} collective-permute-done((bf16[6,32,128]{2,1,0:T(8,128)(2,1)S(1)}, bf16[6,32,128]{2,1,0:T(8,128)(2,1)S(1)}, u32[]{:S(2)}, u32[]{:S(2)}) %collective-permute-start.20) | collective-permute-done | bytes 49184 | tf_op jit(solution)/shard_map/ppermute | solution.py:38
  62.7 2.5 %shard_map.53 = bf16[4,512,128]{2,1,0:T(8,128)(2,1)} custom-call(s32[1]{0:T(128)} %bitcast.place, s32[4]{0:T(128)S(1)} %bitcast.14, bf16[4,512,512]{2,1,0:T(8,128)(2,1)S(1)} %bitcast.8, bf16[4,192,512]{2,1,0:T(8,128)(2,1)S(1)} %bitcast.10, bf16[4,512,128]{2,1,0:T(8,128)(2,1)S(1)} %bitcast.12, bf16[6,32,128]{2,1,0:T(8,128)(2,1)S(1)} %get-tuple-element.37.refs_0_, ...), custom_call_target="tpu_custom_call" | custom-call | tf_op jit(solution)/shard_map/pallas_call | solution.py:483
  (36 shorter events, 6.7 us)
Async XLA Ops:
  3.4 7.7 %collective-permute-start.3 = (bf16[576,128]{1,0:T(8,128)(2,1)S(1)}, bf16[576,128]{1,0:T(8,128)(2,1)S(1)}, u32[]{:S(2)}, u32[]{:S(2)}) collective-permute-start(bf16[576,128]{1,0:T(8,128)(2,1)S(1)} %get-tuple-element.28.refs_4_), channel_id=1, source_target_pairs={{0,2},{1,3},{2,0},{3,1},{4,6},{5,7},{6,4},{7,5},{8,10},{9,11},{10,... | collective-permute-start | bytes 442376 | tf_op jit(solution)/shard_map/ppermute | solution.py:38
  6.4 7.0 %collective-permute-start = (bf16[576,128]{1,0:T(8,128)(2,1)S(1)}, bf16[576,128]{1,0:T(8,128)(2,1)S(1)}, u32[]{:S(2)}, u32[]{:S(2)}) collective-permute-start(bf16[576,128]{1,0:T(8,128)(2,1)S(1)} %get-tuple-element.23.refs_0_), channel_id=1, source_target_pairs={{0,2},{1,3},{2,0},{3,1},{4,6},{5,7},{6,4},{7,5},{8,10},{9,11},{10,... | collective-permute-start | bytes 442376 | tf_op jit(solution)/shard_map/ppermute | solution.py:38
  6.5 6.9 %collective-permute-start.6 = (bf16[6,32,128]{2,1,0:T(8,128)(2,1)S(1)}, bf16[6,32,128]{2,1,0:T(8,128)(2,1)S(1)}, u32[]{:S(2)}, u32[]{:S(2)}) collective-permute-start(bf16[6,32,128]{2,1,0:T(8,128)(2,1)S(1)} %get-tuple-element.30), channel_id=1, source_target_pairs={{0,1},{1,0},{2,3},{3,2},{4,5},{5,4},{6,7},{7,6},{8,9},{9,8},{10,11... | collective-permute-start | bytes 147464 | tf_op jit(solution)/shard_map/ppermute | solution.py:38
  6.5 14.8 %collective-permute-start.4 = (bf16[576,128]{1,0:T(8,128)(2,1)S(1)}, bf16[576,128]{1,0:T(8,128)(2,1)S(1)}, u32[]{:S(2)}, u32[]{:S(2)}) collective-permute-start(bf16[576,128]{1,0:T(8,128)(2,1)S(1)} %get-tuple-element.28.refs_4_), channel_id=1, source_target_pairs={{0,1},{1,0},{2,3},{3,2},{4,5},{5,4},{6,7},{7,6},{8,9},{9,8},{10,11... | collective-permute-start | bytes 442376 | tf_op jit(solution)/shard_map/ppermute | solution.py:38
  7.0 14.3 %collective-permute-start.1 = (bf16[576,128]{1,0:T(8,128)(2,1)S(1)}, bf16[576,128]{1,0:T(8,128)(2,1)S(1)}, u32[]{:S(2)}, u32[]{:S(2)}) collective-permute-start(bf16[576,128]{1,0:T(8,128)(2,1)S(1)} %get-tuple-element.23.refs_0_), channel_id=1, source_target_pairs={{0,1},{1,0},{2,3},{3,2},{4,5},{5,4},{6,7},{7,6},{8,9},{9,8},{10,11... | collective-permute-start | bytes 442376 | tf_op jit(solution)/shard_map/ppermute | solution.py:38
  11.1 10.2 %collective-permute-start.5 = (bf16[576,128]{1,0:T(8,128)(2,1)S(1)}, bf16[576,128]{1,0:T(8,128)(2,1)S(1)}, u32[]{:S(2)}, u32[]{:S(2)}) collective-permute-start(bf16[576,128]{1,0:T(8,128)(2,1)S(1)} %collective-permute-done.3.refs_5_), channel_id=1, source_target_pairs={{0,1},{1,0},{2,3},{3,2},{4,5},{5,4},{6,7},{7,6},{8,9},{9,8},{10,11... | collective-permute-start | bytes 442376 | tf_op jit(solution)/shard_map/ppermute | solution.py:38
  13.4 7.9 %collective-permute-start.2 = (bf16[576,128]{1,0:T(8,128)(2,1)S(1)}, bf16[576,128]{1,0:T(8,128)(2,1)S(1)}, u32[]{:S(2)}, u32[]{:S(2)}) collective-permute-start(bf16[576,128]{1,0:T(8,128)(2,1)S(1)} %collective-permute-done.refs_1_), channel_id=1, source_target_pairs={{0,1},{1,0},{2,3},{3,2},{4,5},{5,4},{6,7},{7,6},{8,9},{9,8},{10,11... | collective-permute-start | bytes 442376 | tf_op jit(solution)/shard_map/ppermute | solution.py:38
  13.4 4.2 %collective-permute-start.7 = (bf16[6,32,128]{2,1,0:T(8,128)(2,1)S(1)}, bf16[6,32,128]{2,1,0:T(8,128)(2,1)S(1)}, u32[]{:S(2)}, u32[]{:S(2)}) collective-permute-start(bf16[6,32,128]{2,1,0:T(8,128)(2,1)S(1)} %get-tuple-element.31), channel_id=1, source_target_pairs={{0,2},{1,3},{2,0},{3,1},{4,6},{5,7},{6,4},{7,5},{8,10},{9,11},{10,... | collective-permute-start | bytes 147464 | tf_op jit(solution)/shard_map/ppermute | solution.py:38
  17.6 3.7 %collective-permute-start.8 = (bf16[6,32,128]{2,1,0:T(8,128)(2,1)S(1)}, bf16[6,32,128]{2,1,0:T(8,128)(2,1)S(1)}, u32[]{:S(2)}, u32[]{:S(2)}) collective-permute-start(bf16[6,32,128]{2,1,0:T(8,128)(2,1)S(1)} %get-tuple-element.32), channel_id=1, source_target_pairs={{0,3},{1,2},{2,1},{3,0},{4,7},{5,6},{6,5},{7,4},{8,11},{9,10},{10,... | collective-permute-start | bytes 147464 | tf_op jit(solution)/shard_map/ppermute | solution.py:38
  25.1 7.2 %collective-permute-start.13 = (bf16[6,128,128]{2,1,0:T(8,128)(2,1)S(1)}, bf16[6,128,128]{2,1,0:T(8,128)(2,1)S(1)}, u32[]{:S(2)}, u32[]{:S(2)}) collective-permute-start(bf16[6,128,128]{2,1,0:T(8,128)(2,1)S(1)} %get-tuple-element.35.even.own), channel_id=1, source_target_pairs={{0,4},{4,0},{8,12},{12,8},{16,20},{20,16},{24,28},{28,24},{1,5},{5... | collective-permute-start | bytes 589832 | tf_op jit(solution)/shard_map/ppermute | solution.py:38
  27.2 5.2 %collective-permute-start.9 = (bf16[6,128,128]{2,1,0:T(8,128)(2,1)S(1)}, bf16[6,128,128]{2,1,0:T(8,128)(2,1)S(1)}, u32[]{:S(2)}, u32[]{:S(2)}) collective-permute-start(bf16[6,128,128]{2,1,0:T(8,128)(2,1)S(1)} %get-tuple-element.35.even.own), channel_id=1, source_target_pairs={{0,1},{1,0},{2,3},{3,2},{4,5},{5,4},{6,7},{7,6},{8,9},{9,8},{10,11... | collective-permute-start | bytes 589832 | tf_op jit(solution)/shard_map/ppermute | solution.py:38
  32.4 1.4 %collective-permute-start.14 = (bf16[6,128,128]{2,1,0:T(8,128)(2,1)S(1)}, bf16[6,128,128]{2,1,0:T(8,128)(2,1)S(1)}, u32[]{:S(2)}, u32[]{:S(2)}) collective-permute-start(bf16[6,128,128]{2,1,0:T(8,128)(2,1)S(1)} %collective-permute-done.13.got.refs_8_), channel_id=1, source_target_pairs={{0,1},{1,0},{2,3},{3,2},{4,5},{5,4},{6,7},{7,6},{8,9},{9,8},{10,11... | collective-permute-start | bytes 589832 | tf_op jit(solution)/shard_map/ppermute | solution.py:38
  34.2 9.9 %collective-permute-start.17 = (bf16[6,128,128]{2,1,0:T(8,128)(2,1)S(1)}, bf16[6,128,128]{2,1,0:T(8,128)(2,1)S(1)}, u32[]{:S(2)}, u32[]{:S(2)}) collective-permute-start(bf16[6,128,128]{2,1,0:T(8,128)(2,1)S(1)} %shard_map.51), channel_id=1, source_target_pairs={{0,8},{4,12},{8,0},{12,4},{16,24},{20,28},{24,16},{28,20},{1,9},{5... | collective-permute-start | bytes 589832 | tf_op jit(solution)/shard_map/ppermute | solution.py:38
  36.0 4.6 %collective-permute-start.10 = (bf16[6,64,128]{2,1,0:T(8,128)(2,1)S(1)}, bf16[6,64,128]{2,1,0:T(8,128)(2,1)S(1)}, u32[]{:S(2)}, u32[]{:S(2)}) collective-permute-start(bf16[6,64,128]{2,1,0:T(8,128)(2,1)S(1)} %get-tuple-element.36.own.own_offset), channel_id=1, source_target_pairs={{0,4},{4,0},{8,12},{12,8},{16,20},{20,16},{24,28},{28,24},{1,5},{5... | collective-permute-start | bytes 294920 | tf_op jit(solution)/shard_map/ppermute | solution.py:38
  41.0 5.7 %collective-permute-start.12 = (bf16[6,64,128]{2,1,0:T(8,128)(2,1)S(1)}, bf16[6,64,128]{2,1,0:T(8,128)(2,1)S(1)}, u32[]{:S(2)}, u32[]{:S(2)}) collective-permute-start(bf16[6,64,128]{2,1,0:T(8,128)(2,1)S(1)} %shard_map.49), channel_id=1, source_target_pairs={{0,12},{4,8},{8,4},{12,0},{16,28},{20,24},{24,20},{28,16},{1,13},{... | collective-permute-start | bytes 294920 | tf_op jit(solution)/shard_map/ppermute | solution.py:38
  42.4 5.4 %collective-permute-start.11 = (bf16[6,64,128]{2,1,0:T(8,128)(2,1)S(1)}, bf16[6,64,128]{2,1,0:T(8,128)(2,1)S(1)}, u32[]{:S(2)}, u32[]{:S(2)}) collective-permute-start(bf16[6,64,128]{2,1,0:T(8,128)(2,1)S(1)} %shard_map.49), channel_id=1, source_target_pairs={{0,8},{4,12},{8,0},{12,4},{16,24},{20,28},{24,16},{28,20},{1,9},{5... | collective-permute-start | bytes 294920 | tf_op jit(solution)/shard_map/ppermute | solution.py:38
  44.0 10.1 %collective-permute-start.18 = (bf16[6,128,128]{2,1,0:T(8,128)(2,1)S(1)}, bf16[6,128,128]{2,1,0:T(8,128)(2,1)S(1)}, u32[]{:S(2)}, u32[]{:S(2)}) collective-permute-start(bf16[6,128,128]{2,1,0:T(8,128)(2,1)S(1)} %collective-permute-done.17.refs_6_), channel_id=1, source_target_pairs={{0,1},{1,0},{2,3},{3,2},{4,5},{5,4},{6,7},{7,6},{8,9},{9,8},{10,11... | collective-permute-start | bytes 589832 | tf_op jit(solution)/shard_map/ppermute | solution.py:38
  48.4 14.4 %copy-start = (bf16[1,1,4,512,512]{4,3,2,1,0:T(8,128)(2,1)S(1)}, bf16[1,1,4,512,512]{4,3,2,1,0:T(8,128)(2,1)}, u32[]{:S(2)}) copy-start(bf16[1,1,4,512,512]{4,3,2,1,0:T(8,128)(2,1)} %param.5) | copy-start | bytes 6291460
  48.4 14.3 %copy-start.1 = (bf16[1,1,4,3,64,512]{5,4,3,2,1,0:T(8,128)(2,1)S(1)}, bf16[1,1,4,3,64,512]{5,4,3,2,1,0:T(8,128)(2,1)}, u32[]{:S(2)}) copy-start(bf16[1,1,4,3,64,512]{5,4,3,2,1,0:T(8,128)(2,1)} %param.6) | copy-start | bytes 2359300
  48.4 4.7 %collective-permute-start.16 = (bf16[6,64,128]{2,1,0:T(8,128)(2,1)S(1)}, bf16[6,64,128]{2,1,0:T(8,128)(2,1)S(1)}, u32[]{:S(2)}, u32[]{:S(2)}) collective-permute-start(bf16[6,64,128]{2,1,0:T(8,128)(2,1)S(1)} %shard_map.50), channel_id=1, source_target_pairs={{0,4},{4,0},{8,24},{12,28},{16,20},{20,16},{24,8},{28,12},{1,5},{5... | collective-permute-start | bytes 294920 | tf_op jit(solution)/shard_map/ppermute | solution.py:582
  49.0 5.2 %collective-permute-start.15 = (bf16[6,64,128]{2,1,0:T(8,128)(2,1)S(1)}, bf16[6,64,128]{2,1,0:T(8,128)(2,1)S(1)}, u32[]{:S(2)}, u32[]{:S(2)}) collective-permute-start(bf16[6,64,128]{2,1,0:T(8,128)(2,1)S(1)} %shard_map.50), channel_id=1, source_target_pairs={{0,4},{4,0},{8,16},{12,20},{16,8},{20,12},{24,28},{28,24},{1,5},{5... | collective-permute-start | bytes 294920 | tf_op jit(solution)/shard_map/ppermute | solution.py:581
  57.7 1.9 %collective-permute-start.19 = (bf16[6,32,128]{2,1,0:T(8,128)(2,1)S(1)}, bf16[6,32,128]{2,1,0:T(8,128)(2,1)S(1)}, u32[]{:S(2)}, u32[]{:S(2)}) collective-permute-start(bf16[6,32,128]{2,1,0:T(8,128)(2,1)S(1)} %get-tuple-element.38), channel_id=1, source_target_pairs={{0,1},{1,0},{2,3},{3,2},{4,5},{5,4},{6,7},{7,6},{8,9},{9,8},{10,11... | collective-permute-start | bytes 147464 | tf_op jit(solution)/shard_map/ppermute | solution.py:38
  57.8 4.2 %collective-permute-start.20 = (bf16[6,32,128]{2,1,0:T(8,128)(2,1)S(1)}, bf16[6,32,128]{2,1,0:T(8,128)(2,1)S(1)}, u32[]{:S(2)}, u32[]{:S(2)}) collective-permute-start(bf16[6,32,128]{2,1,0:T(8,128)(2,1)S(1)} %get-tuple-element.39), channel_id=1, source_target_pairs={{0,2},{1,3},{2,0},{3,1},{4,6},{5,7},{6,4},{7,5},{8,10},{9,11},{10,... | collective-permute-start | bytes 147464 | tf_op jit(solution)/shard_map/ppermute | solution.py:38
  59.0 3.7 %collective-permute-start.21 = (bf16[6,32,128]{2,1,0:T(8,128)(2,1)S(1)}, bf16[6,32,128]{2,1,0:T(8,128)(2,1)S(1)}, u32[]{:S(2)}, u32[]{:S(2)}) collective-permute-start(bf16[6,32,128]{2,1,0:T(8,128)(2,1)S(1)} %get-tuple-element.40), channel_id=1, source_target_pairs={{0,3},{1,2},{2,1},{3,0},{4,7},{5,6},{6,5},{7,4},{8,11},{9,10},{10,... | collective-permute-start | bytes 147464 | tf_op jit(solution)/shard_map/ppermute | solution.py:38
  (2 other events, 28.7 us)

commit v6 on v5

--- a/solution.py
+++ b/solution.py
@@ -92,30 +92,35 @@
 
 def first_kernel(order_far, inverse_far, coupling_far, given_far, *refs):
     maps, rows, inverse_near, coupling_near, given_near = refs[:5]
-    inverse, coupling, order, order_done, done = refs[5:]
+    inverse, coupling, order, order_done, done, near_done = refs[5:]
     count = given_near.shape[0]
     face = coupling.shape[1] // 3
     first = pltpu.make_async_copy(order_far, order, order_done)
     first.start()
+    copies = []
+    for kind, (far, near) in enumerate(((inverse_far, inverse), (coupling_far, coupling))):
+        for slot in range(count):
+            copies.append(pltpu.make_async_copy(far.at[slot], near.at[slot], done.at[kind, slot]))
+    for copy in copies:
+        copy.start()
     first.wait()
-    early = []
-    later = []
-    for p in range(count):
-        slot = order[p]
-        near = (inverse.at[p], coupling.at[p]) if p < 2 else (inverse_near.at[p - 2], coupling_near.at[p - 2])
-        copies = early if p < 2 else later
-        copies.append(pltpu.make_async_copy(inverse_far.at[slot], near[0], done.at[0, p]))
-        copies.append(pltpu.make_async_copy(coupling_far.at[slot], near[1], done.at[1, p]))
-        later.append(pltpu.make_async_copy(given_far.at[slot], given_near.at[p], done.at[2, p]))
-    for copy in early + later:
+    slots = [order[p] for p in range(count)]
+    later = [
+        pltpu.make_async_copy(given_far.at[slots[p]], given_near.at[p], near_done.at[0, p]) for p in range(count)
+    ]
+    for copy in later:
         copy.start()
+    for copy in copies:
+        copy.wait()
+    for p in range(2, count):
+        for kind, (held, near) in enumerate(((inverse, inverse_near), (coupling, coupling_near))):
+            later.append(pltpu.make_async_copy(held.at[slots[p]], near.at[p - 2], near_done.at[kind + 1, p]))
+            later[-1].start()
     values = []
     for p in range(2):
-        early[2 * p].wait()
-        early[2 * p + 1].wait()
-        values.append(face_rows_of(inverse, p, face))
+        values.append(face_rows_of(inverse, slots[p], face))
         rows[p] = values[p]
-    pair_maps(maps, coupling, (0, 1), values, face)
+    pair_maps(maps, coupling, slots[:2], values, face)
     for copy in later:
         copy.wait()
 
@@ -152,8 +157,7 @@
             for i in range(2):
                 sides = ref[i * 3 * face : (i + 1) * 3 * face, :]
                 full = jnp.concatenate([sides, by_half(outs, other) if i == 0 else by_half(other, outs)], axis=1)
-                weights[pos, 2 * j + i, : 3 * face, :] = full
-                weights[pos, 2 * j + i, 3 * face :, :] = full[2 * face :]
+                weights[pos, 2 * j + i] = full
 
 
 def unpack_gains(gain_refs, gains, count):
@@ -205,10 +209,13 @@
     for p in range(count):
         for i, pos in enumerate(chosen):
             rows = entries[i].shape[0]
-            if first:
-                result = dot(entries[i], weights[pos, p, 2 * face :])
-            else:
-                result = dot(jnp.concatenate([lags[pos, p, :rows], entries[i]], axis=1), weights[pos, p])
+            left = entries[i]
+            own = weights[pos, p, 2 * face :]
+            right = jnp.concatenate([own, own], axis=0)
+            if not first:
+                left = jnp.concatenate([lags[pos, p, :rows], left], axis=1)
+                right = jnp.concatenate([weights[pos, p, : 2 * face], right], axis=0)
+            result = dot(left, right)
             head = result[:share] + gains[pos, p].astype(F32)
             result = head if rows == share else jnp.concatenate([head, result[share:]], axis=0)
             states[pos, p, :rows] = result[:, : 2 * face].astype(BF16)
@@ -393,11 +400,11 @@
         for p in range(count - (stage == 2)):
             for i, pos in enumerate(chosen):
                 left = every[i][p][:, :face]
-                right = weights[pos, p, 2 * face : 3 * face]
+                right = weights[pos, p, 2 * face :]
                 added = gains[pos, p].astype(F32)
                 if stage > 0:
                     left = jnp.concatenate([lags[pos, p], left], axis=1)
-                    right = weights[pos, p, : 3 * face]
+                    right = weights[pos, p]
                 if stage == 2:
                     right = right[:, 2 * face :]
                     added = added[:, 2 * face :]
@@ -515,13 +522,14 @@
             shape((count - 2,) + coupling.shape[1:], BF16),
             shape(given.shape, BF16),
         ],
-        [((2,) + inverse.shape[1:], BF16), ((2,) + coupling.shape[1:], BF16)],
+        [(inverse.shape, BF16), (coupling.shape, BF16)],
         [],
         far,
         4,
         (
             pltpu.SMEM(order.shape, order.dtype),
             pltpu.SemaphoreType.DMA,
+            pltpu.SemaphoreType.DMA((2, count)),
             pltpu.SemaphoreType.DMA((3, count)),
         ),
     )
@@ -544,7 +552,7 @@
         [
             shape((SWEEPS, wide, wide), BF16),
             shape((SWEEPS, 2 * share, wide), BF16),
-            shape((groups, count, 4 * face, 4 * face), BF16),
+            shape((groups, count, 3 * face, 4 * face), BF16),
             shape((groups, count, share, 4 * face), BF16),
         ],
         [

time: 65.4 us -> 65.6 us (level)
  no operation moved by 1% of the time
where the time goes in v6:
time: 65.6 us; the launch traced here: 65.5 us
  waiting for transfers between devices  31.8 us (48%)
  starting transfers between devices  18.9 us (29%)
  Pallas kernels  14.6 us (22%)
    ppermute x20, waiting for transfers between devices, swap(): return lax.ppermute(value, axis, [(i, i ^ mask) for i in range(count)])  28.2 us
    ppermute x20, starting transfers between devices, swap(): return lax.ppermute(value, axis, [(i, i ^ mask) for i in range(count)])  16.8 us
    pallas_call x8, Pallas kernels, call(): pl.pallas_call(kernel, out_shape=outs, in_specs=[SMEM] * len(scalars) + [...  14.6 us
    ppermute x1, waiting for transfers between devices, shards(): third = lax.ppermute(joined, 'stream', crossing(masks, 1, 3))  2.59 us
    ppermute x1, starting transfers between devices, shards(): second = lax.ppermute(joined, 'stream', crossing(masks, 1, 2))  1.53 us
  transfers between devices with their start and end apart: 22, of which 13 were waited for; matrix products, arithmetic and copies ran while one was open for 0% of the time, Pallas kernels for 1%

profile of v6, /device:TPU:0, one launch (start us, length us, event | category | flops | bytes accessed | tf_op | source)
XLA Modules:
  0.0 65.5 jit_solution(18060762957286534248)
XLA Ops:
  0.0 2.9 %shard_map.46 = (bf16[576,128]{1,0:T(8,128)(2,1)S(1)}, bf16[2,256,512]{2,1,0:T(8,128)(2,1)S(1)}, bf16[2,512,512]{2,1,0:T(8,128)(2,1)S(1)}, bf16[2,192,512]{2,1,0:T(8,128)(2,1)S(1)}, bf16[4,512,128]{2,1,0:T(8,128)(2,1)S(1)}) custom-call(s32[4]{0:T(128)} %bitcast.13, bf16[4,512,512]{2,1,0:T(8,128)(2,1)} %bitcast.7, bf16[4,192,512]{2,1,0:T(8,128)(2,1)} %bitcast.9, ...), custom_call_target="tpu_custom_call" | custom-call | tf_op jit(solution)/shard_map/pallas_call | solution.py:490
  3.6 3.0 %collective-permute-start.3 = (bf16[576,128]{1,0:T(8,128)(2,1)S(1)}, bf16[576,128]{1,0:T(8,128)(2,1)S(1)}, u32[]{:S(2)}, u32[]{:S(2)}) collective-permute-start(bf16[576,128]{1,0:T(8,128)(2,1)S(1)} %get-tuple-element.28.refs_4_), channel_id=1, source_target_pairs={{0,2},{1,3},{2,0},{3,1},{4,6},{5,7},{6,4},{7,5},{8,10},{9,11},{10,... | collective-permute-start | bytes 442376 | tf_op jit(solution)/shard_map/ppermute | solution.py:38
  7.2 4.1 %collective-permute-done.3.refs_5_ = bf16[576,128]{1,0:T(8,128)(2,1)S(1)} collective-permute-done((bf16[576,128]{1,0:T(8,128)(2,1)S(1)}, bf16[576,128]{1,0:T(8,128)(2,1)S(1)}, u32[]{:S(2)}, u32[]{:S(2)}) %collective-permute-start.3) | collective-permute-done | bytes 147488 | tf_op jit(solution)/shard_map/ppermute | solution.py:38
  11.3 2.3 %collective-permute-done.refs_1_ = bf16[576,128]{1,0:T(8,128)(2,1)S(1)} collective-permute-done((bf16[576,128]{1,0:T(8,128)(2,1)S(1)}, bf16[576,128]{1,0:T(8,128)(2,1)S(1)}, u32[]{:S(2)}, u32[]{:S(2)}) %collective-permute-start) | collective-permute-done | bytes 147488 | tf_op jit(solution)/shard_map/ppermute | solution.py:38
  13.6 1.7 %collective-permute-start.7 = (bf16[6,32,128]{2,1,0:T(8,128)(2,1)S(1)}, bf16[6,32,128]{2,1,0:T(8,128)(2,1)S(1)}, u32[]{:S(2)}, u32[]{:S(2)}) collective-permute-start(bf16[6,32,128]{2,1,0:T(8,128)(2,1)S(1)} %get-tuple-element.31), channel_id=1, source_target_pairs={{0,2},{1,3},{2,0},{3,1},{4,6},{5,7},{6,4},{7,5},{8,10},{9,11},{10,... | collective-permute-start | bytes 147464 | tf_op jit(solution)/shard_map/ppermute | solution.py:38
  15.4 2.4 %collective-permute-done.7.refs_10_ = bf16[6,32,128]{2,1,0:T(8,128)(2,1)S(1)} collective-permute-done((bf16[6,32,128]{2,1,0:T(8,128)(2,1)S(1)}, bf16[6,32,128]{2,1,0:T(8,128)(2,1)S(1)}, u32[]{:S(2)}, u32[]{:S(2)}) %collective-permute-start.7) | collective-permute-done | bytes 49184 | tf_op jit(solution)/shard_map/ppermute | solution.py:38
  18.8 2.8 %collective-permute-done.8.refs_11_ = bf16[6,32,128]{2,1,0:T(8,128)(2,1)S(1)} collective-permute-done((bf16[6,32,128]{2,1,0:T(8,128)(2,1)S(1)}, bf16[6,32,128]{2,1,0:T(8,128)(2,1)S(1)}, u32[]{:S(2)}, u32[]{:S(2)}) %collective-permute-start.8) | collective-permute-done | bytes 49184 | tf_op jit(solution)/shard_map/ppermute | solution.py:38
  21.5 3.8 %shard_map.48 = (bf16[6,128,128]{2,1,0:T(8,128)(2,1)S(1)}, bf16[6,64,128]{2,1,0:T(8,128)(2,1)S(1)}, bf16[4,4,192,256]{3,2,1,0:T(8,128)(2,1)S(1)}, bf16[4,4,32,256]{3,2,1,0:T(8,128)(2,1)S(1)}) custom-call(s32[1]{0:T(128)} %bitcast.place, bf16[576,128]{1,0:T(8,128)(2,1)S(1)} %get-tuple-element.23.refs_0_, bf16[576,128]{1,0:T(8,128)(2,1)S(1)} %collective-permute-done.refs_1_, ...), custom_call_target="tpu_custom_call" | custom-call | tf_op jit(solution)/shard_map/pallas_call | solution.py:490
  25.3 2.1 %collective-permute-start.13 = (bf16[6,128,128]{2,1,0:T(8,128)(2,1)S(1)}, bf16[6,128,128]{2,1,0:T(8,128)(2,1)S(1)}, u32[]{:S(2)}, u32[]{:S(2)}) collective-permute-start(bf16[6,128,128]{2,1,0:T(8,128)(2,1)S(1)} %get-tuple-element.35.even.own), channel_id=1, source_target_pairs={{0,4},{4,0},{8,12},{12,8},{16,20},{20,16},{24,28},{28,24},{1,5},{5... | collective-permute-start | bytes 589832 | tf_op jit(solution)/shard_map/ppermute | solution.py:38
  27.4 5.2 %collective-permute-done.13.got.refs_8_ = bf16[6,128,128]{2,1,0:T(8,128)(2,1)S(1)} collective-permute-done((bf16[6,128,128]{2,1,0:T(8,128)(2,1)S(1)}, bf16[6,128,128]{2,1,0:T(8,128)(2,1)S(1)}, u32[]{:S(2)}, u32[]{:S(2)}) %collective-permute-start.13) | collective-permute-done | bytes 196640 | tf_op jit(solution)/shard_map/ppermute | solution.py:38
  32.6 1.4 %collective-permute-done.14.got_other.refs_9_ = bf16[6,128,128]{2,1,0:T(8,128)(2,1)S(1)} collective-permute-done((bf16[6,128,128]{2,1,0:T(8,128)(2,1)S(1)}, bf16[6,128,128]{2,1,0:T(8,128)(2,1)S(1)}, u32[]{:S(2)}, u32[]{:S(2)}) %collective-permute-start.14) | collective-permute-done | bytes 196640 | tf_op jit(solution)/shard_map/ppermute | solution.py:38
  34.4 1.8 %collective-permute-start.17 = (bf16[6,128,128]{2,1,0:T(8,128)(2,1)S(1)}, bf16[6,128,128]{2,1,0:T(8,128)(2,1)S(1)}, u32[]{:S(2)}, u32[]{:S(2)}) collective-permute-start(bf16[6,128,128]{2,1,0:T(8,128)(2,1)S(1)} %shard_map.51), channel_id=1, source_target_pairs={{0,8},{4,12},{8,0},{12,4},{16,24},{20,28},{24,16},{28,20},{1,9},{5... | collective-permute-start | bytes 589832 | tf_op jit(solution)/shard_map/ppermute | solution.py:38
  36.2 1.5 %collective-permute-start.10 = (bf16[6,64,128]{2,1,0:T(8,128)(2,1)S(1)}, bf16[6,64,128]{2,1,0:T(8,128)(2,1)S(1)}, u32[]{:S(2)}, u32[]{:S(2)}) collective-permute-start(bf16[6,64,128]{2,1,0:T(8,128)(2,1)S(1)} %get-tuple-element.36.own.own_offset), channel_id=1, source_target_pairs={{0,4},{4,0},{8,12},{12,8},{16,20},{20,16},{24,28},{28,24},{1,5},{5... | collective-permute-start | bytes 294920 | tf_op jit(solution)/shard_map/ppermute | solution.py:38
  37.8 3.1 %collective-permute-done.10.entry.got_offset.refs_10_ = bf16[6,64,128]{2,1,0:T(8,128)(2,1)S(1)} collective-permute-done((bf16[6,64,128]{2,1,0:T(8,128)(2,1)S(1)}, bf16[6,64,128]{2,1,0:T(8,128)(2,1)S(1)}, u32[]{:S(2)}, u32[]{:S(2)}) %collective-permute-start.10) | collective-permute-done | bytes 98336 | tf_op jit(solution)/shard_map/ppermute | solution.py:38
  41.2 1.5 %collective-permute-start.12 = (bf16[6,64,128]{2,1,0:T(8,128)(2,1)S(1)}, bf16[6,64,128]{2,1,0:T(8,128)(2,1)S(1)}, u32[]{:S(2)}, u32[]{:S(2)}) collective-permute-start(bf16[6,64,128]{2,1,0:T(8,128)(2,1)S(1)} %shard_map.49), channel_id=1, source_target_pairs={{0,12},{4,8},{8,4},{12,0},{16,28},{20,24},{24,20},{28,16},{1,13},{... | collective-permute-start | bytes 294920 | tf_op jit(solution)/shard_map/ppermute | solution.py:38
  42.7 1.6 %collective-permute-start.11 = (bf16[6,64,128]{2,1,0:T(8,128)(2,1)S(1)}, bf16[6,64,128]{2,1,0:T(8,128)(2,1)S(1)}, u32[]{:S(2)}, u32[]{:S(2)}) collective-permute-start(bf16[6,64,128]{2,1,0:T(8,128)(2,1)S(1)} %shard_map.49), channel_id=1, source_target_pairs={{0,8},{4,12},{8,0},{12,4},{16,24},{20,28},{24,16},{28,20},{1,9},{5... | collective-permute-start | bytes 294920 | tf_op jit(solution)/shard_map/ppermute | solution.py:38
  44.3 2.7 %collective-permute-done.12.across.refs_3_ = bf16[6,64,128]{2,1,0:T(8,128)(2,1)S(1)} collective-permute-done((bf16[6,64,128]{2,1,0:T(8,128)(2,1)S(1)}, bf16[6,64,128]{2,1,0:T(8,128)(2,1)S(1)}, u32[]{:S(2)}, u32[]{:S(2)}) %collective-permute-start.12) | collective-permute-done | bytes 98336 | tf_op jit(solution)/shard_map/ppermute | solution.py:38
  46.9 1.1 %collective-permute-done.11.near.refs_2_ = bf16[6,64,128]{2,1,0:T(8,128)(2,1)S(1)} collective-permute-done((bf16[6,64,128]{2,1,0:T(8,128)(2,1)S(1)}, bf16[6,64,128]{2,1,0:T(8,128)(2,1)S(1)}, u32[]{:S(2)}, u32[]{:S(2)}) %collective-permute-start.11) | collective-permute-done | bytes 98336 | tf_op jit(solution)/shard_map/ppermute | solution.py:38
  49.2 1.5 %collective-permute-start.15 = (bf16[6,64,128]{2,1,0:T(8,128)(2,1)S(1)}, bf16[6,64,128]{2,1,0:T(8,128)(2,1)S(1)}, u32[]{:S(2)}, u32[]{:S(2)}) collective-permute-start(bf16[6,64,128]{2,1,0:T(8,128)(2,1)S(1)} %shard_map.50), channel_id=1, source_target_pairs={{0,4},{4,0},{8,16},{12,20},{16,8},{20,12},{24,28},{28,24},{1,5},{5... | collective-permute-start | bytes 294920 | tf_op jit(solution)/shard_map/ppermute | solution.py:589
  50.7 2.6 %collective-permute-done.16.refs_5_ = bf16[6,64,128]{2,1,0:T(8,128)(2,1)S(1)} collective-permute-done((bf16[6,64,128]{2,1,0:T(8,128)(2,1)S(1)}, bf16[6,64,128]{2,1,0:T(8,128)(2,1)S(1)}, u32[]{:S(2)}, u32[]{:S(2)}) %collective-permute-start.16) | collective-permute-done | bytes 98336 | tf_op jit(solution)/shard_map/ppermute | solution.py:590
  54.4 3.5 %shard_map.52 = (bf16[6,32,128]{2,1,0:T(8,128)(2,1)S(1)}, bf16[6,32,128]{2,1,0:T(8,128)(2,1)S(1)}, bf16[6,32,128]{2,1,0:T(8,128)(2,1)S(1)}, bf16[6,32,128]{2,1,0:T(8,128)(2,1)S(1)}) custom-call(s32[1]{0:T(128)} %bitcast.place, s32[1]{0:T(128)} %bitcast.5.line, bf16[4,4,192,256]{3,2,1,0:T(8,128)(2,1)S(1)} %get-tuple-element.33.refs_0_, ...), custom_call_target="tpu_custom_call" | custom-call | tf_op jit(solution)/shard_map/pallas_call | solution.py:490
  58.0 1.3 %collective-permute-start.20 = (bf16[6,32,128]{2,1,0:T(8,128)(2,1)S(1)}, bf16[6,32,128]{2,1,0:T(8,128)(2,1)S(1)}, u32[]{:S(2)}, u32[]{:S(2)}) collective-permute-start(bf16[6,32,128]{2,1,0:T(8,128)(2,1)S(1)} %get-tuple-element.39), channel_id=1, source_target_pairs={{0,2},{1,3},{2,0},{3,1},{4,6},{5,7},{6,4},{7,5},{8,10},{9,11},{10,... | collective-permute-start | bytes 147464 | tf_op jit(solution)/shard_map/ppermute | solution.py:38
  59.8 2.3 %collective-permute-done.20.refs_2_ = bf16[6,32,128]{2,1,0:T(8,128)(2,1)S(1)} collective-permute-done((bf16[6,32,128]{2,1,0:T(8,128)(2,1)S(1)}, bf16[6,32,128]{2,1,0:T(8,128)(2,1)S(1)}, u32[]{:S(2)}, u32[]{:S(2)}) %collective-permute-start.20) | collective-permute-done | bytes 49184 | tf_op jit(solution)/shard_map/ppermute | solution.py:38
  62.9 2.5 %shard_map.53 = bf16[4,512,128]{2,1,0:T(8,128)(2,1)} custom-call(s32[1]{0:T(128)} %bitcast.place, s32[4]{0:T(128)S(1)} %bitcast.14, bf16[4,512,512]{2,1,0:T(8,128)(2,1)S(1)} %bitcast.8, bf16[4,192,512]{2,1,0:T(8,128)(2,1)S(1)} %bitcast.10, bf16[4,512,128]{2,1,0:T(8,128)(2,1)S(1)} %bitcast.12, bf16[6,32,128]{2,1,0:T(8,128)(2,1)S(1)} %get-tuple-element.37.refs_0_, ...), custom_call_target="tpu_custom_call" | custom-call | tf_op jit(solution)/shard_map/pallas_call | solution.py:490
  (36 shorter events, 6.6 us)
Async XLA Ops:
  3.6 7.7 %collective-permute-start.3 = (bf16[576,128]{1,0:T(8,128)(2,1)S(1)}, bf16[576,128]{1,0:T(8,128)(2,1)S(1)}, u32[]{:S(2)}, u32[]{:S(2)}) collective-permute-start(bf16[576,128]{1,0:T(8,128)(2,1)S(1)} %get-tuple-element.28.refs_4_), channel_id=1, source_target_pairs={{0,2},{1,3},{2,0},{3,1},{4,6},{5,7},{6,4},{7,5},{8,10},{9,11},{10,... | collective-permute-start | bytes 442376 | tf_op jit(solution)/shard_map/ppermute | solution.py:38
  6.6 7.0 %collective-permute-start = (bf16[576,128]{1,0:T(8,128)(2,1)S(1)}, bf16[576,128]{1,0:T(8,128)(2,1)S(1)}, u32[]{:S(2)}, u32[]{:S(2)}) collective-permute-start(bf16[576,128]{1,0:T(8,128)(2,1)S(1)} %get-tuple-element.23.refs_0_), channel_id=1, source_target_pairs={{0,2},{1,3},{2,0},{3,1},{4,6},{5,7},{6,4},{7,5},{8,10},{9,11},{10,... | collective-permute-start | bytes 442376 | tf_op jit(solution)/shard_map/ppermute | solution.py:38
  6.7 6.9 %collective-permute-start.6 = (bf16[6,32,128]{2,1,0:T(8,128)(2,1)S(1)}, bf16[6,32,128]{2,1,0:T(8,128)(2,1)S(1)}, u32[]{:S(2)}, u32[]{:S(2)}) collective-permute-start(bf16[6,32,128]{2,1,0:T(8,128)(2,1)S(1)} %get-tuple-element.30), channel_id=1, source_target_pairs={{0,1},{1,0},{2,3},{3,2},{4,5},{5,4},{6,7},{7,6},{8,9},{9,8},{10,11... | collective-permute-start | bytes 147464 | tf_op jit(solution)/shard_map/ppermute | solution.py:38
  6.7 14.8 %collective-permute-start.4 = (bf16[576,128]{1,0:T(8,128)(2,1)S(1)}, bf16[576,128]{1,0:T(8,128)(2,1)S(1)}, u32[]{:S(2)}, u32[]{:S(2)}) collective-permute-start(bf16[576,128]{1,0:T(8,128)(2,1)S(1)} %get-tuple-element.28.refs_4_), channel_id=1, source_target_pairs={{0,1},{1,0},{2,3},{3,2},{4,5},{5,4},{6,7},{7,6},{8,9},{9,8},{10,11... | collective-permute-start | bytes 442376 | tf_op jit(solution)/shard_map/ppermute | solution.py:38
  7.2 14.3 %collective-permute-start.1 = (bf16[576,128]{1,0:T(8,128)(2,1)S(1)}, bf16[576,128]{1,0:T(8,128)(2,1)S(1)}, u32[]{:S(2)}, u32[]{:S(2)}) collective-permute-start(bf16[576,128]{1,0:T(8,128)(2,1)S(1)} %get-tuple-element.23.refs_0_), channel_id=1, source_target_pairs={{0,1},{1,0},{2,3},{3,2},{4,5},{5,4},{6,7},{7,6},{8,9},{9,8},{10,11... | collective-permute-start | bytes 442376 | tf_op jit(solution)/shard_map/ppermute | solution.py:38
  11.3 10.2 %collective-permute-start.5 = (bf16[576,128]{1,0:T(8,128)(2,1)S(1)}, bf16[576,128]{1,0:T(8,128)(2,1)S(1)}, u32[]{:S(2)}, u32[]{:S(2)}) collective-permute-start(bf16[576,128]{1,0:T(8,128)(2,1)S(1)} %collective-permute-done.3.refs_5_), channel_id=1, source_target_pairs={{0,1},{1,0},{2,3},{3,2},{4,5},{5,4},{6,7},{7,6},{8,9},{9,8},{10,11... | collective-permute-start | bytes 442376 | tf_op jit(solution)/shard_map/ppermute | solution.py:38
  13.6 7.9 %collective-permute-start.2 = (bf16[576,128]{1,0:T(8,128)(2,1)S(1)}, bf16[576,128]{1,0:T(8,128)(2,1)S(1)}, u32[]{:S(2)}, u32[]{:S(2)}) collective-permute-start(bf16[576,128]{1,0:T(8,128)(2,1)S(1)} %collective-permute-done.refs_1_), channel_id=1, source_target_pairs={{0,1},{1,0},{2,3},{3,2},{4,5},{5,4},{6,7},{7,6},{8,9},{9,8},{10,11... | collective-permute-start | bytes 442376 | tf_op jit(solution)/shard_map/ppermute | solution.py:38
  13.6 4.2 %collective-permute-start.7 = (bf16[6,32,128]{2,1,0:T(8,128)(2,1)S(1)}, bf16[6,32,128]{2,1,0:T(8,128)(2,1)S(1)}, u32[]{:S(2)}, u32[]{:S(2)}) collective-permute-start(bf16[6,32,128]{2,1,0:T(8,128)(2,1)S(1)} %get-tuple-element.31), channel_id=1, source_target_pairs={{0,2},{1,3},{2,0},{3,1},{4,6},{5,7},{6,4},{7,5},{8,10},{9,11},{10,... | collective-permute-start | bytes 147464 | tf_op jit(solution)/shard_map/ppermute | solution.py:38
  17.8 3.7 %collective-permute-start.8 = (bf16[6,32,128]{2,1,0:T(8,128)(2,1)S(1)}, bf16[6,32,128]{2,1,0:T(8,128)(2,1)S(1)}, u32[]{:S(2)}, u32[]{:S(2)}) collective-permute-start(bf16[6,32,128]{2,1,0:T(8,128)(2,1)S(1)} %get-tuple-element.32), channel_id=1, source_target_pairs={{0,3},{1,2},{2,1},{3,0},{4,7},{5,6},{6,5},{7,4},{8,11},{9,10},{10,... | collective-permute-start | bytes 147464 | tf_op jit(solution)/shard_map/ppermute | solution.py:38
  25.3 7.3 %collective-permute-start.13 = (bf16[6,128,128]{2,1,0:T(8,128)(2,1)S(1)}, bf16[6,128,128]{2,1,0:T(8,128)(2,1)S(1)}, u32[]{:S(2)}, u32[]{:S(2)}) collective-permute-start(bf16[6,128,128]{2,1,0:T(8,128)(2,1)S(1)} %get-tuple-element.35.even.own), channel_id=1, source_target_pairs={{0,4},{4,0},{8,12},{12,8},{16,20},{20,16},{24,28},{28,24},{1,5},{5... | collective-permute-start | bytes 589832 | tf_op jit(solution)/shard_map/ppermute | solution.py:38
  27.4 5.2 %collective-permute-start.9 = (bf16[6,128,128]{2,1,0:T(8,128)(2,1)S(1)}, bf16[6,128,128]{2,1,0:T(8,128)(2,1)S(1)}, u32[]{:S(2)}, u32[]{:S(2)}) collective-permute-start(bf16[6,128,128]{2,1,0:T(8,128)(2,1)S(1)} %get-tuple-element.35.even.own), channel_id=1, source_target_pairs={{0,1},{1,0},{2,3},{3,2},{4,5},{5,4},{6,7},{7,6},{8,9},{9,8},{10,11... | collective-permute-start | bytes 589832 | tf_op jit(solution)/shard_map/ppermute | solution.py:38
  32.6 1.4 %collective-permute-start.14 = (bf16[6,128,128]{2,1,0:T(8,128)(2,1)S(1)}, bf16[6,128,128]{2,1,0:T(8,128)(2,1)S(1)}, u32[]{:S(2)}, u32[]{:S(2)}) collective-permute-start(bf16[6,128,128]{2,1,0:T(8,128)(2,1)S(1)} %collective-permute-done.13.got.refs_8_), channel_id=1, source_target_pairs={{0,1},{1,0},{2,3},{3,2},{4,5},{5,4},{6,7},{7,6},{8,9},{9,8},{10,11... | collective-permute-start | bytes 589832 | tf_op jit(solution)/shard_map/ppermute | solution.py:38
  34.4 9.9 %collective-permute-start.17 = (bf16[6,128,128]{2,1,0:T(8,128)(2,1)S(1)}, bf16[6,128,128]{2,1,0:T(8,128)(2,1)S(1)}, u32[]{:S(2)}, u32[]{:S(2)}) collective-permute-start(bf16[6,128,128]{2,1,0:T(8,128)(2,1)S(1)} %shard_map.51), channel_id=1, source_target_pairs={{0,8},{4,12},{8,0},{12,4},{16,24},{20,28},{24,16},{28,20},{1,9},{5... | collective-permute-start | bytes 589832 | tf_op jit(solution)/shard_map/ppermute | solution.py:38
  36.2 4.6 %collective-permute-start.10 = (bf16[6,64,128]{2,1,0:T(8,128)(2,1)S(1)}, bf16[6,64,128]{2,1,0:T(8,128)(2,1)S(1)}, u32[]{:S(2)}, u32[]{:S(2)}) collective-permute-start(bf16[6,64,128]{2,1,0:T(8,128)(2,1)S(1)} %get-tuple-element.36.own.own_offset), channel_id=1, source_target_pairs={{0,4},{4,0},{8,12},{12,8},{16,20},{20,16},{24,28},{28,24},{1,5},{5... | collective-permute-start | bytes 294920 | tf_op jit(solution)/shard_map/ppermute | solution.py:38
  41.2 21.8 %copy-start = (bf16[1,1,4,512,512]{4,3,2,1,0:T(8,128)(2,1)S(1)}, bf16[1,1,4,512,512]{4,3,2,1,0:T(8,128)(2,1)}, u32[]{:S(2)}) copy-start(bf16[1,1,4,512,512]{4,3,2,1,0:T(8,128)(2,1)} %param.5) | copy-start | bytes 6291460
  41.2 21.7 %copy-start.1 = (bf16[1,1,4,3,64,512]{5,4,3,2,1,0:T(8,128)(2,1)S(1)}, bf16[1,1,4,3,64,512]{5,4,3,2,1,0:T(8,128)(2,1)}, u32[]{:S(2)}) copy-start(bf16[1,1,4,3,64,512]{5,4,3,2,1,0:T(8,128)(2,1)} %param.6) | copy-start | bytes 2359300
  41.2 5.7 %collective-permute-start.12 = (bf16[6,64,128]{2,1,0:T(8,128)(2,1)S(1)}, bf16[6,64,128]{2,1,0:T(8,128)(2,1)S(1)}, u32[]{:S(2)}, u32[]{:S(2)}) collective-permute-start(bf16[6,64,128]{2,1,0:T(8,128)(2,1)S(1)} %shard_map.49), channel_id=1, source_target_pairs={{0,12},{4,8},{8,4},{12,0},{16,28},{20,24},{24,20},{28,16},{1,13},{... | collective-permute-start | bytes 294920 | tf_op jit(solution)/shard_map/ppermute | solution.py:38
  42.7 5.4 %collective-permute-start.11 = (bf16[6,64,128]{2,1,0:T(8,128)(2,1)S(1)}, bf16[6,64,128]{2,1,0:T(8,128)(2,1)S(1)}, u32[]{:S(2)}, u32[]{:S(2)}) collective-permute-start(bf16[6,64,128]{2,1,0:T(8,128)(2,1)S(1)} %shard_map.49), channel_id=1, source_target_pairs={{0,8},{4,12},{8,0},{12,4},{16,24},{20,28},{24,16},{28,20},{1,9},{5... | collective-permute-start | bytes 294920 | tf_op jit(solution)/shard_map/ppermute | solution.py:38
  44.3 10.1 %collective-permute-start.18 = (bf16[6,128,128]{2,1,0:T(8,128)(2,1)S(1)}, bf16[6,128,128]{2,1,0:T(8,128)(2,1)S(1)}, u32[]{:S(2)}, u32[]{:S(2)}) collective-permute-start(bf16[6,128,128]{2,1,0:T(8,128)(2,1)S(1)} %collective-permute-done.17.refs_6_), channel_id=1, source_target_pairs={{0,1},{1,0},{2,3},{3,2},{4,5},{5,4},{6,7},{7,6},{8,9},{9,8},{10,11... | collective-permute-start | bytes 589832 | tf_op jit(solution)/shard_map/ppermute | solution.py:38
  48.6 4.7 %collective-permute-start.16 = (bf16[6,64,128]{2,1,0:T(8,128)(2,1)S(1)}, bf16[6,64,128]{2,1,0:T(8,128)(2,1)S(1)}, u32[]{:S(2)}, u32[]{:S(2)}) collective-permute-start(bf16[6,64,128]{2,1,0:T(8,128)(2,1)S(1)} %shard_map.50), channel_id=1, source_target_pairs={{0,4},{4,0},{8,24},{12,28},{16,20},{20,16},{24,8},{28,12},{1,5},{5... | collective-permute-start | bytes 294920 | tf_op jit(solution)/shard_map/ppermute | solution.py:590
  49.2 5.2 %collective-permute-start.15 = (bf16[6,64,128]{2,1,0:T(8,128)(2,1)S(1)}, bf16[6,64,128]{2,1,0:T(8,128)(2,1)S(1)}, u32[]{:S(2)}, u32[]{:S(2)}) collective-permute-start(bf16[6,64,128]{2,1,0:T(8,128)(2,1)S(1)} %shard_map.50), channel_id=1, source_target_pairs={{0,4},{4,0},{8,16},{12,20},{16,8},{20,12},{24,28},{28,24},{1,5},{5... | collective-permute-start | bytes 294920 | tf_op jit(solution)/shard_map/ppermute | solution.py:589
  57.9 1.9 %collective-permute-start.19 = (bf16[6,32,128]{2,1,0:T(8,128)(2,1)S(1)}, bf16[6,32,128]{2,1,0:T(8,128)(2,1)S(1)}, u32[]{:S(2)}, u32[]{:S(2)}) collective-permute-start(bf16[6,32,128]{2,1,0:T(8,128)(2,1)S(1)} %get-tuple-element.38), channel_id=1, source_target_pairs={{0,1},{1,0},{2,3},{3,2},{4,5},{5,4},{6,7},{7,6},{8,9},{9,8},{10,11... | collective-permute-start | bytes 147464 | tf_op jit(solution)/shard_map/ppermute | solution.py:38
  58.0 4.2 %collective-permute-start.20 = (bf16[6,32,128]{2,1,0:T(8,128)(2,1)S(1)}, bf16[6,32,128]{2,1,0:T(8,128)(2,1)S(1)}, u32[]{:S(2)}, u32[]{:S(2)}) collective-permute-start(bf16[6,32,128]{2,1,0:T(8,128)(2,1)S(1)} %get-tuple-element.39), channel_id=1, source_target_pairs={{0,2},{1,3},{2,0},{3,1},{4,6},{5,7},{6,4},{7,5},{8,10},{9,11},{10,... | collective-permute-start | bytes 147464 | tf_op jit(solution)/shard_map/ppermute | solution.py:38
  59.2 3.7 %collective-permute-start.21 = (bf16[6,32,128]{2,1,0:T(8,128)(2,1)S(1)}, bf16[6,32,128]{2,1,0:T(8,128)(2,1)S(1)}, u32[]{:S(2)}, u32[]{:S(2)}) collective-permute-start(bf16[6,32,128]{2,1,0:T(8,128)(2,1)S(1)} %get-tuple-element.40), channel_id=1, source_target_pairs={{0,3},{1,2},{2,1},{3,0},{4,7},{5,6},{6,5},{7,4},{8,11},{9,10},{10,... | collective-permute-start | bytes 147464 | tf_op jit(solution)/shard_map/ppermute | solution.py:38
  (2 other events, 43.5 us)

commit v7 on v6

--- a/solution.py
+++ b/solution.py
@@ -91,8 +91,8 @@
 
 
 def first_kernel(order_far, inverse_far, coupling_far, given_far, *refs):
-    maps, rows, inverse_near, coupling_near, given_near = refs[:5]
-    inverse, coupling, order, order_done, done, near_done = refs[5:]
+    maps, rows, coupling_near, given_near = refs[:4]
+    inverse, coupling, order, order_done, done, near_done = refs[4:]
     count = given_near.shape[0]
     face = coupling.shape[1] // 3
     first = pltpu.make_async_copy(order_far, order, order_done)
@@ -106,26 +106,24 @@
     first.wait()
     slots = [order[p] for p in range(count)]
     later = [
-        pltpu.make_async_copy(given_far.at[slots[p]], given_near.at[p], near_done.at[0, p]) for p in range(count)
+        pltpu.make_async_copy(given_far.at[slots[p]], given_near.at[p], near_done.at[p]) for p in range(count)
     ]
     for copy in later:
         copy.start()
     for copy in copies:
         copy.wait()
+    values = [face_rows_of(inverse, slots[p], face) for p in range(2)]
+    pair_maps(maps, coupling, slots[:2], values, face)
     for p in range(2, count):
-        for kind, (held, near) in enumerate(((inverse, inverse_near), (coupling, coupling_near))):
-            later.append(pltpu.make_async_copy(held.at[slots[p]], near.at[p - 2], near_done.at[kind + 1, p]))
-            later[-1].start()
-    values = []
-    for p in range(2):
         values.append(face_rows_of(inverse, slots[p], face))
+        coupling_near[p - 2] = coupling[slots[p]]
+    for p in range(count):
         rows[p] = values[p]
-    pair_maps(maps, coupling, slots[:2], values, face)
     for copy in later:
         copy.wait()
 
 
-def rest_kernel(place, early_rows, inverse, coupling, given, *refs):
+def rest_kernel(place, rows, coupling, given, *refs):
     count, _, width = given.shape
     maps = refs[: count // 2 - 1]
     gains = refs[count // 2 - 1 : -1]
@@ -133,10 +131,9 @@
     face = coupling.shape[1] // 3
     groups = len(gains)
     share = width // groups
-    rows = [face_rows_of(inverse, p, face) for p in range(count - 2)]
+    rows = [rows[p] for p in range(count)]
     for j, target in enumerate(maps):
-        pair_maps(target, coupling, (2 * j, 2 * j + 1), rows[2 * j : 2 * j + 2], face)
-    rows = [early_rows[0], early_rows[1]] + rows
+        pair_maps(target, coupling, (2 * j, 2 * j + 1), rows[2 * j + 2 : 2 * j + 4], face)
     every = [dot(rows[p], given[p]).T for p in range(count)]
     tiles = [gain[:, : 2 * face] for gain in every]
     for p in range(0, count, 2):
@@ -209,13 +206,16 @@
     for p in range(count):
         for i, pos in enumerate(chosen):
             rows = entries[i].shape[0]
-            left = entries[i]
-            own = weights[pos, p, 2 * face :]
-            right = jnp.concatenate([own, own], axis=0)
-            if not first:
-                left = jnp.concatenate([lags[pos, p, :rows], left], axis=1)
-                right = jnp.concatenate([weights[pos, p, : 2 * face], right], axis=0)
-            result = dot(left, right)
+            if p == 0 and not first:
+                result = dot(lags[pos, p, :rows], weights[pos, p, : 2 * face])
+            else:
+                left = entries[i]
+                own = weights[pos, p, 2 * face :]
+                right = jnp.concatenate([own, own], axis=0)
+                if not first:
+                    left = jnp.concatenate([lags[pos, p, :rows], left], axis=1)
+                    right = jnp.concatenate([weights[pos, p, : 2 * face], right], axis=0)
+                result = dot(left, right)
             head = result[:share] + gains[pos, p].astype(F32)
             result = head if rows == share else jnp.concatenate([head, result[share:]], axis=0)
             states[pos, p, :rows] = result[:, : 2 * face].astype(BF16)
@@ -517,8 +517,7 @@
         first_kernel,
         [
             shape((3 * 3 * face, 2 * face), BF16),
-            shape((2, 4 * face, nodes), BF16),
-            shape((count - 2,) + inverse.shape[1:], BF16),
+            shape((count, 4 * face, nodes), BF16),
             shape((count - 2,) + coupling.shape[1:], BF16),
             shape(given.shape, BF16),
         ],
@@ -530,7 +529,7 @@
             pltpu.SMEM(order.shape, order.dtype),
             pltpu.SemaphoreType.DMA,
             pltpu.SemaphoreType.DMA((2, count)),
-            pltpu.SemaphoreType.DMA((3, count)),
+            pltpu.SemaphoreType.DMA((count,)),
         ),
     )
     all_maps = gather_list(maps, "span")

time: 65.6 us -> 65 us (level)
  no operation moved by 1% of the time
where the time goes in v7:
time: 65 us; the launch traced here: 64.8 us
  waiting for transfers between devices  31.8 us (49%)
  starting transfers between devices  18.9 us (29%)
  Pallas kernels  14 us (22%)
    ppermute x20, waiting for transfers between devices, swap(): return lax.ppermute(value, axis, [(i, i ^ mask) for i in range(count)])  28.1 us
    ppermute x20, starting transfers between devices, swap(): return lax.ppermute(value, axis, [(i, i ^ mask) for i in range(count)])  16.8 us
    pallas_call x8, Pallas kernels, call(): pl.pallas_call(kernel, out_shape=outs, in_specs=[SMEM] * len(scalars) + [...  14 us
    ppermute x1, waiting for transfers between devices, shards(): third = lax.ppermute(joined, 'stream', crossing(masks, 1, 3))  2.59 us
    ppermute x1, starting transfers between devices, shards(): second = lax.ppermute(joined, 'stream', crossing(masks, 1, 2))  1.53 us
  transfers between devices with their start and end apart: 22, of which 13 were waited for; matrix products, arithmetic and copies ran while one was open for 0% of the time, Pallas kernels for 1%

profile of v7, /device:TPU:0, one launch (start us, length us, event | category | flops | bytes accessed | tf_op | source)
XLA Modules:
  0.0 64.8 jit_solution(15366701558363854758)
XLA Ops:
  0.0 2.3 %shard_map.46 = (bf16[576,128]{1,0:T(8,128)(2,1)S(1)}, bf16[4,256,512]{2,1,0:T(8,128)(2,1)S(1)}, bf16[2,192,512]{2,1,0:T(8,128)(2,1)S(1)}, bf16[4,512,128]{2,1,0:T(8,128)(2,1)S(1)}) custom-call(s32[4]{0:T(128)} %bitcast.13, bf16[4,512,512]{2,1,0:T(8,128)(2,1)} %bitcast.7, bf16[4,192,512]{2,1,0:T(8,128)(2,1)} %bitcast.9, bf16[4,512,128]{2,1,0:T(8,128)(2,1)} %bitcast.11), custom_call_target="tpu_custom_call" | custom-call | tf_op jit(solution)/shard_map/pallas_call | solution.py:490
  3.0 3.0 %collective-permute-start.3 = (bf16[576,128]{1,0:T(8,128)(2,1)S(1)}, bf16[576,128]{1,0:T(8,128)(2,1)S(1)}, u32[]{:S(2)}, u32[]{:S(2)}) collective-permute-start(bf16[576,128]{1,0:T(8,128)(2,1)S(1)} %get-tuple-element.26.refs_4_), channel_id=1, source_target_pairs={{0,2},{1,3},{2,0},{3,1},{4,6},{5,7},{6,4},{7,5},{8,10},{9,11},{10,... | collective-permute-start | bytes 442376 | tf_op jit(solution)/shard_map/ppermute | solution.py:38
  6.6 4.1 %collective-permute-done.3.refs_5_ = bf16[576,128]{1,0:T(8,128)(2,1)S(1)} collective-permute-done((bf16[576,128]{1,0:T(8,128)(2,1)S(1)}, bf16[576,128]{1,0:T(8,128)(2,1)S(1)}, u32[]{:S(2)}, u32[]{:S(2)}) %collective-permute-start.3) | collective-permute-done | bytes 147488 | tf_op jit(solution)/shard_map/ppermute | solution.py:38
  10.7 2.3 %collective-permute-done.refs_1_ = bf16[576,128]{1,0:T(8,128)(2,1)S(1)} collective-permute-done((bf16[576,128]{1,0:T(8,128)(2,1)S(1)}, bf16[576,128]{1,0:T(8,128)(2,1)S(1)}, u32[]{:S(2)}, u32[]{:S(2)}) %collective-permute-start) | collective-permute-done | bytes 147488 | tf_op jit(solution)/shard_map/ppermute | solution.py:38
  13.0 1.7 %collective-permute-start.7 = (bf16[6,32,128]{2,1,0:T(8,128)(2,1)S(1)}, bf16[6,32,128]{2,1,0:T(8,128)(2,1)S(1)}, u32[]{:S(2)}, u32[]{:S(2)}) collective-permute-start(bf16[6,32,128]{2,1,0:T(8,128)(2,1)S(1)} %get-tuple-element.29), channel_id=1, source_target_pairs={{0,2},{1,3},{2,0},{3,1},{4,6},{5,7},{6,4},{7,5},{8,10},{9,11},{10,... | collective-permute-start | bytes 147464 | tf_op jit(solution)/shard_map/ppermute | solution.py:38
  14.8 2.4 %collective-permute-done.7.refs_10_ = bf16[6,32,128]{2,1,0:T(8,128)(2,1)S(1)} collective-permute-done((bf16[6,32,128]{2,1,0:T(8,128)(2,1)S(1)}, bf16[6,32,128]{2,1,0:T(8,128)(2,1)S(1)}, u32[]{:S(2)}, u32[]{:S(2)}) %collective-permute-start.7) | collective-permute-done | bytes 49184 | tf_op jit(solution)/shard_map/ppermute | solution.py:38
  18.2 2.8 %collective-permute-done.8.refs_11_ = bf16[6,32,128]{2,1,0:T(8,128)(2,1)S(1)} collective-permute-done((bf16[6,32,128]{2,1,0:T(8,128)(2,1)S(1)}, bf16[6,32,128]{2,1,0:T(8,128)(2,1)S(1)}, u32[]{:S(2)}, u32[]{:S(2)}) %collective-permute-start.8) | collective-permute-done | bytes 49184 | tf_op jit(solution)/shard_map/ppermute | solution.py:38
  20.9 3.7 %shard_map.48 = (bf16[6,128,128]{2,1,0:T(8,128)(2,1)S(1)}, bf16[6,64,128]{2,1,0:T(8,128)(2,1)S(1)}, bf16[4,4,192,256]{3,2,1,0:T(8,128)(2,1)S(1)}, bf16[4,4,32,256]{3,2,1,0:T(8,128)(2,1)S(1)}) custom-call(s32[1]{0:T(128)} %bitcast.place, bf16[576,128]{1,0:T(8,128)(2,1)S(1)} %get-tuple-element.22.refs_0_, bf16[576,128]{1,0:T(8,128)(2,1)S(1)} %collective-permute-done.refs_1_, ...), custom_call_target="tpu_custom_call" | custom-call | tf_op jit(solution)/shard_map/pallas_call | solution.py:490
  24.7 2.1 %collective-permute-start.13 = (bf16[6,128,128]{2,1,0:T(8,128)(2,1)S(1)}, bf16[6,128,128]{2,1,0:T(8,128)(2,1)S(1)}, u32[]{:S(2)}, u32[]{:S(2)}) collective-permute-start(bf16[6,128,128]{2,1,0:T(8,128)(2,1)S(1)} %get-tuple-element.33.even.own), channel_id=1, source_target_pairs={{0,4},{4,0},{8,12},{12,8},{16,20},{20,16},{24,28},{28,24},{1,5},{5... | collective-permute-start | bytes 589832 | tf_op jit(solution)/shard_map/ppermute | solution.py:38
  26.8 5.2 %collective-permute-done.13.got.refs_8_ = bf16[6,128,128]{2,1,0:T(8,128)(2,1)S(1)} collective-permute-done((bf16[6,128,128]{2,1,0:T(8,128)(2,1)S(1)}, bf16[6,128,128]{2,1,0:T(8,128)(2,1)S(1)}, u32[]{:S(2)}, u32[]{:S(2)}) %collective-permute-start.13) | collective-permute-done | bytes 196640 | tf_op jit(solution)/shard_map/ppermute | solution.py:38
  32.0 1.4 %collective-permute-done.14.got_other.refs_9_ = bf16[6,128,128]{2,1,0:T(8,128)(2,1)S(1)} collective-permute-done((bf16[6,128,128]{2,1,0:T(8,128)(2,1)S(1)}, bf16[6,128,128]{2,1,0:T(8,128)(2,1)S(1)}, u32[]{:S(2)}, u32[]{:S(2)}) %collective-permute-start.14) | collective-permute-done | bytes 196640 | tf_op jit(solution)/shard_map/ppermute | solution.py:38
  33.8 1.9 %collective-permute-start.17 = (bf16[6,128,128]{2,1,0:T(8,128)(2,1)S(1)}, bf16[6,128,128]{2,1,0:T(8,128)(2,1)S(1)}, u32[]{:S(2)}, u32[]{:S(2)}) collective-permute-start(bf16[6,128,128]{2,1,0:T(8,128)(2,1)S(1)} %shard_map.51), channel_id=1, source_target_pairs={{0,8},{4,12},{8,0},{12,4},{16,24},{20,28},{24,16},{28,20},{1,9},{5... | collective-permute-start | bytes 589832 | tf_op jit(solution)/shard_map/ppermute | solution.py:38
  35.6 1.5 %collective-permute-start.10 = (bf16[6,64,128]{2,1,0:T(8,128)(2,1)S(1)}, bf16[6,64,128]{2,1,0:T(8,128)(2,1)S(1)}, u32[]{:S(2)}, u32[]{:S(2)}) collective-permute-start(bf16[6,64,128]{2,1,0:T(8,128)(2,1)S(1)} %get-tuple-element.34.own.own_offset), channel_id=1, source_target_pairs={{0,4},{4,0},{8,12},{12,8},{16,20},{20,16},{24,28},{28,24},{1,5},{5... | collective-permute-start | bytes 294920 | tf_op jit(solution)/shard_map/ppermute | solution.py:38
  37.2 3.1 %collective-permute-done.10.entry.got_offset.refs_10_ = bf16[6,64,128]{2,1,0:T(8,128)(2,1)S(1)} collective-permute-done((bf16[6,64,128]{2,1,0:T(8,128)(2,1)S(1)}, bf16[6,64,128]{2,1,0:T(8,128)(2,1)S(1)}, u32[]{:S(2)}, u32[]{:S(2)}) %collective-permute-start.10) | collective-permute-done | bytes 98336 | tf_op jit(solution)/shard_map/ppermute | solution.py:38
  40.6 1.5 %collective-permute-start.12 = (bf16[6,64,128]{2,1,0:T(8,128)(2,1)S(1)}, bf16[6,64,128]{2,1,0:T(8,128)(2,1)S(1)}, u32[]{:S(2)}, u32[]{:S(2)}) collective-permute-start(bf16[6,64,128]{2,1,0:T(8,128)(2,1)S(1)} %shard_map.49), channel_id=1, source_target_pairs={{0,12},{4,8},{8,4},{12,0},{16,28},{20,24},{24,20},{28,16},{1,13},{... | collective-permute-start | bytes 294920 | tf_op jit(solution)/shard_map/ppermute | solution.py:38
  42.1 1.6 %collective-permute-start.11 = (bf16[6,64,128]{2,1,0:T(8,128)(2,1)S(1)}, bf16[6,64,128]{2,1,0:T(8,128)(2,1)S(1)}, u32[]{:S(2)}, u32[]{:S(2)}) collective-permute-start(bf16[6,64,128]{2,1,0:T(8,128)(2,1)S(1)} %shard_map.49), channel_id=1, source_target_pairs={{0,8},{4,12},{8,0},{12,4},{16,24},{20,28},{24,16},{28,20},{1,9},{5... | collective-permute-start | bytes 294920 | tf_op jit(solution)/shard_map/ppermute | solution.py:38
  43.7 2.7 %collective-permute-done.12.across.refs_3_ = bf16[6,64,128]{2,1,0:T(8,128)(2,1)S(1)} collective-permute-done((bf16[6,64,128]{2,1,0:T(8,128)(2,1)S(1)}, bf16[6,64,128]{2,1,0:T(8,128)(2,1)S(1)}, u32[]{:S(2)}, u32[]{:S(2)}) %collective-permute-start.12) | collective-permute-done | bytes 98336 | tf_op jit(solution)/shard_map/ppermute | solution.py:38
  46.3 1.1 %collective-permute-done.11.near.refs_2_ = bf16[6,64,128]{2,1,0:T(8,128)(2,1)S(1)} collective-permute-done((bf16[6,64,128]{2,1,0:T(8,128)(2,1)S(1)}, bf16[6,64,128]{2,1,0:T(8,128)(2,1)S(1)}, u32[]{:S(2)}, u32[]{:S(2)}) %collective-permute-start.11) | collective-permute-done | bytes 98336 | tf_op jit(solution)/shard_map/ppermute | solution.py:38
  48.6 1.5 %collective-permute-start.15 = (bf16[6,64,128]{2,1,0:T(8,128)(2,1)S(1)}, bf16[6,64,128]{2,1,0:T(8,128)(2,1)S(1)}, u32[]{:S(2)}, u32[]{:S(2)}) collective-permute-start(bf16[6,64,128]{2,1,0:T(8,128)(2,1)S(1)} %shard_map.50), channel_id=1, source_target_pairs={{0,4},{4,0},{8,16},{12,20},{16,8},{20,12},{24,28},{28,24},{1,5},{5... | collective-permute-start | bytes 294920 | tf_op jit(solution)/shard_map/ppermute | solution.py:588
  50.1 2.6 %collective-permute-done.16.refs_5_ = bf16[6,64,128]{2,1,0:T(8,128)(2,1)S(1)} collective-permute-done((bf16[6,64,128]{2,1,0:T(8,128)(2,1)S(1)}, bf16[6,64,128]{2,1,0:T(8,128)(2,1)S(1)}, u32[]{:S(2)}, u32[]{:S(2)}) %collective-permute-start.16) | collective-permute-done | bytes 98336 | tf_op jit(solution)/shard_map/ppermute | solution.py:589
  53.7 3.5 %shard_map.52 = (bf16[6,32,128]{2,1,0:T(8,128)(2,1)S(1)}, bf16[6,32,128]{2,1,0:T(8,128)(2,1)S(1)}, bf16[6,32,128]{2,1,0:T(8,128)(2,1)S(1)}, bf16[6,32,128]{2,1,0:T(8,128)(2,1)S(1)}) custom-call(s32[1]{0:T(128)} %bitcast.place, s32[1]{0:T(128)} %bitcast.5.line, bf16[4,4,192,256]{3,2,1,0:T(8,128)(2,1)S(1)} %get-tuple-element.31.refs_0_, ...), custom_call_target="tpu_custom_call" | custom-call | tf_op jit(solution)/shard_map/pallas_call | solution.py:490
  57.3 1.2 %collective-permute-start.20 = (bf16[6,32,128]{2,1,0:T(8,128)(2,1)S(1)}, bf16[6,32,128]{2,1,0:T(8,128)(2,1)S(1)}, u32[]{:S(2)}, u32[]{:S(2)}) collective-permute-start(bf16[6,32,128]{2,1,0:T(8,128)(2,1)S(1)} %get-tuple-element.37), channel_id=1, source_target_pairs={{0,2},{1,3},{2,0},{3,1},{4,6},{5,7},{6,4},{7,5},{8,10},{9,11},{10,... | collective-permute-start | bytes 147464 | tf_op jit(solution)/shard_map/ppermute | solution.py:38
  59.2 2.3 %collective-permute-done.20.refs_2_ = bf16[6,32,128]{2,1,0:T(8,128)(2,1)S(1)} collective-permute-done((bf16[6,32,128]{2,1,0:T(8,128)(2,1)S(1)}, bf16[6,32,128]{2,1,0:T(8,128)(2,1)S(1)}, u32[]{:S(2)}, u32[]{:S(2)}) %collective-permute-start.20) | collective-permute-done | bytes 49184 | tf_op jit(solution)/shard_map/ppermute | solution.py:38
  62.3 2.5 %shard_map.53 = bf16[4,512,128]{2,1,0:T(8,128)(2,1)} custom-call(s32[1]{0:T(128)} %bitcast.place, s32[4]{0:T(128)S(1)} %bitcast.14, bf16[4,512,512]{2,1,0:T(8,128)(2,1)S(1)} %bitcast.8, bf16[4,192,512]{2,1,0:T(8,128)(2,1)S(1)} %bitcast.10, bf16[4,512,128]{2,1,0:T(8,128)(2,1)S(1)} %bitcast.12, bf16[6,32,128]{2,1,0:T(8,128)(2,1)S(1)} %get-tuple-element.35.refs_0_, ...), custom_call_target="tpu_custom_call" | custom-call | tf_op jit(solution)/shard_map/pallas_call | solution.py:490
  (36 shorter events, 6.6 us)
Async XLA Ops:
  3.0 7.7 %collective-permute-start.3 = (bf16[576,128]{1,0:T(8,128)(2,1)S(1)}, bf16[576,128]{1,0:T(8,128)(2,1)S(1)}, u32[]{:S(2)}, u32[]{:S(2)}) collective-permute-start(bf16[576,128]{1,0:T(8,128)(2,1)S(1)} %get-tuple-element.26.refs_4_), channel_id=1, source_target_pairs={{0,2},{1,3},{2,0},{3,1},{4,6},{5,7},{6,4},{7,5},{8,10},{9,11},{10,... | collective-permute-start | bytes 442376 | tf_op jit(solution)/shard_map/ppermute | solution.py:38
  6.0 7.0 %collective-permute-start = (bf16[576,128]{1,0:T(8,128)(2,1)S(1)}, bf16[576,128]{1,0:T(8,128)(2,1)S(1)}, u32[]{:S(2)}, u32[]{:S(2)}) collective-permute-start(bf16[576,128]{1,0:T(8,128)(2,1)S(1)} %get-tuple-element.22.refs_0_), channel_id=1, source_target_pairs={{0,2},{1,3},{2,0},{3,1},{4,6},{5,7},{6,4},{7,5},{8,10},{9,11},{10,... | collective-permute-start | bytes 442376 | tf_op jit(solution)/shard_map/ppermute | solution.py:38
  6.1 6.9 %collective-permute-start.6 = (bf16[6,32,128]{2,1,0:T(8,128)(2,1)S(1)}, bf16[6,32,128]{2,1,0:T(8,128)(2,1)S(1)}, u32[]{:S(2)}, u32[]{:S(2)}) collective-permute-start(bf16[6,32,128]{2,1,0:T(8,128)(2,1)S(1)} %get-tuple-element.28), channel_id=1, source_target_pairs={{0,1},{1,0},{2,3},{3,2},{4,5},{5,4},{6,7},{7,6},{8,9},{9,8},{10,11... | collective-permute-start | bytes 147464 | tf_op jit(solution)/shard_map/ppermute | solution.py:38
  6.1 14.8 %collective-permute-start.4 = (bf16[576,128]{1,0:T(8,128)(2,1)S(1)}, bf16[576,128]{1,0:T(8,128)(2,1)S(1)}, u32[]{:S(2)}, u32[]{:S(2)}) collective-permute-start(bf16[576,128]{1,0:T(8,128)(2,1)S(1)} %get-tuple-element.26.refs_4_), channel_id=1, source_target_pairs={{0,1},{1,0},{2,3},{3,2},{4,5},{5,4},{6,7},{7,6},{8,9},{9,8},{10,11... | collective-permute-start | bytes 442376 | tf_op jit(solution)/shard_map/ppermute | solution.py:38
  6.6 14.3 %collective-permute-start.1 = (bf16[576,128]{1,0:T(8,128)(2,1)S(1)}, bf16[576,128]{1,0:T(8,128)(2,1)S(1)}, u32[]{:S(2)}, u32[]{:S(2)}) collective-permute-start(bf16[576,128]{1,0:T(8,128)(2,1)S(1)} %get-tuple-element.22.refs_0_), channel_id=1, source_target_pairs={{0,1},{1,0},{2,3},{3,2},{4,5},{5,4},{6,7},{7,6},{8,9},{9,8},{10,11... | collective-permute-start | bytes 442376 | tf_op jit(solution)/shard_map/ppermute | solution.py:38
  10.7 10.2 %collective-permute-start.5 = (bf16[576,128]{1,0:T(8,128)(2,1)S(1)}, bf16[576,128]{1,0:T(8,128)(2,1)S(1)}, u32[]{:S(2)}, u32[]{:S(2)}) collective-permute-start(bf16[576,128]{1,0:T(8,128)(2,1)S(1)} %collective-permute-done.3.refs_5_), channel_id=1, source_target_pairs={{0,1},{1,0},{2,3},{3,2},{4,5},{5,4},{6,7},{7,6},{8,9},{9,8},{10,11... | collective-permute-start | bytes 442376 | tf_op jit(solution)/shard_map/ppermute | solution.py:38
  13.0 7.9 %collective-permute-start.2 = (bf16[576,128]{1,0:T(8,128)(2,1)S(1)}, bf16[576,128]{1,0:T(8,128)(2,1)S(1)}, u32[]{:S(2)}, u32[]{:S(2)}) collective-permute-start(bf16[576,128]{1,0:T(8,128)(2,1)S(1)} %collective-permute-done.refs_1_), channel_id=1, source_target_pairs={{0,1},{1,0},{2,3},{3,2},{4,5},{5,4},{6,7},{7,6},{8,9},{9,8},{10,11... | collective-permute-start | bytes 442376 | tf_op jit(solution)/shard_map/ppermute | solution.py:38
  13.0 4.2 %collective-permute-start.7 = (bf16[6,32,128]{2,1,0:T(8,128)(2,1)S(1)}, bf16[6,32,128]{2,1,0:T(8,128)(2,1)S(1)}, u32[]{:S(2)}, u32[]{:S(2)}) collective-permute-start(bf16[6,32,128]{2,1,0:T(8,128)(2,1)S(1)} %get-tuple-element.29), channel_id=1, source_target_pairs={{0,2},{1,3},{2,0},{3,1},{4,6},{5,7},{6,4},{7,5},{8,10},{9,11},{10,... | collective-permute-start | bytes 147464 | tf_op jit(solution)/shard_map/ppermute | solution.py:38
  17.2 3.7 %collective-permute-start.8 = (bf16[6,32,128]{2,1,0:T(8,128)(2,1)S(1)}, bf16[6,32,128]{2,1,0:T(8,128)(2,1)S(1)}, u32[]{:S(2)}, u32[]{:S(2)}) collective-permute-start(bf16[6,32,128]{2,1,0:T(8,128)(2,1)S(1)} %get-tuple-element.30), channel_id=1, source_target_pairs={{0,3},{1,2},{2,1},{3,0},{4,7},{5,6},{6,5},{7,4},{8,11},{9,10},{10,... | collective-permute-start | bytes 147464 | tf_op jit(solution)/shard_map/ppermute | solution.py:38
  24.7 7.3 %collective-permute-start.13 = (bf16[6,128,128]{2,1,0:T(8,128)(2,1)S(1)}, bf16[6,128,128]{2,1,0:T(8,128)(2,1)S(1)}, u32[]{:S(2)}, u32[]{:S(2)}) collective-permute-start(bf16[6,128,128]{2,1,0:T(8,128)(2,1)S(1)} %get-tuple-element.33.even.own), channel_id=1, source_target_pairs={{0,4},{4,0},{8,12},{12,8},{16,20},{20,16},{24,28},{28,24},{1,5},{5... | collective-permute-start | bytes 589832 | tf_op jit(solution)/shard_map/ppermute | solution.py:38
  26.8 5.2 %collective-permute-start.9 = (bf16[6,128,128]{2,1,0:T(8,128)(2,1)S(1)}, bf16[6,128,128]{2,1,0:T(8,128)(2,1)S(1)}, u32[]{:S(2)}, u32[]{:S(2)}) collective-permute-start(bf16[6,128,128]{2,1,0:T(8,128)(2,1)S(1)} %get-tuple-element.33.even.own), channel_id=1, source_target_pairs={{0,1},{1,0},{2,3},{3,2},{4,5},{5,4},{6,7},{7,6},{8,9},{9,8},{10,11... | collective-permute-start | bytes 589832 | tf_op jit(solution)/shard_map/ppermute | solution.py:38
  32.0 1.4 %collective-permute-start.14 = (bf16[6,128,128]{2,1,0:T(8,128)(2,1)S(1)}, bf16[6,128,128]{2,1,0:T(8,128)(2,1)S(1)}, u32[]{:S(2)}, u32[]{:S(2)}) collective-permute-start(bf16[6,128,128]{2,1,0:T(8,128)(2,1)S(1)} %collective-permute-done.13.got.refs_8_), channel_id=1, source_target_pairs={{0,1},{1,0},{2,3},{3,2},{4,5},{5,4},{6,7},{7,6},{8,9},{9,8},{10,11... | collective-permute-start | bytes 589832 | tf_op jit(solution)/shard_map/ppermute | solution.py:38
  33.8 9.9 %collective-permute-start.17 = (bf16[6,128,128]{2,1,0:T(8,128)(2,1)S(1)}, bf16[6,128,128]{2,1,0:T(8,128)(2,1)S(1)}, u32[]{:S(2)}, u32[]{:S(2)}) collective-permute-start(bf16[6,128,128]{2,1,0:T(8,128)(2,1)S(1)} %shard_map.51), channel_id=1, source_target_pairs={{0,8},{4,12},{8,0},{12,4},{16,24},{20,28},{24,16},{28,20},{1,9},{5... | collective-permute-start | bytes 589832 | tf_op jit(solution)/shard_map/ppermute | solution.py:38
  35.6 4.6 %collective-permute-start.10 = (bf16[6,64,128]{2,1,0:T(8,128)(2,1)S(1)}, bf16[6,64,128]{2,1,0:T(8,128)(2,1)S(1)}, u32[]{:S(2)}, u32[]{:S(2)}) collective-permute-start(bf16[6,64,128]{2,1,0:T(8,128)(2,1)S(1)} %get-tuple-element.34.own.own_offset), channel_id=1, source_target_pairs={{0,4},{4,0},{8,12},{12,8},{16,20},{20,16},{24,28},{28,24},{1,5},{5... | collective-permute-start | bytes 294920 | tf_op jit(solution)/shard_map/ppermute | solution.py:38
  40.6 21.7 %copy-start = (bf16[1,1,4,512,512]{4,3,2,1,0:T(8,128)(2,1)S(1)}, bf16[1,1,4,512,512]{4,3,2,1,0:T(8,128)(2,1)}, u32[]{:S(2)}) copy-start(bf16[1,1,4,512,512]{4,3,2,1,0:T(8,128)(2,1)} %param.5) | copy-start | bytes 6291460
  40.6 21.7 %copy-start.1 = (bf16[1,1,4,3,64,512]{5,4,3,2,1,0:T(8,128)(2,1)S(1)}, bf16[1,1,4,3,64,512]{5,4,3,2,1,0:T(8,128)(2,1)}, u32[]{:S(2)}) copy-start(bf16[1,1,4,3,64,512]{5,4,3,2,1,0:T(8,128)(2,1)} %param.6) | copy-start | bytes 2359300
  40.6 5.7 %collective-permute-start.12 = (bf16[6,64,128]{2,1,0:T(8,128)(2,1)S(1)}, bf16[6,64,128]{2,1,0:T(8,128)(2,1)S(1)}, u32[]{:S(2)}, u32[]{:S(2)}) collective-permute-start(bf16[6,64,128]{2,1,0:T(8,128)(2,1)S(1)} %shard_map.49), channel_id=1, source_target_pairs={{0,12},{4,8},{8,4},{12,0},{16,28},{20,24},{24,20},{28,16},{1,13},{... | collective-permute-start | bytes 294920 | tf_op jit(solution)/shard_map/ppermute | solution.py:38
  42.1 5.4 %collective-permute-start.11 = (bf16[6,64,128]{2,1,0:T(8,128)(2,1)S(1)}, bf16[6,64,128]{2,1,0:T(8,128)(2,1)S(1)}, u32[]{:S(2)}, u32[]{:S(2)}) collective-permute-start(bf16[6,64,128]{2,1,0:T(8,128)(2,1)S(1)} %shard_map.49), channel_id=1, source_target_pairs={{0,8},{4,12},{8,0},{12,4},{16,24},{20,28},{24,16},{28,20},{1,9},{5... | collective-permute-start | bytes 294920 | tf_op jit(solution)/shard_map/ppermute | solution.py:38
  43.7 10.1 %collective-permute-start.18 = (bf16[6,128,128]{2,1,0:T(8,128)(2,1)S(1)}, bf16[6,128,128]{2,1,0:T(8,128)(2,1)S(1)}, u32[]{:S(2)}, u32[]{:S(2)}) collective-permute-start(bf16[6,128,128]{2,1,0:T(8,128)(2,1)S(1)} %collective-permute-done.17.refs_6_), channel_id=1, source_target_pairs={{0,1},{1,0},{2,3},{3,2},{4,5},{5,4},{6,7},{7,6},{8,9},{9,8},{10,11... | collective-permute-start | bytes 589832 | tf_op jit(solution)/shard_map/ppermute | solution.py:38
  48.0 4.7 %collective-permute-start.16 = (bf16[6,64,128]{2,1,0:T(8,128)(2,1)S(1)}, bf16[6,64,128]{2,1,0:T(8,128)(2,1)S(1)}, u32[]{:S(2)}, u32[]{:S(2)}) collective-permute-start(bf16[6,64,128]{2,1,0:T(8,128)(2,1)S(1)} %shard_map.50), channel_id=1, source_target_pairs={{0,4},{4,0},{8,24},{12,28},{16,20},{20,16},{24,8},{28,12},{1,5},{5... | collective-permute-start | bytes 294920 | tf_op jit(solution)/shard_map/ppermute | solution.py:589
  48.6 5.2 %collective-permute-start.15 = (bf16[6,64,128]{2,1,0:T(8,128)(2,1)S(1)}, bf16[6,64,128]{2,1,0:T(8,128)(2,1)S(1)}, u32[]{:S(2)}, u32[]{:S(2)}) collective-permute-start(bf16[6,64,128]{2,1,0:T(8,128)(2,1)S(1)} %shard_map.50), channel_id=1, source_target_pairs={{0,4},{4,0},{8,16},{12,20},{16,8},{20,12},{24,28},{28,24},{1,5},{5... | collective-permute-start | bytes 294920 | tf_op jit(solution)/shard_map/ppermute | solution.py:588
  57.3 1.9 %collective-permute-start.19 = (bf16[6,32,128]{2,1,0:T(8,128)(2,1)S(1)}, bf16[6,32,128]{2,1,0:T(8,128)(2,1)S(1)}, u32[]{:S(2)}, u32[]{:S(2)}) collective-permute-start(bf16[6,32,128]{2,1,0:T(8,128)(2,1)S(1)} %get-tuple-element.36), channel_id=1, source_target_pairs={{0,1},{1,0},{2,3},{3,2},{4,5},{5,4},{6,7},{7,6},{8,9},{9,8},{10,11... | collective-permute-start | bytes 147464 | tf_op jit(solution)/shard_map/ppermute | solution.py:38
  57.3 4.2 %collective-permute-start.20 = (bf16[6,32,128]{2,1,0:T(8,128)(2,1)S(1)}, bf16[6,32,128]{2,1,0:T(8,128)(2,1)S(1)}, u32[]{:S(2)}, u32[]{:S(2)}) collective-permute-start(bf16[6,32,128]{2,1,0:T(8,128)(2,1)S(1)} %get-tuple-element.37), channel_id=1, source_target_pairs={{0,2},{1,3},{2,0},{3,1},{4,6},{5,7},{6,4},{7,5},{8,10},{9,11},{10,... | collective-permute-start | bytes 147464 | tf_op jit(solution)/shard_map/ppermute | solution.py:38
  58.6 3.7 %collective-permute-start.21 = (bf16[6,32,128]{2,1,0:T(8,128)(2,1)S(1)}, bf16[6,32,128]{2,1,0:T(8,128)(2,1)S(1)}, u32[]{:S(2)}, u32[]{:S(2)}) collective-permute-start(bf16[6,32,128]{2,1,0:T(8,128)(2,1)S(1)} %get-tuple-element.38), channel_id=1, source_target_pairs={{0,3},{1,2},{2,1},{3,0},{4,7},{5,6},{6,5},{7,4},{8,11},{9,10},{10,... | collective-permute-start | bytes 147464 | tf_op jit(solution)/shard_map/ppermute | solution.py:38
  (2 other events, 43.4 us)

commit v8 on v7

--- a/solution.py
+++ b/solution.py
@@ -110,11 +110,18 @@
     ]
     for copy in later:
         copy.start()
-    for copy in copies:
-        copy.wait()
-    values = [face_rows_of(inverse, slots[p], face) for p in range(2)]
+
+    def arrived(p):
+        for kind, (far, near) in enumerate(((inverse_far, inverse), (coupling_far, coupling))):
+            pltpu.make_async_copy(far.at[slots[p]], near.at[slots[p]], done.at[kind, slots[p]]).wait()
+
+    values = []
+    for p in range(2):
+        arrived(p)
+        values.append(face_rows_of(inverse, slots[p], face))
     pair_maps(maps, coupling, slots[:2], values, face)
     for p in range(2, count):
+        arrived(p)
         values.append(face_rows_of(inverse, slots[p], face))
         coupling_near[p - 2] = coupling[slots[p]]
     for p in range(count):

time: 65 us -> 65 us (level)
  no operation moved by 1% of the time
where the time goes in v8:
time: 65 us; the launch traced here: 64.9 us
  waiting for transfers between devices  31.8 us (49%)
  starting transfers between devices  18.9 us (29%)
  Pallas kernels  14 us (22%)
    ppermute x20, waiting for transfers between devices, swap(): return lax.ppermute(value, axis, [(i, i ^ mask) for i in range(count)])  28.2 us
    ppermute x20, starting transfers between devices, swap(): return lax.ppermute(value, axis, [(i, i ^ mask) for i in range(count)])  16.8 us
    pallas_call x8, Pallas kernels, call(): pl.pallas_call(kernel, out_shape=outs, in_specs=[SMEM] * len(scalars) + [...  14 us
    ppermute x1, waiting for transfers between devices, shards(): third = lax.ppermute(joined, 'stream', crossing(masks, 1, 3))  2.59 us
    ppermute x1, starting transfers between devices, shards(): second = lax.ppermute(joined, 'stream', crossing(masks, 1, 2))  1.52 us
  transfers between devices with their start and end apart: 22, of which 13 were waited for; matrix products, arithmetic and copies ran while one was open for 0% of the time, Pallas kernels for 1%

profile of v8, /device:TPU:0, one launch (start us, length us, event | category | flops | bytes accessed | tf_op | source)
XLA Modules:
  0.0 64.9 jit_solution(9178620974670792529)
XLA Ops:
  0.0 2.3 %shard_map.46 = (bf16[576,128]{1,0:T(8,128)(2,1)S(1)}, bf16[4,256,512]{2,1,0:T(8,128)(2,1)S(1)}, bf16[2,192,512]{2,1,0:T(8,128)(2,1)S(1)}, bf16[4,512,128]{2,1,0:T(8,128)(2,1)S(1)}) custom-call(s32[4]{0:T(128)} %bitcast.13, bf16[4,512,512]{2,1,0:T(8,128)(2,1)} %bitcast.7, bf16[4,192,512]{2,1,0:T(8,128)(2,1)} %bitcast.9, bf16[4,512,128]{2,1,0:T(8,128)(2,1)} %bitcast.11), custom_call_target="tpu_custom_call" | custom-call | tf_op jit(solution)/shard_map/pallas_call | solution.py:497
  3.0 3.0 %collective-permute-start.3 = (bf16[576,128]{1,0:T(8,128)(2,1)S(1)}, bf16[576,128]{1,0:T(8,128)(2,1)S(1)}, u32[]{:S(2)}, u32[]{:S(2)}) collective-permute-start(bf16[576,128]{1,0:T(8,128)(2,1)S(1)} %get-tuple-element.26.refs_4_), channel_id=1, source_target_pairs={{0,2},{1,3},{2,0},{3,1},{4,6},{5,7},{6,4},{7,5},{8,10},{9,11},{10,... | collective-permute-start | bytes 442376 | tf_op jit(solution)/shard_map/ppermute | solution.py:38
  6.6 4.1 %collective-permute-done.3.refs_5_ = bf16[576,128]{1,0:T(8,128)(2,1)S(1)} collective-permute-done((bf16[576,128]{1,0:T(8,128)(2,1)S(1)}, bf16[576,128]{1,0:T(8,128)(2,1)S(1)}, u32[]{:S(2)}, u32[]{:S(2)}) %collective-permute-start.3) | collective-permute-done | bytes 147488 | tf_op jit(solution)/shard_map/ppermute | solution.py:38
  10.7 2.3 %collective-permute-done.refs_1_ = bf16[576,128]{1,0:T(8,128)(2,1)S(1)} collective-permute-done((bf16[576,128]{1,0:T(8,128)(2,1)S(1)}, bf16[576,128]{1,0:T(8,128)(2,1)S(1)}, u32[]{:S(2)}, u32[]{:S(2)}) %collective-permute-start) | collective-permute-done | bytes 147488 | tf_op jit(solution)/shard_map/ppermute | solution.py:38
  13.0 1.7 %collective-permute-start.7 = (bf16[6,32,128]{2,1,0:T(8,128)(2,1)S(1)}, bf16[6,32,128]{2,1,0:T(8,128)(2,1)S(1)}, u32[]{:S(2)}, u32[]{:S(2)}) collective-permute-start(bf16[6,32,128]{2,1,0:T(8,128)(2,1)S(1)} %get-tuple-element.29), channel_id=1, source_target_pairs={{0,2},{1,3},{2,0},{3,1},{4,6},{5,7},{6,4},{7,5},{8,10},{9,11},{10,... | collective-permute-start | bytes 147464 | tf_op jit(solution)/shard_map/ppermute | solution.py:38
  14.8 2.4 %collective-permute-done.7.refs_10_ = bf16[6,32,128]{2,1,0:T(8,128)(2,1)S(1)} collective-permute-done((bf16[6,32,128]{2,1,0:T(8,128)(2,1)S(1)}, bf16[6,32,128]{2,1,0:T(8,128)(2,1)S(1)}, u32[]{:S(2)}, u32[]{:S(2)}) %collective-permute-start.7) | collective-permute-done | bytes 49184 | tf_op jit(solution)/shard_map/ppermute | solution.py:38
  18.2 2.8 %collective-permute-done.8.refs_11_ = bf16[6,32,128]{2,1,0:T(8,128)(2,1)S(1)} collective-permute-done((bf16[6,32,128]{2,1,0:T(8,128)(2,1)S(1)}, bf16[6,32,128]{2,1,0:T(8,128)(2,1)S(1)}, u32[]{:S(2)}, u32[]{:S(2)}) %collective-permute-start.8) | collective-permute-done | bytes 49184 | tf_op jit(solution)/shard_map/ppermute | solution.py:38
  20.9 3.7 %shard_map.48 = (bf16[6,128,128]{2,1,0:T(8,128)(2,1)S(1)}, bf16[6,64,128]{2,1,0:T(8,128)(2,1)S(1)}, bf16[4,4,192,256]{3,2,1,0:T(8,128)(2,1)S(1)}, bf16[4,4,32,256]{3,2,1,0:T(8,128)(2,1)S(1)}) custom-call(s32[1]{0:T(128)} %bitcast.place, bf16[576,128]{1,0:T(8,128)(2,1)S(1)} %get-tuple-element.22.refs_0_, bf16[576,128]{1,0:T(8,128)(2,1)S(1)} %collective-permute-done.refs_1_, ...), custom_call_target="tpu_custom_call" | custom-call | tf_op jit(solution)/shard_map/pallas_call | solution.py:497
  24.7 2.2 %collective-permute-start.13 = (bf16[6,128,128]{2,1,0:T(8,128)(2,1)S(1)}, bf16[6,128,128]{2,1,0:T(8,128)(2,1)S(1)}, u32[]{:S(2)}, u32[]{:S(2)}) collective-permute-start(bf16[6,128,128]{2,1,0:T(8,128)(2,1)S(1)} %get-tuple-element.33.even.own), channel_id=1, source_target_pairs={{0,4},{4,0},{8,12},{12,8},{16,20},{20,16},{24,28},{28,24},{1,5},{5... | collective-permute-start | bytes 589832 | tf_op jit(solution)/shard_map/ppermute | solution.py:38
  26.9 5.2 %collective-permute-done.13.got.refs_8_ = bf16[6,128,128]{2,1,0:T(8,128)(2,1)S(1)} collective-permute-done((bf16[6,128,128]{2,1,0:T(8,128)(2,1)S(1)}, bf16[6,128,128]{2,1,0:T(8,128)(2,1)S(1)}, u32[]{:S(2)}, u32[]{:S(2)}) %collective-permute-start.13) | collective-permute-done | bytes 196640 | tf_op jit(solution)/shard_map/ppermute | solution.py:38
  32.0 1.4 %collective-permute-done.14.got_other.refs_9_ = bf16[6,128,128]{2,1,0:T(8,128)(2,1)S(1)} collective-permute-done((bf16[6,128,128]{2,1,0:T(8,128)(2,1)S(1)}, bf16[6,128,128]{2,1,0:T(8,128)(2,1)S(1)}, u32[]{:S(2)}, u32[]{:S(2)}) %collective-permute-start.14) | collective-permute-done | bytes 196640 | tf_op jit(solution)/shard_map/ppermute | solution.py:38
  33.8 1.9 %collective-permute-start.17 = (bf16[6,128,128]{2,1,0:T(8,128)(2,1)S(1)}, bf16[6,128,128]{2,1,0:T(8,128)(2,1)S(1)}, u32[]{:S(2)}, u32[]{:S(2)}) collective-permute-start(bf16[6,128,128]{2,1,0:T(8,128)(2,1)S(1)} %shard_map.51), channel_id=1, source_target_pairs={{0,8},{4,12},{8,0},{12,4},{16,24},{20,28},{24,16},{28,20},{1,9},{5... | collective-permute-start | bytes 589832 | tf_op jit(solution)/shard_map/ppermute | solution.py:38
  35.7 1.5 %collective-permute-start.10 = (bf16[6,64,128]{2,1,0:T(8,128)(2,1)S(1)}, bf16[6,64,128]{2,1,0:T(8,128)(2,1)S(1)}, u32[]{:S(2)}, u32[]{:S(2)}) collective-permute-start(bf16[6,64,128]{2,1,0:T(8,128)(2,1)S(1)} %get-tuple-element.34.own.own_offset), channel_id=1, source_target_pairs={{0,4},{4,0},{8,12},{12,8},{16,20},{20,16},{24,28},{28,24},{1,5},{5... | collective-permute-start | bytes 294920 | tf_op jit(solution)/shard_map/ppermute | solution.py:38
  37.2 3.1 %collective-permute-done.10.entry.got_offset.refs_10_ = bf16[6,64,128]{2,1,0:T(8,128)(2,1)S(1)} collective-permute-done((bf16[6,64,128]{2,1,0:T(8,128)(2,1)S(1)}, bf16[6,64,128]{2,1,0:T(8,128)(2,1)S(1)}, u32[]{:S(2)}, u32[]{:S(2)}) %collective-permute-start.10) | collective-permute-done | bytes 98336 | tf_op jit(solution)/shard_map/ppermute | solution.py:38
  40.7 1.5 %collective-permute-start.12 = (bf16[6,64,128]{2,1,0:T(8,128)(2,1)S(1)}, bf16[6,64,128]{2,1,0:T(8,128)(2,1)S(1)}, u32[]{:S(2)}, u32[]{:S(2)}) collective-permute-start(bf16[6,64,128]{2,1,0:T(8,128)(2,1)S(1)} %shard_map.49), channel_id=1, source_target_pairs={{0,12},{4,8},{8,4},{12,0},{16,28},{20,24},{24,20},{28,16},{1,13},{... | collective-permute-start | bytes 294920 | tf_op jit(solution)/shard_map/ppermute | solution.py:38
  42.2 1.6 %collective-permute-start.11 = (bf16[6,64,128]{2,1,0:T(8,128)(2,1)S(1)}, bf16[6,64,128]{2,1,0:T(8,128)(2,1)S(1)}, u32[]{:S(2)}, u32[]{:S(2)}) collective-permute-start(bf16[6,64,128]{2,1,0:T(8,128)(2,1)S(1)} %shard_map.49), channel_id=1, source_target_pairs={{0,8},{4,12},{8,0},{12,4},{16,24},{20,28},{24,16},{28,20},{1,9},{5... | collective-permute-start | bytes 294920 | tf_op jit(solution)/shard_map/ppermute | solution.py:38
  43.7 2.7 %collective-permute-done.12.across.refs_3_ = bf16[6,64,128]{2,1,0:T(8,128)(2,1)S(1)} collective-permute-done((bf16[6,64,128]{2,1,0:T(8,128)(2,1)S(1)}, bf16[6,64,128]{2,1,0:T(8,128)(2,1)S(1)}, u32[]{:S(2)}, u32[]{:S(2)}) %collective-permute-start.12) | collective-permute-done | bytes 98336 | tf_op jit(solution)/shard_map/ppermute | solution.py:38
  46.4 1.1 %collective-permute-done.11.near.refs_2_ = bf16[6,64,128]{2,1,0:T(8,128)(2,1)S(1)} collective-permute-done((bf16[6,64,128]{2,1,0:T(8,128)(2,1)S(1)}, bf16[6,64,128]{2,1,0:T(8,128)(2,1)S(1)}, u32[]{:S(2)}, u32[]{:S(2)}) %collective-permute-start.11) | collective-permute-done | bytes 98336 | tf_op jit(solution)/shard_map/ppermute | solution.py:38
  48.6 1.5 %collective-permute-start.15 = (bf16[6,64,128]{2,1,0:T(8,128)(2,1)S(1)}, bf16[6,64,128]{2,1,0:T(8,128)(2,1)S(1)}, u32[]{:S(2)}, u32[]{:S(2)}) collective-permute-start(bf16[6,64,128]{2,1,0:T(8,128)(2,1)S(1)} %shard_map.50), channel_id=1, source_target_pairs={{0,4},{4,0},{8,16},{12,20},{16,8},{20,12},{24,28},{28,24},{1,5},{5... | collective-permute-start | bytes 294920 | tf_op jit(solution)/shard_map/ppermute | solution.py:595
  50.2 2.6 %collective-permute-done.16.refs_5_ = bf16[6,64,128]{2,1,0:T(8,128)(2,1)S(1)} collective-permute-done((bf16[6,64,128]{2,1,0:T(8,128)(2,1)S(1)}, bf16[6,64,128]{2,1,0:T(8,128)(2,1)S(1)}, u32[]{:S(2)}, u32[]{:S(2)}) %collective-permute-start.16) | collective-permute-done | bytes 98336 | tf_op jit(solution)/shard_map/ppermute | solution.py:596
  53.8 3.5 %shard_map.52 = (bf16[6,32,128]{2,1,0:T(8,128)(2,1)S(1)}, bf16[6,32,128]{2,1,0:T(8,128)(2,1)S(1)}, bf16[6,32,128]{2,1,0:T(8,128)(2,1)S(1)}, bf16[6,32,128]{2,1,0:T(8,128)(2,1)S(1)}) custom-call(s32[1]{0:T(128)} %bitcast.place, s32[1]{0:T(128)} %bitcast.5.line, bf16[4,4,192,256]{3,2,1,0:T(8,128)(2,1)S(1)} %get-tuple-element.31.refs_0_, ...), custom_call_target="tpu_custom_call" | custom-call | tf_op jit(solution)/shard_map/pallas_call | solution.py:497
  57.4 1.2 %collective-permute-start.20 = (bf16[6,32,128]{2,1,0:T(8,128)(2,1)S(1)}, bf16[6,32,128]{2,1,0:T(8,128)(2,1)S(1)}, u32[]{:S(2)}, u32[]{:S(2)}) collective-permute-start(bf16[6,32,128]{2,1,0:T(8,128)(2,1)S(1)} %get-tuple-element.37), channel_id=1, source_target_pairs={{0,2},{1,3},{2,0},{3,1},{4,6},{5,7},{6,4},{7,5},{8,10},{9,11},{10,... | collective-permute-start | bytes 147464 | tf_op jit(solution)/shard_map/ppermute | solution.py:38
  59.3 2.3 %collective-permute-done.20.refs_2_ = bf16[6,32,128]{2,1,0:T(8,128)(2,1)S(1)} collective-permute-done((bf16[6,32,128]{2,1,0:T(8,128)(2,1)S(1)}, bf16[6,32,128]{2,1,0:T(8,128)(2,1)S(1)}, u32[]{:S(2)}, u32[]{:S(2)}) %collective-permute-start.20) | collective-permute-done | bytes 49184 | tf_op jit(solution)/shard_map/ppermute | solution.py:38
  62.4 2.5 %shard_map.53 = bf16[4,512,128]{2,1,0:T(8,128)(2,1)} custom-call(s32[1]{0:T(128)} %bitcast.place, s32[4]{0:T(128)S(1)} %bitcast.14, bf16[4,512,512]{2,1,0:T(8,128)(2,1)S(1)} %bitcast.8, bf16[4,192,512]{2,1,0:T(8,128)(2,1)S(1)} %bitcast.10, bf16[4,512,128]{2,1,0:T(8,128)(2,1)S(1)} %bitcast.12, bf16[6,32,128]{2,1,0:T(8,128)(2,1)S(1)} %get-tuple-element.35.refs_0_, ...), custom_call_target="tpu_custom_call" | custom-call | tf_op jit(solution)/shard_map/pallas_call | solution.py:497
  (36 shorter events, 6.6 us)
Async XLA Ops:
  3.0 7.7 %collective-permute-start.3 = (bf16[576,128]{1,0:T(8,128)(2,1)S(1)}, bf16[576,128]{1,0:T(8,128)(2,1)S(1)}, u32[]{:S(2)}, u32[]{:S(2)}) collective-permute-start(bf16[576,128]{1,0:T(8,128)(2,1)S(1)} %get-tuple-element.26.refs_4_), channel_id=1, source_target_pairs={{0,2},{1,3},{2,0},{3,1},{4,6},{5,7},{6,4},{7,5},{8,10},{9,11},{10,... | collective-permute-start | bytes 442376 | tf_op jit(solution)/shard_map/ppermute | solution.py:38
  6.0 7.0 %collective-permute-start = (bf16[576,128]{1,0:T(8,128)(2,1)S(1)}, bf16[576,128]{1,0:T(8,128)(2,1)S(1)}, u32[]{:S(2)}, u32[]{:S(2)}) collective-permute-start(bf16[576,128]{1,0:T(8,128)(2,1)S(1)} %get-tuple-element.22.refs_0_), channel_id=1, source_target_pairs={{0,2},{1,3},{2,0},{3,1},{4,6},{5,7},{6,4},{7,5},{8,10},{9,11},{10,... | collective-permute-start | bytes 442376 | tf_op jit(solution)/shard_map/ppermute | solution.py:38
  6.1 6.9 %collective-permute-start.6 = (bf16[6,32,128]{2,1,0:T(8,128)(2,1)S(1)}, bf16[6,32,128]{2,1,0:T(8,128)(2,1)S(1)}, u32[]{:S(2)}, u32[]{:S(2)}) collective-permute-start(bf16[6,32,128]{2,1,0:T(8,128)(2,1)S(1)} %get-tuple-element.28), channel_id=1, source_target_pairs={{0,1},{1,0},{2,3},{3,2},{4,5},{5,4},{6,7},{7,6},{8,9},{9,8},{10,11... | collective-permute-start | bytes 147464 | tf_op jit(solution)/shard_map/ppermute | solution.py:38
  6.1 14.8 %collective-permute-start.4 = (bf16[576,128]{1,0:T(8,128)(2,1)S(1)}, bf16[576,128]{1,0:T(8,128)(2,1)S(1)}, u32[]{:S(2)}, u32[]{:S(2)}) collective-permute-start(bf16[576,128]{1,0:T(8,128)(2,1)S(1)} %get-tuple-element.26.refs_4_), channel_id=1, source_target_pairs={{0,1},{1,0},{2,3},{3,2},{4,5},{5,4},{6,7},{7,6},{8,9},{9,8},{10,11... | collective-permute-start | bytes 442376 | tf_op jit(solution)/shard_map/ppermute | solution.py:38
  6.6 14.3 %collective-permute-start.1 = (bf16[576,128]{1,0:T(8,128)(2,1)S(1)}, bf16[576,128]{1,0:T(8,128)(2,1)S(1)}, u32[]{:S(2)}, u32[]{:S(2)}) collective-permute-start(bf16[576,128]{1,0:T(8,128)(2,1)S(1)} %get-tuple-element.22.refs_0_), channel_id=1, source_target_pairs={{0,1},{1,0},{2,3},{3,2},{4,5},{5,4},{6,7},{7,6},{8,9},{9,8},{10,11... | collective-permute-start | bytes 442376 | tf_op jit(solution)/shard_map/ppermute | solution.py:38
  10.7 10.2 %collective-permute-start.5 = (bf16[576,128]{1,0:T(8,128)(2,1)S(1)}, bf16[576,128]{1,0:T(8,128)(2,1)S(1)}, u32[]{:S(2)}, u32[]{:S(2)}) collective-permute-start(bf16[576,128]{1,0:T(8,128)(2,1)S(1)} %collective-permute-done.3.refs_5_), channel_id=1, source_target_pairs={{0,1},{1,0},{2,3},{3,2},{4,5},{5,4},{6,7},{7,6},{8,9},{9,8},{10,11... | collective-permute-start | bytes 442376 | tf_op jit(solution)/shard_map/ppermute | solution.py:38
  13.0 7.9 %collective-permute-start.2 = (bf16[576,128]{1,0:T(8,128)(2,1)S(1)}, bf16[576,128]{1,0:T(8,128)(2,1)S(1)}, u32[]{:S(2)}, u32[]{:S(2)}) collective-permute-start(bf16[576,128]{1,0:T(8,128)(2,1)S(1)} %collective-permute-done.refs_1_), channel_id=1, source_target_pairs={{0,1},{1,0},{2,3},{3,2},{4,5},{5,4},{6,7},{7,6},{8,9},{9,8},{10,11... | collective-permute-start | bytes 442376 | tf_op jit(solution)/shard_map/ppermute | solution.py:38
  13.0 4.2 %collective-permute-start.7 = (bf16[6,32,128]{2,1,0:T(8,128)(2,1)S(1)}, bf16[6,32,128]{2,1,0:T(8,128)(2,1)S(1)}, u32[]{:S(2)}, u32[]{:S(2)}) collective-permute-start(bf16[6,32,128]{2,1,0:T(8,128)(2,1)S(1)} %get-tuple-element.29), channel_id=1, source_target_pairs={{0,2},{1,3},{2,0},{3,1},{4,6},{5,7},{6,4},{7,5},{8,10},{9,11},{10,... | collective-permute-start | bytes 147464 | tf_op jit(solution)/shard_map/ppermute | solution.py:38
  17.2 3.7 %collective-permute-start.8 = (bf16[6,32,128]{2,1,0:T(8,128)(2,1)S(1)}, bf16[6,32,128]{2,1,0:T(8,128)(2,1)S(1)}, u32[]{:S(2)}, u32[]{:S(2)}) collective-permute-start(bf16[6,32,128]{2,1,0:T(8,128)(2,1)S(1)} %get-tuple-element.30), channel_id=1, source_target_pairs={{0,3},{1,2},{2,1},{3,0},{4,7},{5,6},{6,5},{7,4},{8,11},{9,10},{10,... | collective-permute-start | bytes 147464 | tf_op jit(solution)/shard_map/ppermute | solution.py:38
  24.7 7.4 %collective-permute-start.13 = (bf16[6,128,128]{2,1,0:T(8,128)(2,1)S(1)}, bf16[6,128,128]{2,1,0:T(8,128)(2,1)S(1)}, u32[]{:S(2)}, u32[]{:S(2)}) collective-permute-start(bf16[6,128,128]{2,1,0:T(8,128)(2,1)S(1)} %get-tuple-element.33.even.own), channel_id=1, source_target_pairs={{0,4},{4,0},{8,12},{12,8},{16,20},{20,16},{24,28},{28,24},{1,5},{5... | collective-permute-start | bytes 589832 | tf_op jit(solution)/shard_map/ppermute | solution.py:38
  26.8 5.2 %collective-permute-start.9 = (bf16[6,128,128]{2,1,0:T(8,128)(2,1)S(1)}, bf16[6,128,128]{2,1,0:T(8,128)(2,1)S(1)}, u32[]{:S(2)}, u32[]{:S(2)}) collective-permute-start(bf16[6,128,128]{2,1,0:T(8,128)(2,1)S(1)} %get-tuple-element.33.even.own), channel_id=1, source_target_pairs={{0,1},{1,0},{2,3},{3,2},{4,5},{5,4},{6,7},{7,6},{8,9},{9,8},{10,11... | collective-permute-start | bytes 589832 | tf_op jit(solution)/shard_map/ppermute | solution.py:38
  32.0 1.4 %collective-permute-start.14 = (bf16[6,128,128]{2,1,0:T(8,128)(2,1)S(1)}, bf16[6,128,128]{2,1,0:T(8,128)(2,1)S(1)}, u32[]{:S(2)}, u32[]{:S(2)}) collective-permute-start(bf16[6,128,128]{2,1,0:T(8,128)(2,1)S(1)} %collective-permute-done.13.got.refs_8_), channel_id=1, source_target_pairs={{0,1},{1,0},{2,3},{3,2},{4,5},{5,4},{6,7},{7,6},{8,9},{9,8},{10,11... | collective-permute-start | bytes 589832 | tf_op jit(solution)/shard_map/ppermute | solution.py:38
  33.8 9.9 %collective-permute-start.17 = (bf16[6,128,128]{2,1,0:T(8,128)(2,1)S(1)}, bf16[6,128,128]{2,1,0:T(8,128)(2,1)S(1)}, u32[]{:S(2)}, u32[]{:S(2)}) collective-permute-start(bf16[6,128,128]{2,1,0:T(8,128)(2,1)S(1)} %shard_map.51), channel_id=1, source_target_pairs={{0,8},{4,12},{8,0},{12,4},{16,24},{20,28},{24,16},{28,20},{1,9},{5... | collective-permute-start | bytes 589832 | tf_op jit(solution)/shard_map/ppermute | solution.py:38
  35.7 4.6 %collective-permute-start.10 = (bf16[6,64,128]{2,1,0:T(8,128)(2,1)S(1)}, bf16[6,64,128]{2,1,0:T(8,128)(2,1)S(1)}, u32[]{:S(2)}, u32[]{:S(2)}) collective-permute-start(bf16[6,64,128]{2,1,0:T(8,128)(2,1)S(1)} %get-tuple-element.34.own.own_offset), channel_id=1, source_target_pairs={{0,4},{4,0},{8,12},{12,8},{16,20},{20,16},{24,28},{28,24},{1,5},{5... | collective-permute-start | bytes 294920 | tf_op jit(solution)/shard_map/ppermute | solution.py:38
  40.6 21.7 %copy-start = (bf16[1,1,4,512,512]{4,3,2,1,0:T(8,128)(2,1)S(1)}, bf16[1,1,4,512,512]{4,3,2,1,0:T(8,128)(2,1)}, u32[]{:S(2)}) copy-start(bf16[1,1,4,512,512]{4,3,2,1,0:T(8,128)(2,1)} %param.5) | copy-start | bytes 6291460
  40.6 21.7 %copy-start.1 = (bf16[1,1,4,3,64,512]{5,4,3,2,1,0:T(8,128)(2,1)S(1)}, bf16[1,1,4,3,64,512]{5,4,3,2,1,0:T(8,128)(2,1)}, u32[]{:S(2)}) copy-start(bf16[1,1,4,3,64,512]{5,4,3,2,1,0:T(8,128)(2,1)} %param.6) | copy-start | bytes 2359300
  40.7 5.7 %collective-permute-start.12 = (bf16[6,64,128]{2,1,0:T(8,128)(2,1)S(1)}, bf16[6,64,128]{2,1,0:T(8,128)(2,1)S(1)}, u32[]{:S(2)}, u32[]{:S(2)}) collective-permute-start(bf16[6,64,128]{2,1,0:T(8,128)(2,1)S(1)} %shard_map.49), channel_id=1, source_target_pairs={{0,12},{4,8},{8,4},{12,0},{16,28},{20,24},{24,20},{28,16},{1,13},{... | collective-permute-start | bytes 294920 | tf_op jit(solution)/shard_map/ppermute | solution.py:38
  42.2 5.4 %collective-permute-start.11 = (bf16[6,64,128]{2,1,0:T(8,128)(2,1)S(1)}, bf16[6,64,128]{2,1,0:T(8,128)(2,1)S(1)}, u32[]{:S(2)}, u32[]{:S(2)}) collective-permute-start(bf16[6,64,128]{2,1,0:T(8,128)(2,1)S(1)} %shard_map.49), channel_id=1, source_target_pairs={{0,8},{4,12},{8,0},{12,4},{16,24},{20,28},{24,16},{28,20},{1,9},{5... | collective-permute-start | bytes 294920 | tf_op jit(solution)/shard_map/ppermute | solution.py:38
  43.7 10.1 %collective-permute-start.18 = (bf16[6,128,128]{2,1,0:T(8,128)(2,1)S(1)}, bf16[6,128,128]{2,1,0:T(8,128)(2,1)S(1)}, u32[]{:S(2)}, u32[]{:S(2)}) collective-permute-start(bf16[6,128,128]{2,1,0:T(8,128)(2,1)S(1)} %collective-permute-done.17.refs_6_), channel_id=1, source_target_pairs={{0,1},{1,0},{2,3},{3,2},{4,5},{5,4},{6,7},{7,6},{8,9},{9,8},{10,11... | collective-permute-start | bytes 589832 | tf_op jit(solution)/shard_map/ppermute | solution.py:38
  48.1 4.7 %collective-permute-start.16 = (bf16[6,64,128]{2,1,0:T(8,128)(2,1)S(1)}, bf16[6,64,128]{2,1,0:T(8,128)(2,1)S(1)}, u32[]{:S(2)}, u32[]{:S(2)}) collective-permute-start(bf16[6,64,128]{2,1,0:T(8,128)(2,1)S(1)} %shard_map.50), channel_id=1, source_target_pairs={{0,4},{4,0},{8,24},{12,28},{16,20},{20,16},{24,8},{28,12},{1,5},{5... | collective-permute-start | bytes 294920 | tf_op jit(solution)/shard_map/ppermute | solution.py:596
  48.6 5.2 %collective-permute-start.15 = (bf16[6,64,128]{2,1,0:T(8,128)(2,1)S(1)}, bf16[6,64,128]{2,1,0:T(8,128)(2,1)S(1)}, u32[]{:S(2)}, u32[]{:S(2)}) collective-permute-start(bf16[6,64,128]{2,1,0:T(8,128)(2,1)S(1)} %shard_map.50), channel_id=1, source_target_pairs={{0,4},{4,0},{8,16},{12,20},{16,8},{20,12},{24,28},{28,24},{1,5},{5... | collective-permute-start | bytes 294920 | tf_op jit(solution)/shard_map/ppermute | solution.py:595
  57.3 1.9 %collective-permute-start.19 = (bf16[6,32,128]{2,1,0:T(8,128)(2,1)S(1)}, bf16[6,32,128]{2,1,0:T(8,128)(2,1)S(1)}, u32[]{:S(2)}, u32[]{:S(2)}) collective-permute-start(bf16[6,32,128]{2,1,0:T(8,128)(2,1)S(1)} %get-tuple-element.36), channel_id=1, source_target_pairs={{0,1},{1,0},{2,3},{3,2},{4,5},{5,4},{6,7},{7,6},{8,9},{9,8},{10,11... | collective-permute-start | bytes 147464 | tf_op jit(solution)/shard_map/ppermute | solution.py:38
  57.4 4.2 %collective-permute-start.20 = (bf16[6,32,128]{2,1,0:T(8,128)(2,1)S(1)}, bf16[6,32,128]{2,1,0:T(8,128)(2,1)S(1)}, u32[]{:S(2)}, u32[]{:S(2)}) collective-permute-start(bf16[6,32,128]{2,1,0:T(8,128)(2,1)S(1)} %get-tuple-element.37), channel_id=1, source_target_pairs={{0,2},{1,3},{2,0},{3,1},{4,6},{5,7},{6,4},{7,5},{8,10},{9,11},{10,... | collective-permute-start | bytes 147464 | tf_op jit(solution)/shard_map/ppermute | solution.py:38
  58.6 3.7 %collective-permute-start.21 = (bf16[6,32,128]{2,1,0:T(8,128)(2,1)S(1)}, bf16[6,32,128]{2,1,0:T(8,128)(2,1)S(1)}, u32[]{:S(2)}, u32[]{:S(2)}) collective-permute-start(bf16[6,32,128]{2,1,0:T(8,128)(2,1)S(1)} %get-tuple-element.38), channel_id=1, source_target_pairs={{0,3},{1,2},{2,1},{3,0},{4,7},{5,6},{6,5},{7,4},{8,11},{9,10},{10,... | collective-permute-start | bytes 147464 | tf_op jit(solution)/shard_map/ppermute | solution.py:38
  (2 other events, 43.4 us)
